TPU v7x, 256 devices: a whole 4x4x8 slice. The times are simulated.
256 devices in a mesh: lev: 2 (over x_lo), gx: 16 (over x_hi, z), gy: 8 (over y, core).
Axes of the slice: x: 4 (x_hi: 2, x_lo: 2; x = x_hi * 2 + x_lo), y: 4, z: 8, core: 2. Of those that a mesh axis runs over, the one named last changes fastest.
Arguments:
- initial_conc: float32 [4, 4, 1024, 1024], P(None, 'lev', 'gx', 'gy'), may hold values from -6 to 6
- diffusivity: float32 [4, 1024, 1024], P('lev', 'gx', 'gy'), may hold values from 0.02 to 0.2
- wind_east: float32 [4, 1024, 1024], P('lev', 'gx', 'gy'), may hold values from -0.4 to 0.4
- wind_north: float32 [4, 1024, 1024], P('lev', 'gx', 'gy'), may hold values from -0.4 to 0.4
- level_weight: float32 [4, 4], P(None, 'lev'), may hold values from 0.05 to 0.5
- sounding_owner: int32 [65536, 1], P(('gx', 'gy')), may hold values from 0 to 127; in each aligned block of 512 rows (0 to 511, 512 to 1023, ...) at most 16 rows name the same one
- sounding_column: int32 [65536], P(('gx', 'gy')), may hold values from 0 to 8191
- observed: float32 [65536], P(('gx', 'gy')), may hold values from -15 to 15
Outputs:
- forecast: float32 [4, 4, 1024, 1024], P(None, 'lev', 'gx', 'gy')
- model_column: float32 [65536], P(('gx', 'gy'))
- gradient: float32 [4, 4, 1024, 1024], P(None, 'lev', 'gx', 'gy')
Inputs may be any that keep to these rules, and one draw needn't show every extreme that they name: `sounding_owner`: among the 512 soundings of one device, at most 16 have the same owner, and this many is reached.
All inputs are finite; a program needn't handle non-finite values.
Results may differ from a plain program's by a relative error of at most 0.00002.
Values sent between devices are 32-bit elements; how exact they have to be, the bound alone decides.
No kernel may reach another device: no remote copies, remote signals or barrier semaphores. Data moves between devices by JAX's collectives and lax.ppermute only.
A program may use at most 64 MiB of HBM per device.

v0:
```python
import functools

import jax
import jax.numpy as jnp
from jax import lax
from jax.experimental import pallas as pl
from jax.experimental.pallas import tpu as pltpu
from jax.sharding import PartitionSpec as P

STEPS = 4
CAP = 16
HALO = 4
EDGE = 8
F32 = jnp.float32
BF16 = jnp.bfloat16
VMEM = pl.BlockSpec(memory_space=pltpu.VMEM)
SMEM = pl.BlockSpec(memory_space=pltpu.SMEM)


def call(body, outs, inputs, specs=None, us=1.0):
    return pl.pallas_call(
        body,
        out_shape=outs,
        in_specs=specs or [VMEM] * len(inputs),
        out_specs=jax.tree.map(lambda _: VMEM, outs),
        compiler_params=pltpu.CompilerParams(vmem_limit_bytes=16 << 20),
        cost_estimate=pl.CostEstimate(
            flops=int(us * 1e6), bytes_accessed=int(us * 3e6), transcendentals=0
        ),
    )(*inputs)


def split3(x):
    a = x.astype(BF16)
    r = x - a.astype(F32)
    b = r.astype(BF16)
    c = (r - b.astype(F32)).astype(BF16)
    return a, b, c


def nt(a, b):
    return lax.dot_general(a, b, (((1,), (1,)), ((), ())), preferred_element_type=F32)


def nn(a, b):
    return jnp.dot(a, b, preferred_element_type=F32)


def iota(shape, dim):
    return lax.broadcasted_iota(jnp.int32, shape, dim)


def request_body(groups, owner, column, observed, req, rank):
    rows, lanes = owner.shape
    before = (iota((lanes, lanes), 0) < iota((lanes, lanes), 1)).astype(F32).astype(BF16)
    ones = jnp.ones((lanes, lanes), BF16)
    carry = jnp.zeros((groups, lanes), F32)
    total = jnp.zeros((groups, lanes), F32)
    blank = jnp.zeros((lanes - 2 * CAP, lanes), F32)
    for j in range(rows):
        onehot = (iota((groups, lanes), 0) == owner[j : j + 1, :]).astype(F32)
        hot = onehot.astype(BF16)
        prior = nn(hot, before) + carry
        place = jnp.sum(onehot * prior, axis=0, keepdims=True)
        carry = carry + nn(hot, ones)
        place = place.astype(jnp.int32)
        rank[j : j + 1, :] = place
        slot = (iota((CAP, lanes), 0) == place).astype(F32)
        code = column[j : j + 1, :] + 1
        low = code & (lanes - 1)
        obs = split3(observed[j : j + 1, :])
        codes = ((code - low).astype(F32), low.astype(F32), None)
        for part, o in zip(codes, obs):
            top = jnp.zeros_like(slot) if part is None else slot * part
            values = jnp.concatenate([top, slot * o.astype(F32), blank], axis=0)
            total = total + nt(hot, values.astype(BF16))
    req[...] = total


def edges_body(conc, kk, uu, vv, high, low):
    n = conc.shape[2]
    f = 0
    for t in range(conc.shape[0]):
        for l in range(conc.shape[1]):
            high[f] = conc[t, l, n - EDGE : n, :]
            low[f] = conc[t, l, 0:EDGE, :]
            f += 1
    for c in (kk, uu, vv):
        for l in range(c.shape[0]):
            high[f] = c[l, n - EDGE : n, :]
            low[f] = c[l, 0:EDGE, :]
            f += 1


def inside(axis):
    i, n = lax.axis_index(axis), lax.axis_size(axis)
    return (i > 0).astype(F32), (i < n - 1).astype(F32)


def tall(tile, f, below, above, keep):
    return jnp.concatenate([below[f] * keep[0], tile, above[f] * keep[1]], axis=0)


def tiles(conc, kk, uu, vv):
    out = [conc[t, l] for t in range(conc.shape[0]) for l in range(conc.shape[1])]
    return out + [c[l] for c in (kk, uu, vv) for l in range(c.shape[0])]


def lanes_body(conc, kk, uu, vv, below, above, high, low):
    keep = inside("gx")
    m = conc.shape[3]
    up = down = None
    for f, tile in enumerate(tiles(conc, kk, uu, vv)):
        x = tall(tile, f, below, above, keep)
        at = iota(x.shape, 1)
        mine = (at >= HALO * f) & (at < HALO * (f + 1))
        a = pltpu.roll(x, (HALO * f + HALO) % m, 1)
        b = pltpu.roll(x, (HALO * f) % m, 1) if f else x
        up = jnp.where(mine, a, 0.0 if up is None else up)
        down = jnp.where(mine, b, 0.0 if down is None else down)
    high[...] = up
    low[...] = down


def forward_body(conc, kk, uu, vv, below, above, left, right, weight, out, column, coef):
    keep = inside("gx")
    keep_l, keep_r = inside("gy")
    n, m = conc.shape[2], conc.shape[3]
    from_left = left[...] * keep_l
    from_right = right[...] * keep_r
    at = iota(from_left.shape, 1)

    def wide(tile, f):
        x = tall(tile, f, below, above, keep)
        a = pltpu.roll(from_right, (m - HALO * f) % m, 1) if f else from_right
        b = pltpu.roll(from_left, (m - HALO - HALO * f) % m, 1)
        side = jnp.where(at < HALO, a, jnp.where(at >= m - HALO, b, 0.0))
        return jnp.concatenate([x, side], axis=1)

    tracers, levels = conc.shape[0], conc.shape[1]
    total = jnp.zeros((n, m), F32)
    base = tracers * levels
    for l in range(levels):
        k = wide(kk[l], base + l)
        u = 0.5 * wide(uu[l], base + levels + l)
        v = 0.5 * wide(vv[l], base + 2 * levels + l)
        coef[l, 0] = 1.0 - 4.0 * k
        coef[l, 1] = k - u
        coef[l, 2] = k + u
        coef[l, 3] = k - v
        coef[l, 4] = k + v
        for t in range(tracers):
            c = wide(conc[t, l], t * levels + l)
            rows, cols = c.shape
            for _ in range(STEPS):
                c = (
                    coef[l, 0] * c
                    + coef[l, 1] * pltpu.roll(c, rows - 1, 0)
                    + coef[l, 2] * pltpu.roll(c, 1, 0)
                    + coef[l, 3] * pltpu.roll(c, cols - 1, 1)
                    + coef[l, 4] * pltpu.roll(c, 1, 1)
                )
            c = c[EDGE : EDGE + n, :m]
            out[t, l] = c
            total = total + weight[t, l] * c
    column[...] = total


def slots(code, n, m):
    where = code.astype(jnp.int32) - 1
    x, y = where // m, where & (m - 1)
    x = jnp.where(where < 0, -1, x)
    xs, ys = [], []
    for s in range(CAP):
        xs.append((iota((n, x.shape[1]), 0) == x[s : s + 1, :]).astype(F32))
        ys.append((iota((m, x.shape[1]), 0) == y[s : s + 1, :]).astype(F32).astype(BF16))
    return xs, ys


def serve_body(asked, mine, other, values, force):
    n, m = mine.shape
    field = mine[...] + other[...]
    t = asked[...].T
    xs, ys = slots(t[:CAP], n, m)
    f1, f2, f3 = split3(field)
    fields = jnp.concatenate([f1, f2, f3], axis=0)
    o1, o2, o3 = (o.astype(F32) for o in split3(t[CAP : 2 * CAP]))
    picked = []
    sums = jnp.zeros((4 * n, m), F32)
    for s in range(CAP):
        z = nn(fields, ys[s])
        z = (z[:n] + z[n : 2 * n] + z[2 * n :]) * xs[s]
        picked.append(jnp.sum(z, axis=0, keepdims=True))
        x = xs[s]
        lhs = [x] + [x * o[s : s + 1, :] for o in (o1, o2, o3)]
        sums = sums + nt(jnp.concatenate(lhs, axis=0).astype(BF16), ys[s])
    rows = t.shape[0]
    picked.append(jnp.zeros((rows - CAP, t.shape[1]), F32))
    values[...] = jnp.concatenate(picked, axis=0).T
    count, seen = sums[:n], sums[n : 2 * n] + sums[2 * n : 3 * n] + sums[3 * n :]
    force[...] = count * field - seen


def answer_body(groups, got, owner, rank, out):
    rows, lanes = owner.shape
    t = got[...].T[:CAP]
    parts = jnp.concatenate(split3(t), axis=0)
    for j in range(rows):
        onehot = (iota((groups, lanes), 0) == owner[j : j + 1, :]).astype(F32)
        z = nn(parts, onehot.astype(BF16))
        z = z[:CAP] + z[CAP : 2 * CAP] + z[2 * CAP :]
        slot = iota((CAP, lanes), 0) == rank[j : j + 1, :]
        out[j : j + 1, :] = jnp.sum(jnp.where(slot, z, 0.0), axis=0, keepdims=True)


def tall_body(force, below, above, out):
    keep = inside("gx")
    out[...] = jnp.concatenate(
        [below[...] * keep[0], force[...], above[...] * keep[1]], axis=0
    )


def adjoint_body(force, left, right, coef, weight, out):
    keep_l, keep_r = inside("gy")
    n, m = out.shape[2], out.shape[3]
    at = iota(force.shape, 1)
    a, b = right[...] * keep_r, left[...] * keep_l
    side = jnp.where(at < HALO, a, jnp.where(at >= m - HALO, b, 0.0))
    start = jnp.concatenate([force[...], side], axis=1)
    rows, cols = start.shape
    for l in range(out.shape[1]):
        a = start
        for _ in range(STEPS):
            a = (
                coef[l, 0] * a
                + pltpu.roll(coef[l, 2] * a, rows - 1, 0)
                + pltpu.roll(coef[l, 1] * a, 1, 0)
                + pltpu.roll(coef[l, 4] * a, cols - 1, 1)
                + pltpu.roll(coef[l, 3] * a, 1, 1)
            )
        a = a[EDGE : EDGE + n, :m]
        for t in range(out.shape[0]):
            out[t, l] = weight[t, l] * a


def ring(value, axis, step):
    n = lax.axis_size(axis)
    return lax.ppermute(value, axis, [(i, (i + step) % n) for i in range(n)])


def shards(conc, kk, uu, vv, weight, owner, column, observed):
    S = jax.ShapeDtypeStruct
    tracers, levels, n, m = conc.shape
    fields = (tracers + 3) * levels
    groups = lax.axis_size("gx") * lax.axis_size("gy")
    owner = owner.reshape(-1, 128)
    column = column.reshape(-1, 128)
    obs = observed.reshape(-1, 128)
    edge = S((fields, EDGE, m), F32)
    high, low = call(edges_body, (edge, edge), (conc, kk, uu, vv))
    req, rank = call(
        functools.partial(request_body, groups),
        (S((groups, 128), F32), S(owner.shape, jnp.int32)),
        (owner, column, obs),
    )
    asked = lax.all_to_all(req, ("gx", "gy"), 0, 0, tiled=True)
    below = ring(high, "gx", 1)
    above = ring(low, "gx", -1)
    strip = S((n + 2 * EDGE, m), F32)
    high, low = call(lanes_body, (strip, strip), (conc, kk, uu, vv, below, above))
    left = ring(high, "gy", 1)
    right = ring(low, "gy", -1)
    forecast, mine, coef = call(
        forward_body,
        (
            S(conc.shape, F32),
            S((n, m), F32),
            S((levels, 5, n + 2 * EDGE, 2 * m), F32),
        ),
        (conc, kk, uu, vv, below, above, left, right, weight),
        [VMEM] * 8 + [SMEM],
        us=3.0,
    )
    other = lax.ppermute(mine, "lev", [(0, 1), (1, 0)])
    values, force = call(
        serve_body, (S((groups, 128), F32), S((n, m), F32)), (asked, mine, other), us=2.0
    )
    got = lax.all_to_all(values, ("gx", "gy"), 0, 0, tiled=True)
    below = ring(force[n - EDGE :], "gx", 1)
    above = ring(force[:EDGE], "gx", -1)
    force = call(tall_body, strip, (force, below, above))
    left = ring(force, "gy", 1)
    right = ring(force, "gy", -1)
    gradient = call(
        adjoint_body,
        S(conc.shape, F32),
        (force, left, right, coef, weight),
        [VMEM] * 4 + [SMEM],
        us=2.0,
    )
    model = call(
        functools.partial(answer_body, groups), S(owner.shape, F32), (got, owner, rank)
    )
    return (forecast, model.reshape(-1), gradient)


def solution(mesh):
    return jax.shard_map(
        shards,
        mesh=mesh,
        in_specs=(
            P(None, "lev", "gx", "gy"),
            P("lev", "gx", "gy"),
            P("lev", "gx", "gy"),
            P("lev", "gx", "gy"),
            P(None, "lev"),
            P(("gx", "gy"), None),
            P(("gx", "gy")),
            P(("gx", "gy")),
        ),
        out_specs=(P(None, "lev", "gx", "gy"), P(("gx", "gy")), P(None, "lev", "gx", "gy")),
        check_vma=False,
    )
```

profile of v0, /device:TPU:1, one launch (start us, length us, event | category | flops | bytes accessed | tf_op | source)
XLA Modules:
  0.0 72.9 jit_solution(11133579451605503190)
XLA Ops:
  0.6 0.9 %copy-done = f32[4,2,64,128]{3,2,1,0:T(8,128)S(1)} copy-done((f32[4,2,64,128]{3,2,1,0:T(8,128)S(1)}, f32[4,2,64,128]{3,2,1,0:T(8,128)}, u32[]{:S(2)}) %copy-start) | copy-done | bytes 262168
  1.6 0.8 %copy-done.2 = f32[2,64,128]{2,1,0:T(8,128)S(1)} copy-done((f32[2,64,128]{2,1,0:T(8,128)S(1)}, f32[2,64,128]{2,1,0:T(8,128)}, u32[]{:S(2)}) %copy-start.2) | copy-done | bytes 65560
  2.4 0.8 %copy-done.4 = f32[2,64,128]{2,1,0:T(8,128)S(1)} copy-done((f32[2,64,128]{2,1,0:T(8,128)S(1)}, f32[2,64,128]{2,1,0:T(8,128)}, u32[]{:S(2)}) %copy-start.4) | copy-done | bytes 65560
  3.3 0.8 %copy-done.6 = f32[2,64,128]{2,1,0:T(8,128)S(1)} copy-done((f32[2,64,128]{2,1,0:T(8,128)S(1)}, f32[2,64,128]{2,1,0:T(8,128)}, u32[]{:S(2)}) %copy-start.6) | copy-done | bytes 65560
  4.1 2.5 %collective-permute-start = (f32[14,8,128]{2,1,0:T(8,128)S(1)}, f32[14,8,128]{2,1,0:T(8,128)S(1)}, u32[]{:S(2)}, u32[]{:S(2)}) collective-permute-start(f32[14,8,128]{2,1,0:T(8,128)S(1)} %get-tuple-element.14), channel_id=1, source_target_pairs={{0,8},{8,16},{16,24},{24,32},{32,40},{40,48},{48,56},{56,64},{64,7... | collective-permute-start | bytes 172040 | tf_op jit(solution)/shard_map/ppermute | solution.py:248
  6.7 6.5 %collective-permute-start.1 = (f32[14,8,128]{2,1,0:T(8,128)S(1)}, f32[14,8,128]{2,1,0:T(8,128)S(1)}, u32[]{:S(2)}, u32[]{:S(2)}) collective-permute-start(f32[14,8,128]{2,1,0:T(8,128)S(1)} %get-tuple-element.15), channel_id=1, source_target_pairs={{0,120},{8,0},{16,8},{24,16},{32,24},{40,32},{48,40},{56,48},{64,5... | collective-permute-start | bytes 172040 | tf_op jit(solution)/shard_map/ppermute | solution.py:248
  13.8 1.3 %shard_map.106 = (f32[128,128]{1,0:T(8,128)}, s32[4,128]{1,0:T(4,128)S(1)}) custom-call(s32[4,128]{1,0:T(4,128)S(1)} %bitcast.14, s32[4,128]{1,0:T(4,128)S(1)} %bitcast.16, f32[4,128]{1,0:T(4,128)S(1)} %bitcast.17), custom_call_target="tpu_custom_call" | custom-call | flops 1000000 | bytes 3000000 | tf_op jit(solution)/shard_map/pallas_call | solution.py:21
  15.1 10.8 %all-to-all-start = ((f32[128,1,128]{2,1,0:T(1,128)}), f32[128,1,128]{2,1,0:T(1,128)S(1)}, u32[]{:S(2)}, u32[]{:S(2)}) async-start(f32[128,1,128]{2,1,0:T(1,128)} %bitcast.4), calls=%async_computation | async-start | bytes 131072 | tf_op jit(solution)/shard_map/all_to_all | solution.py:266
  26.4 1.6 %collective-permute-start.2 = (f32[80,128]{1,0:T(8,128)S(1)}, f32[80,128]{1,0:T(8,128)S(1)}, u32[]{:S(2)}, u32[]{:S(2)}) collective-permute-start(f32[80,128]{1,0:T(8,128)S(1)} %get-tuple-element.16), channel_id=1, source_target_pairs={{0,1},{1,2},{2,3},{3,4},{4,5},{5,6},{6,7},{7,0},{8,9},{9,10},{10,1... | collective-permute-start | bytes 122888 | tf_op jit(solution)/shard_map/ppermute | solution.py:248
  28.1 1.0 %collective-permute-done.2.left = f32[80,128]{1,0:T(8,128)S(1)} collective-permute-done((f32[80,128]{1,0:T(8,128)S(1)}, f32[80,128]{1,0:T(8,128)S(1)}, u32[]{:S(2)}, u32[]{:S(2)}) %collective-permute-start.2) | collective-permute-done | bytes 40992 | tf_op jit(solution)/shard_map/ppermute | solution.py:248
  29.1 2.7 %collective-permute-done.3.right = f32[80,128]{1,0:T(8,128)S(1)} collective-permute-done((f32[80,128]{1,0:T(8,128)S(1)}, f32[80,128]{1,0:T(8,128)S(1)}, u32[]{:S(2)}, u32[]{:S(2)}) %collective-permute-start.3) | collective-permute-done | bytes 40992 | tf_op jit(solution)/shard_map/ppermute | solution.py:248
  31.8 4.6 %shard_map.105 = (f32[4,2,64,128]{3,2,1,0:T(8,128)}, f32[64,128]{1,0:T(8,128)S(1)}, f32[2,5,80,256]{3,2,1,0:T(8,128)S(1)}) custom-call(f32[4,2,64,128]{3,2,1,0:T(8,128)S(1)} %copy-done.1, f32[2,64,128]{2,1,0:T(8,128)S(1)} %copy-done.3, f32[2,64,128]{2,1,0:T(8,128)S(1)} %copy-done.5, f32[2,64,128]{2,1,0:T(8,128)S(1)} %copy-done.7, ...), custom_call_target="tpu_custom_call" | custom-call | flops 3000000 | bytes 9000000 | tf_op jit(solution)/shard_map/pallas_call | solution.py:21
  36.7 1.5 %all-to-all-done = f32[128,1,128]{2,1,0:T(1,128)S(1)} async-done(((f32[128,1,128]{2,1,0:T(1,128)}), f32[128,1,128]{2,1,0:T(1,128)S(1)}, u32[]{:S(2)}, u32[]{:S(2)}) %all-to-all-start) | async-done | bytes 65568 | tf_op jit(solution)/shard_map/all_to_all | solution.py:266
  38.2 1.0 %collective-permute-done.4.other = f32[64,128]{1,0:T(8,128)S(1)} collective-permute-done((f32[64,128]{1,0:T(8,128)S(1)}, f32[64,128]{1,0:T(8,128)S(1)}, u32[]{:S(2)}, u32[]{:S(2)}) %collective-permute-start.4) | collective-permute-done | bytes 32800 | tf_op jit(solution)/shard_map/ppermute | solution.py:284
  39.2 1.4 %shard_map.107 = (f32[128,128]{1,0:T(8,128)}, f32[64,128]{1,0:T(8,128)S(1)}) custom-call(f32[128,128]{1,0:T(8,128)S(1)} %bitcast.13, f32[64,128]{1,0:T(8,128)S(1)} %get-tuple-element.20.mine, f32[64,128]{1,0:T(8,128)S(1)} %collective-permute-done.4.other), custom_call_target="tpu_custom_call" | custom-call | flops 2000000 | bytes 6000000 | tf_op jit(solution)/shard_map/pallas_call | solution.py:21
  40.6 13.1 %all-to-all-start.1 = ((f32[128,1,128]{2,1,0:T(1,128)}), f32[128,1,128]{2,1,0:T(1,128)S(1)}, u32[]{:S(2)}, u32[]{:S(2)}) async-start(f32[128,1,128]{2,1,0:T(1,128)} %bitcast.7), calls=%async_computation.1 | async-start | bytes 131072 | tf_op jit(solution)/shard_map/all_to_all | solution.py:288
  53.8 5.8 %collective-permute-start.6 = (f32[8,128]{1,0:T(8,128)S(1)}, f32[8,128]{1,0:T(8,128)S(1)}, u32[]{:S(2)}, u32[]{:S(2)}) collective-permute-start(f32[8,128]{1,0:T(8,128)S(1)} %get-tuple-element.25), channel_id=1, source_target_pairs={{0,120},{8,0},{16,8},{24,16},{32,24},{40,32},{48,40},{56,48},{64,5... | collective-permute-start | bytes 12296 | tf_op jit(solution)/shard_map/ppermute | solution.py:248
  59.5 0.8 %collective-permute-done.6.above = f32[8,128]{1,0:T(8,128)S(1)} collective-permute-done((f32[8,128]{1,0:T(8,128)S(1)}, f32[8,128]{1,0:T(8,128)S(1)}, u32[]{:S(2)}, u32[]{:S(2)}) %collective-permute-start.6) | collective-permute-done | bytes 4128 | tf_op jit(solution)/shard_map/ppermute | solution.py:248
  60.3 5.6 %collective-permute-done.5.below = f32[8,128]{1,0:T(8,128)S(1)} collective-permute-done((f32[8,128]{1,0:T(8,128)S(1)}, f32[8,128]{1,0:T(8,128)S(1)}, u32[]{:S(2)}, u32[]{:S(2)}) %collective-permute-start.5) | collective-permute-done | bytes 4128 | tf_op jit(solution)/shard_map/ppermute | solution.py:248
  65.9 1.5 %collective-permute-start.8 = (f32[80,128]{1,0:T(8,128)S(1)}, f32[80,128]{1,0:T(8,128)S(1)}, u32[]{:S(2)}, u32[]{:S(2)}) collective-permute-start(f32[80,128]{1,0:T(8,128)S(1)} %shard_map.109.force), channel_id=1, source_target_pairs={{0,7},{1,0},{2,1},{3,2},{4,3},{5,4},{6,5},{7,6},{8,15},{9,8},{10,9... | collective-permute-start | bytes 122888 | tf_op jit(solution)/shard_map/ppermute | solution.py:248
  67.4 1.1 %collective-permute-start.7 = (f32[80,128]{1,0:T(8,128)S(1)}, f32[80,128]{1,0:T(8,128)S(1)}, u32[]{:S(2)}, u32[]{:S(2)}) collective-permute-start(f32[80,128]{1,0:T(8,128)S(1)} %shard_map.109.force), channel_id=1, source_target_pairs={{0,1},{1,2},{2,3},{3,4},{4,5},{5,6},{6,7},{7,0},{8,9},{9,10},{10,1... | collective-permute-start | bytes 122888 | tf_op jit(solution)/shard_map/ppermute | solution.py:248
  68.5 1.7 %collective-permute-done.8.right = f32[80,128]{1,0:T(8,128)S(1)} collective-permute-done((f32[80,128]{1,0:T(8,128)S(1)}, f32[80,128]{1,0:T(8,128)S(1)}, u32[]{:S(2)}, u32[]{:S(2)}) %collective-permute-start.8) | collective-permute-done | bytes 40992 | tf_op jit(solution)/shard_map/ppermute | solution.py:248
  70.2 1.9 %shard_map.110 = f32[4,2,64,128]{3,2,1,0:T(8,128)} custom-call(f32[80,128]{1,0:T(8,128)S(1)} %shard_map.109.force, f32[80,128]{1,0:T(8,128)S(1)} %collective-permute-done.7.left, f32[80,128]{1,0:T(8,128)S(1)} %collective-permute-done.8.right, f32[2,5,80,256]{3,2,1,0:T(8,128)S(1)} %get-tuple-element.24.coef, f32[4,2]{1,0:T(4,128)S(1)} %copy.13.weight), custom_call_target="tpu_custom_call" | custom-call | flops 2000000 | bytes 6000000 | tf_op jit(solution)/shard_map/pallas_call | solution.py:21
  72.1 0.8 %shard_map.108 = f32[4,128]{1,0:T(4,128)} custom-call(f32[128,128]{1,0:T(8,128)S(1)} %bitcast.12, s32[4,128]{1,0:T(4,128)S(1)} %bitcast.15, s32[4,128]{1,0:T(4,128)S(1)} %get-tuple-element.22.rank), custom_call_target="tpu_custom_call" | custom-call | flops 1000000 | bytes 3000000 | tf_op jit(solution)/shard_map/pallas_call | solution.py:21
  (32 shorter events, 1.5 us)
Async XLA Ops:
  0.6 1.0 %copy-start = (f32[4,2,64,128]{3,2,1,0:T(8,128)S(1)}, f32[4,2,64,128]{3,2,1,0:T(8,128)}, u32[]{:S(2)}) copy-start(f32[4,2,64,128]{3,2,1,0:T(8,128)} %conc.5) | copy-start | bytes 786436
  1.6 0.8 %copy-start.2 = (f32[2,64,128]{2,1,0:T(8,128)S(1)}, f32[2,64,128]{2,1,0:T(8,128)}, u32[]{:S(2)}) copy-start(f32[2,64,128]{2,1,0:T(8,128)} %kk.5) | copy-start | bytes 196612
  2.4 0.8 %copy-start.4 = (f32[2,64,128]{2,1,0:T(8,128)S(1)}, f32[2,64,128]{2,1,0:T(8,128)}, u32[]{:S(2)}) copy-start(f32[2,64,128]{2,1,0:T(8,128)} %uu.5) | copy-start | bytes 196612
  3.3 0.8 %copy-start.6 = (f32[2,64,128]{2,1,0:T(8,128)S(1)}, f32[2,64,128]{2,1,0:T(8,128)}, u32[]{:S(2)}) copy-start(f32[2,64,128]{2,1,0:T(8,128)} %vv.5) | copy-start | bytes 196612
  4.1 9.1 %copy-start.10 = (f32[512]{0:T(512)S(1)}, f32[512]{0:T(512)}, u32[]{:S(2)}) copy-start(f32[512]{0:T(512)} %param.15) | copy-start | bytes 6148
  4.1 21.9 %copy-start.1 = (f32[4,2,64,128]{3,2,1,0:T(8,128)S(1)}, f32[4,2,64,128]{3,2,1,0:T(8,128)}, u32[]{:S(2)}) copy-start(f32[4,2,64,128]{3,2,1,0:T(8,128)} %conc.5) | copy-start | bytes 786436
  4.1 21.9 %copy-start.7 = (f32[2,64,128]{2,1,0:T(8,128)S(1)}, f32[2,64,128]{2,1,0:T(8,128)}, u32[]{:S(2)}) copy-start(f32[2,64,128]{2,1,0:T(8,128)} %vv.5) | copy-start | bytes 196612
  4.1 21.8 %collective-permute-start = (f32[14,8,128]{2,1,0:T(8,128)S(1)}, f32[14,8,128]{2,1,0:T(8,128)S(1)}, u32[]{:S(2)}, u32[]{:S(2)}) collective-permute-start(f32[14,8,128]{2,1,0:T(8,128)S(1)} %get-tuple-element.14), channel_id=1, source_target_pairs={{0,8},{8,16},{16,24},{24,32},{32,40},{40,48},{48,56},{56,64},{64,7... | collective-permute-start | bytes 172040 | tf_op jit(solution)/shard_map/ppermute | solution.py:248
  6.7 19.3 %collective-permute-start.1 = (f32[14,8,128]{2,1,0:T(8,128)S(1)}, f32[14,8,128]{2,1,0:T(8,128)S(1)}, u32[]{:S(2)}, u32[]{:S(2)}) collective-permute-start(f32[14,8,128]{2,1,0:T(8,128)S(1)} %get-tuple-element.15), channel_id=1, source_target_pairs={{0,120},{8,0},{16,8},{24,16},{32,24},{40,32},{48,40},{56,48},{64,5... | collective-permute-start | bytes 172040 | tf_op jit(solution)/shard_map/ppermute | solution.py:248
  13.2 0.7 copy-start.9
  13.2 0.7 copy-start.8
  15.1 10.9 %copy-start.3 = (f32[2,64,128]{2,1,0:T(8,128)S(1)}, f32[2,64,128]{2,1,0:T(8,128)}, u32[]{:S(2)}) copy-start(f32[2,64,128]{2,1,0:T(8,128)} %kk.5) | copy-start | bytes 196612
  15.1 10.9 %copy-start.5 = (f32[2,64,128]{2,1,0:T(8,128)S(1)}, f32[2,64,128]{2,1,0:T(8,128)}, u32[]{:S(2)}) copy-start(f32[2,64,128]{2,1,0:T(8,128)} %uu.5) | copy-start | bytes 196612
  15.1 23.1 %all-to-all-start = ((f32[128,1,128]{2,1,0:T(1,128)}), f32[128,1,128]{2,1,0:T(1,128)S(1)}, u32[]{:S(2)}, u32[]{:S(2)}) async-start(f32[128,1,128]{2,1,0:T(1,128)} %bitcast.4), calls=%async_computation | async-start | bytes 131072 | tf_op jit(solution)/shard_map/all_to_all | solution.py:266
  26.4 1.7 %copy-start.11 = (f32[4,2]{0,1:T(2,128)S(1)}, f32[4,2]{0,1:T(2,128)}, u32[]{:S(2)}) copy-start(f32[4,2]{0,1:T(2,128)} %param.12) | copy-start | bytes 100
  26.4 2.7 %collective-permute-start.2 = (f32[80,128]{1,0:T(8,128)S(1)}, f32[80,128]{1,0:T(8,128)S(1)}, u32[]{:S(2)}, u32[]{:S(2)}) collective-permute-start(f32[80,128]{1,0:T(8,128)S(1)} %get-tuple-element.16), channel_id=1, source_target_pairs={{0,1},{1,2},{2,3},{3,4},{4,5},{5,6},{6,7},{7,0},{8,9},{9,10},{10,1... | collective-permute-start | bytes 122888 | tf_op jit(solution)/shard_map/ppermute | solution.py:248
  28.0 3.8 %collective-permute-start.3 = (f32[80,128]{1,0:T(8,128)S(1)}, f32[80,128]{1,0:T(8,128)S(1)}, u32[]{:S(2)}, u32[]{:S(2)}) collective-permute-start(f32[80,128]{1,0:T(8,128)S(1)} %get-tuple-element.17), channel_id=1, source_target_pairs={{0,7},{1,0},{2,1},{3,2},{4,3},{5,4},{6,5},{7,6},{8,15},{9,8},{10,9... | collective-permute-start | bytes 122888 | tf_op jit(solution)/shard_map/ppermute | solution.py:248
  36.4 2.8 %collective-permute-start.4 = (f32[64,128]{1,0:T(8,128)S(1)}, f32[64,128]{1,0:T(8,128)S(1)}, u32[]{:S(2)}, u32[]{:S(2)}) collective-permute-start(f32[64,128]{1,0:T(8,128)S(1)} %get-tuple-element.20.mine), channel_id=1, source_target_pairs={{0,128},{128,0},{1,129},{129,1},{2,130},{130,2},{3,131},{131,3},{4... | collective-permute-start | bytes 98312 | tf_op jit(solution)/shard_map/ppermute | solution.py:284
  40.6 31.5 %all-to-all-start.1 = ((f32[128,1,128]{2,1,0:T(1,128)}), f32[128,1,128]{2,1,0:T(1,128)S(1)}, u32[]{:S(2)}, u32[]{:S(2)}) async-start(f32[128,1,128]{2,1,0:T(1,128)} %bitcast.7), calls=%async_computation.1 | async-start | bytes 131072 | tf_op jit(solution)/shard_map/all_to_all | solution.py:288
  53.8 6.5 %collective-permute-start.6 = (f32[8,128]{1,0:T(8,128)S(1)}, f32[8,128]{1,0:T(8,128)S(1)}, u32[]{:S(2)}, u32[]{:S(2)}) collective-permute-start(f32[8,128]{1,0:T(8,128)S(1)} %get-tuple-element.25), channel_id=1, source_target_pairs={{0,120},{8,0},{16,8},{24,16},{32,24},{40,32},{48,40},{56,48},{64,5... | collective-permute-start | bytes 12296 | tf_op jit(solution)/shard_map/ppermute | solution.py:248
  59.5 6.4 %collective-permute-start.5 = (f32[8,128]{1,0:T(8,128)S(1)}, f32[8,128]{1,0:T(8,128)S(1)}, u32[]{:S(2)}, u32[]{:S(2)}) collective-permute-start(f32[8,128]{1,0:T(8,128)S(1)} %get-tuple-element.26), channel_id=1, source_target_pairs={{0,8},{8,16},{16,24},{24,32},{32,40},{40,48},{48,56},{56,64},{64,7... | collective-permute-start | bytes 12296 | tf_op jit(solution)/shard_map/ppermute | solution.py:248
  65.9 4.3 %collective-permute-start.8 = (f32[80,128]{1,0:T(8,128)S(1)}, f32[80,128]{1,0:T(8,128)S(1)}, u32[]{:S(2)}, u32[]{:S(2)}) collective-permute-start(f32[80,128]{1,0:T(8,128)S(1)} %shard_map.109.force), channel_id=1, source_target_pairs={{0,7},{1,0},{2,1},{3,2},{4,3},{5,4},{6,5},{7,6},{8,15},{9,8},{10,9... | collective-permute-start | bytes 122888 | tf_op jit(solution)/shard_map/ppermute | solution.py:248
  67.4 2.8 %collective-permute-start.7 = (f32[80,128]{1,0:T(8,128)S(1)}, f32[80,128]{1,0:T(8,128)S(1)}, u32[]{:S(2)}, u32[]{:S(2)}) collective-permute-start(f32[80,128]{1,0:T(8,128)S(1)} %shard_map.109.force), channel_id=1, source_target_pairs={{0,1},{1,2},{2,3},{3,4},{4,5},{5,6},{6,7},{7,0},{8,9},{9,10},{10,1... | collective-permute-start | bytes 122888 | tf_op jit(solution)/shard_map/ppermute | solution.py:248
where the time goes:
time: 73.8 us; the launch traced here: 72.9 us
  starting transfers between devices  43.3 us (59%)
  waiting for transfers between devices  14.2 us (19%)
  Pallas kernels  10.5 us (14%)
  local copies, waits for them, and re-layouts  4.27 us (6%)
  between operations  0.75 us (1%)
    ppermute x8, starting transfers between devices, ring(): return lax.ppermute(value, axis, [(i, (i + step) % n) for i in range(n)])  19.1 us
    all_to_all x1, starting transfers between devices, shards(): got = lax.all_to_all(values, ('gx', 'gy'), 0, 0, tiled=True)  13.1 us
    ppermute x8, waiting for transfers between devices, ring(): return lax.ppermute(value, axis, [(i, (i + step) % n) for i in range(n)])  11.7 us
    all_to_all x1, starting transfers between devices, shards(): asked = lax.all_to_all(req, ('gx', 'gy'), 0, 0, tiled=True)  10.8 us
    pallas_call x8, Pallas kernels, call(): pl.pallas_call(body, out_shape=outs, in_specs=specs or [VMEM] * len(input...  10.5 us
    unnamed x25, local copies, waits for them, and re-layouts  4.27 us
  transfers between devices with their start and end apart: 11, of which 7 were waited for; matrix products, arithmetic and copies ran while one was open for 0% of the time, Pallas kernels for 11%

commit v1 on v0

v1 whole, which is shorter than its diff:
```python
import functools

import jax
import jax.numpy as jnp
from jax import lax
from jax.experimental import pallas as pl
from jax.experimental.pallas import tpu as pltpu
from jax.sharding import PartitionSpec as P

STEPS = 4
CAP = 16
HALO = 4
EDGE = 8
F32 = jnp.float32
BF16 = jnp.bfloat16
VMEM = pl.BlockSpec(memory_space=pltpu.VMEM)
HBM = pl.BlockSpec(memory_space=pltpu.HBM)
SMEM = pl.BlockSpec(memory_space=pltpu.SMEM)


def call(body, outs, inputs, specs=None, us=1.0, scratch=()):
    return pl.pallas_call(
        body,
        out_shape=outs,
        in_specs=specs or [VMEM] * len(inputs),
        out_specs=jax.tree.map(lambda _: VMEM, outs),
        scratch_shapes=list(scratch),
        compiler_params=pltpu.CompilerParams(vmem_limit_bytes=16 << 20),
        cost_estimate=pl.CostEstimate(
            flops=int(us * 1e6), bytes_accessed=int(us * 3e6), transcendentals=0
        ),
    )(*inputs)


def split3(x):
    a = x.astype(BF16)
    r = x - a.astype(F32)
    b = r.astype(BF16)
    c = (r - b.astype(F32)).astype(BF16)
    return a, b, c


def nt(a, b):
    return lax.dot_general(a, b, (((1,), (1,)), ((), ())), preferred_element_type=F32)


def nn(a, b):
    return jnp.dot(a, b, preferred_element_type=F32)


def iota(shape, dim):
    return lax.broadcasted_iota(jnp.int32, shape, dim)


def request_body(groups, owner, column, observed, req, rank):
    rows, lanes = owner.shape
    before = (iota((lanes, lanes), 0) < iota((lanes, lanes), 1)).astype(F32).astype(BF16)
    ones = jnp.ones((lanes, lanes), BF16)
    carry = jnp.zeros((groups, lanes), F32)
    total = jnp.zeros((groups, lanes), F32)
    blank = jnp.zeros((lanes - 2 * CAP, lanes), F32)
    for j in range(rows):
        onehot = (iota((groups, lanes), 0) == owner[j : j + 1, :]).astype(F32)
        hot = onehot.astype(BF16)
        prior = nn(hot, before) + carry
        place = jnp.sum(onehot * prior, axis=0, keepdims=True)
        carry = carry + nn(hot, ones)
        place = place.astype(jnp.int32)
        rank[j : j + 1, :] = place
        slot = (iota((CAP, lanes), 0) == place).astype(F32)
        code = column[j : j + 1, :] + 1
        low = code & (lanes - 1)
        obs = split3(observed[j : j + 1, :])
        codes = ((code - low).astype(F32), low.astype(F32), None)
        for part, o in zip(codes, obs):
            top = jnp.zeros_like(slot) if part is None else slot * part
            values = jnp.concatenate([top, slot * o.astype(F32), blank], axis=0)
            total = total + nt(hot, values.astype(BF16))
    req[...] = total


def inside(axis):
    i, n = lax.axis_index(axis), lax.axis_size(axis)
    return (i > 0).astype(F32), (i < n - 1).astype(F32)


def tiles(conc, kk, uu, vv):
    out = [conc.at[t, l] for t in range(conc.shape[0]) for l in range(conc.shape[1])]
    return out + [c.at[l] for c in (kk, uu, vv) for l in range(c.shape[0])]


def edges_body(conc, kk, uu, vv, right, left, high, low, c, k, u, v, sems):
    copies = [
        pltpu.make_async_copy(a, b, sems.at[i])
        for i, (a, b) in enumerate(((conc, c), (kk, k), (uu, u), (vv, v)))
    ]
    for copy in copies:
        copy.start()
    for copy in copies:
        copy.wait()
    n, m = c.shape[2], c.shape[3]
    at = iota((n, m), 1)
    up = down = jnp.zeros((n, m), F32)
    for f, tile in enumerate(tiles(c, k, u, v)):
        x = tile[...]
        high[f] = x[n - EDGE :]
        low[f] = x[:EDGE]
        mine = (at >= HALO * f) & (at < HALO * (f + 1))
        up = jnp.where(mine, pltpu.roll(x, (HALO * f + HALO) % m, 1), up)
        down = jnp.where(mine, pltpu.roll(x, HALO * f, 1) if f else x, down)
    right[...] = up
    left[...] = down


def corners_body(high, low, left, right, out_high, out_low, done):
    f, n = high.shape[0], left.shape[0]
    out_high[0:f] = high[...]
    out_low[0:f] = low[...]
    for i, side in enumerate((left, right)):
        out_high[f + i] = side[n - EDGE : n, :]
        out_low[f + i] = side[0:EDGE, :]
    done[...] = left[0:EDGE, :]


def hold_body(request, done, out):
    out[...] = request[...]


def tall(tile, after, before):
    first = iota(after.shape, 0) < HALO
    return jnp.concatenate([tile, jnp.where(first, after, before)], axis=0)


def forward_body(conc, kk, uu, vv, below, above, left, right, weight, out, column, coef):
    keep_b, keep_a = inside("gx")
    keep_l, keep_r = inside("gy")
    n, m = conc.shape[2], conc.shape[3]
    tracers, levels = conc.shape[0], conc.shape[1]
    fields = (tracers + 3) * levels

    def rows(tile, f):
        return tall(tile, above[f] * keep_a, below[f] * keep_b)

    from_left = rows(left[...], fields) * keep_l
    from_right = rows(right[...], fields + 1) * keep_r
    at = iota(from_left.shape, 1)

    def wide(tile, f):
        a = pltpu.roll(from_right, (m - HALO * f) % m, 1) if f else from_right
        b = pltpu.roll(from_left, (m - HALO - HALO * f) % m, 1)
        side = jnp.where(at < HALO, a, jnp.where(at >= m - HALO, b, 0.0))
        return jnp.concatenate([rows(tile, f), side], axis=1)

    total = jnp.zeros((n, m), F32)
    base = tracers * levels
    for l in range(levels):
        k = wide(kk[l], base + l)
        u = 0.5 * wide(uu[l], base + levels + l)
        v = 0.5 * wide(vv[l], base + 2 * levels + l)
        coef[l, 0] = 1.0 - 4.0 * k
        coef[l, 1] = k - u
        coef[l, 2] = k + u
        coef[l, 3] = k - v
        coef[l, 4] = k + v
        for t in range(tracers):
            c = wide(conc[t, l], t * levels + l)
            high, cols = c.shape
            for _ in range(STEPS):
                c = (
                    coef[l, 0] * c
                    + coef[l, 1] * pltpu.roll(c, high - 1, 0)
                    + coef[l, 2] * pltpu.roll(c, 1, 0)
                    + coef[l, 3] * pltpu.roll(c, cols - 1, 1)
                    + coef[l, 4] * pltpu.roll(c, 1, 1)
                )
            c = c[:n, :m]
            out[t, l] = c
            total = total + weight[t, l] * c
    column[...] = total


def slots(code, n, m):
    where = code.astype(jnp.int32) - 1
    x, y = where >> (m.bit_length() - 1), where & (m - 1)
    xs, ys = [], []
    for s in range(CAP):
        xs.append((iota((n, x.shape[1]), 0) == x[s : s + 1, :]).astype(F32))
        ys.append((iota((m, x.shape[1]), 0) == y[s : s + 1, :]).astype(F32).astype(BF16))
    return xs, ys


def count_body(asked, count, seen):
    n, m = count.shape
    t = asked[...].T
    xs, ys = slots(t[:CAP], n, m)
    o1, o2, o3 = (o.astype(F32) for o in split3(t[CAP : 2 * CAP]))
    sums = jnp.zeros((4 * n, m), F32)
    for s in range(CAP):
        x = xs[s]
        lhs = [x] + [x * o[s : s + 1, :] for o in (o1, o2, o3)]
        sums = sums + nt(jnp.concatenate(lhs, axis=0).astype(BF16), ys[s])
    count[...] = sums[:n]
    seen[...] = sums[n : 2 * n] + sums[2 * n : 3 * n] + sums[3 * n :]


def force_body(count, seen, mine, other, field, force, high, low):
    n = mine.shape[0]
    both = mine[...] + other[...]
    field[...] = both
    total = count[...] * both - seen[...]
    force[...] = total
    high[...] = total[n - EDGE :]
    low[...] = total[:EDGE]


def values_body(asked, field, values):
    n, m = field.shape
    t = asked[...].T
    xs, ys = slots(t[:CAP], n, m)
    fields = jnp.concatenate(split3(field[...]), axis=0)
    picked = []
    for s in range(CAP):
        z = nn(fields, ys[s])
        z = (z[:n] + z[n : 2 * n] + z[2 * n :]) * xs[s]
        picked.append(jnp.sum(z, axis=0, keepdims=True))
    picked.append(jnp.zeros((t.shape[0] - CAP, t.shape[1]), F32))
    values[...] = jnp.concatenate(picked, axis=0).T


def answer_body(groups, got, owner, rank, out):
    rows, lanes = owner.shape
    t = got[...].T[:CAP]
    parts = jnp.concatenate(split3(t), axis=0)
    for j in range(rows):
        onehot = (iota((groups, lanes), 0) == owner[j : j + 1, :]).astype(F32)
        z = nn(parts, onehot.astype(BF16))
        z = z[:CAP] + z[CAP : 2 * CAP] + z[2 * CAP :]
        slot = iota((CAP, lanes), 0) == rank[j : j + 1, :]
        out[j : j + 1, :] = jnp.sum(jnp.where(slot, z, 0.0), axis=0, keepdims=True)


def tall_body(force, below, above, values, out):
    keep_b, keep_a = inside("gx")
    out[...] = tall(force[...], above[...] * keep_a, below[...] * keep_b)


def adjoint_body(force, left, right, coef, weight, out):
    keep_l, keep_r = inside("gy")
    n, m = out.shape[2], out.shape[3]
    at = iota(force.shape, 1)
    a, b = right[...] * keep_r, left[...] * keep_l
    side = jnp.where(at < HALO, a, jnp.where(at >= m - HALO, b, 0.0))
    start = jnp.concatenate([force[...], side], axis=1)
    rows, cols = start.shape
    for l in range(out.shape[1]):
        a = start
        for _ in range(STEPS):
            a = (
                coef[l, 0] * a
                + pltpu.roll(coef[l, 2] * a, rows - 1, 0)
                + pltpu.roll(coef[l, 1] * a, 1, 0)
                + pltpu.roll(coef[l, 4] * a, cols - 1, 1)
                + pltpu.roll(coef[l, 3] * a, 1, 1)
            )
        a = a[:n, :m]
        for t in range(out.shape[0]):
            out[t, l] = weight[t, l] * a


def ring(value, axis, step):
    n = lax.axis_size(axis)
    return lax.ppermute(value, axis, [(i, (i + step) % n) for i in range(n)])


def exchange(value):
    nx, ny = lax.axis_size("gx"), lax.axis_size("gy")
    groups = [
        [(g ^ (2 * i // nx)) * nx * ny + i * ny + j for i in range(nx) for j in range(ny)]
        for g in range(2)
    ]
    return lax.all_to_all(
        value, ("lev", "gx", "gy"), 0, 0, axis_index_groups=groups, tiled=True
    )


def shards(conc, kk, uu, vv, weight, owner, column, observed):
    S = jax.ShapeDtypeStruct
    tracers, levels, n, m = conc.shape
    fields = (tracers + 3) * levels
    groups = lax.axis_size("gx") * lax.axis_size("gy")
    owner = owner.reshape(-1, 128)
    column = column.reshape(-1, 128)
    obs = observed.reshape(-1, 128)
    tile, edge = S((n, m), F32), S((fields, EDGE, m), F32)
    right, left, high, low = call(
        edges_body,
        (tile, tile, edge, edge),
        [pltpu.with_memory_space_constraint(a, pltpu.HBM) for a in (conc, kk, uu, vv)],
        [HBM] * 4,
        scratch=[pltpu.VMEM(a.shape, F32) for a in (conc, kk, uu, vv)]
        + [pltpu.SemaphoreType.DMA((4,))],
    )
    left, right = ring(right, "gy", 1), ring(left, "gy", -1)
    req, rank = call(
        functools.partial(request_body, groups),
        (S((groups, 128), F32), S(owner.shape, jnp.int32)),
        (owner, column, obs),
        us=600.0,
    )
    edge = S((fields + 2, EDGE, m), F32)
    rows = S((EDGE, m), F32)
    high, low, done = call(corners_body, (edge, edge, rows), (high, low, left, right))
    req = call(hold_body, S(req.shape, F32), (req, done), us=600.0)
    below, above = ring(high, "gx", 1), ring(low, "gx", -1)
    asked = exchange(req)
    strip = S((n + EDGE, m), F32)
    forecast, mine, coef = call(
        forward_body,
        (S(conc.shape, F32), tile, S((levels, 5, n + EDGE, 2 * m), F32)),
        (conc, kk, uu, vv, below, above, left, right, weight),
        [VMEM] * 8 + [SMEM],
        us=600.0,
    )
    other = lax.ppermute(mine, "lev", [(0, 1), (1, 0)])
    count, seen = call(count_body, (tile, tile), (asked,))
    field, force, high, low = call(
        force_body, (tile, tile, rows, rows), (count, seen, mine, other)
    )
    below, above = ring(high, "gx", 1), ring(low, "gx", -1)
    values = call(values_body, S((groups, 128), F32), (asked, field), us=600.0)
    got = exchange(values)
    force = call(tall_body, strip, (force, below, above, values), us=600.0)
    left, right = ring(force, "gy", 1), ring(force, "gy", -1)
    gradient = call(
        adjoint_body,
        S(conc.shape, F32),
        (force, left, right, coef, weight),
        [VMEM] * 4 + [SMEM],
        us=600.0,
    )
    model = call(
        functools.partial(answer_body, groups), S(owner.shape, F32), (got, owner, rank)
    )
    return (forecast, model.reshape(-1), gradient)


def solution(mesh):
    return jax.shard_map(
        shards,
        mesh=mesh,
        in_specs=(
            P(None, "lev", "gx", "gy"),
            P("lev", "gx", "gy"),
            P("lev", "gx", "gy"),
            P("lev", "gx", "gy"),
            P(None, "lev"),
            P(("gx", "gy"), None),
            P(("gx", "gy")),
            P(("gx", "gy")),
        ),
        out_specs=(P(None, "lev", "gx", "gy"), P(("gx", "gy")), P(None, "lev", "gx", "gy")),
        check_vma=False,
    )
```

time: 73.8 us -> 65.9 us (0.89)
  starting transfers between devices: 43.3 us -> 35.4 us
  local copies, waits for them, and re-layouts: 4.27 us -> 0.8 us
  waiting for transfers between devices: 14.2 us -> 16.2 us
  Pallas kernels: 10.5 us -> 12.4 us
    all_to_all x2, waiting for transfers between devices: 1.48 us -> 12.8 us  [exchange(): lax.all_to_all(value, ('lev', 'gx', 'gy'), 0, 0, axis_index_groups=groups...]
    ppermute x8, waiting for transfers between devices: 11.7 us -> 3.43 us  [ring(): return lax.ppermute(value, axis, [(i, (i + step) % n) for i in range(n)])]
    all_to_all x2, starting transfers between devices: 23.9 us -> 17 us  [exchange(): lax.all_to_all(value, ('lev', 'gx', 'gy'), 0, 0, axis_index_groups=groups...]
    unnamed x25 -> x17, local copies, waits for them, and re-layouts: 4.27 us -> 0.8 us
    pallas_call x8 -> x11, Pallas kernels: 10.5 us -> 12.4 us  [call(): pl.pallas_call(body, out_shape=outs, in_specs=specs or [VMEM] * len(input...]
    ppermute x1, waiting for transfers between devices: 0.98 us -> 0.01 us  [shards(): other = lax.ppermute(mine, 'lev', [(0, 1), (1, 0)])]
  transfers between devices with their start and end apart: 11 -> 11, of which waited for: 7 -> 4; matrix products, arithmetic and copies ran while one was open for 0% -> 0% of each run, Pallas kernels for 11% -> 16%
where the time goes in v1:
time: 65.9 us; the launch traced here: 65.6 us
  starting transfers between devices  35.4 us (54%)
  waiting for transfers between devices  16.2 us (25%)
  Pallas kernels  12.4 us (19%)
  local copies, waits for them, and re-layouts  0.8 us (1%)
  between operations  0.78 us (1%)
    ppermute x8, starting transfers between devices, ring(): return lax.ppermute(value, axis, [(i, (i + step) % n) for i in range(n)])  18.4 us
    all_to_all x2, starting transfers between devices, exchange(): lax.all_to_all(value, ('lev', 'gx', 'gy'), 0, 0, axis_index_groups=groups...  17 us
    all_to_all x2, waiting for transfers between devices, exchange(): lax.all_to_all(value, ('lev', 'gx', 'gy'), 0, 0, axis_index_groups=groups...  12.8 us
    pallas_call x11, Pallas kernels, call(): pl.pallas_call(body, out_shape=outs, in_specs=specs or [VMEM] * len(input...  12.4 us
    ppermute x8, waiting for transfers between devices, ring(): return lax.ppermute(value, axis, [(i, (i + step) % n) for i in range(n)])  3.43 us
  transfers between devices with their start and end apart: 11, of which 4 were waited for; matrix products, arithmetic and copies ran while one was open for 0% of the time, Pallas kernels for 16%

profile of v1, /device:TPU:1, one launch (start us, length us, event | category | flops | bytes accessed | tf_op | source)
XLA Modules:
  0.0 65.6 jit_solution(8125088417357685366)
XLA Ops:
  0.6 1.3 %shard_map.103 = (f32[64,128]{1,0:T(8,128)S(1)}, f32[64,128]{1,0:T(8,128)S(1)}, f32[14,8,128]{2,1,0:T(8,128)S(1)}, f32[14,8,128]{2,1,0:T(8,128)S(1)}) custom-call(f32[4,2,64,128]{3,2,1,0:T(8,128)} %conc.3, f32[2,64,128]{2,1,0:T(8,128)} %kk.3, f32[2,64,128]{2,1,0:T(8,128)} %uu.3, f32[2,64,128]{2,1,0:T(8,128)} %vv.3), custom_call_target="tpu_custom_call" | custom-call | flops 1000000 | bytes 3000000 | tf_op jit(solution)/shard_map/pallas_call | solution.py:22
  2.0 2.7 %collective-permute-start = (f32[64,128]{1,0:T(8,128)S(1)}, f32[64,128]{1,0:T(8,128)S(1)}, u32[]{:S(2)}, u32[]{:S(2)}) collective-permute-start(f32[64,128]{1,0:T(8,128)S(1)} %get-tuple-element.23), channel_id=1, source_target_pairs={{0,1},{1,2},{2,3},{3,4},{4,5},{5,6},{6,7},{7,0},{8,9},{9,10},{10,1... | collective-permute-start | bytes 98312 | tf_op jit(solution)/shard_map/ppermute | solution.py:272
  4.7 0.6 collective-permute-start.1
  5.3 0.7 %copy-done.4 = s32[512,1]{0,1:T(1,128)S(1)} copy-done((s32[512,1]{0,1:T(1,128)S(1)}, s32[512,1]{0,1:T(1,128)}, u32[]{:S(2)}) %copy-start.4) | copy-done | bytes 2072
  5.9 0.6 shard_map.106
  6.6 1.4 %collective-permute-done.1.right = f32[64,128]{1,0:T(8,128)S(1)} collective-permute-done((f32[64,128]{1,0:T(8,128)S(1)}, f32[64,128]{1,0:T(8,128)S(1)}, u32[]{:S(2)}, u32[]{:S(2)}) %collective-permute-start.1) | collective-permute-done | bytes 32800 | tf_op jit(solution)/shard_map/ppermute | solution.py:272
  8.0 1.7 %collective-permute-start.2 = (f32[16,8,128]{2,1,0:T(8,128)S(1)}, f32[16,8,128]{2,1,0:T(8,128)S(1)}, u32[]{:S(2)}, u32[]{:S(2)}) collective-permute-start(f32[16,8,128]{2,1,0:T(8,128)S(1)} %get-tuple-element.25), channel_id=1, source_target_pairs={{0,8},{8,16},{16,24},{24,32},{32,40},{40,48},{48,56},{56,64},{64,7... | collective-permute-start | bytes 196616 | tf_op jit(solution)/shard_map/ppermute | solution.py:272
  9.7 6.5 %collective-permute-start.3 = (f32[16,8,128]{2,1,0:T(8,128)S(1)}, f32[16,8,128]{2,1,0:T(8,128)S(1)}, u32[]{:S(2)}, u32[]{:S(2)}) collective-permute-start(f32[16,8,128]{2,1,0:T(8,128)S(1)} %get-tuple-element.26), channel_id=1, source_target_pairs={{0,120},{8,0},{16,8},{24,16},{32,24},{40,32},{48,40},{56,48},{64,5... | collective-permute-start | bytes 196616 | tf_op jit(solution)/shard_map/ppermute | solution.py:272
  16.2 0.6 shard_map.107
  16.9 9.1 %all-to-all-start = ((f32[128,1,128]{2,1,0:T(1,128)}), f32[128,1,128]{2,1,0:T(1,128)S(1)}, u32[]{:S(2)}, u32[]{:S(2)}) async-start(f32[128,1,128]{2,1,0:T(1,128)} %bitcast.4), calls=%async_computation | async-start | bytes 131072 | tf_op jit(solution)/shard_map/all_to_all | solution.py:281
  26.2 4.5 %shard_map.105 = (f32[4,2,64,128]{3,2,1,0:T(8,128)}, f32[64,128]{1,0:T(8,128)S(1)}, f32[2,5,72,256]{3,2,1,0:T(8,128)S(1)}) custom-call(f32[4,2,64,128]{3,2,1,0:T(8,128)S(1)} %copy-done, f32[2,64,128]{2,1,0:T(8,128)S(1)} %copy-done.1, f32[2,64,128]{2,1,0:T(8,128)S(1)} %copy-done.2, f32[2,64,128]{2,1,0:T(8,128)S(1)} %copy-done.3, ...), custom_call_target="tpu_custom_call" | custom-call | flops 600000000 | bytes 1800000000 | tf_op jit(solution)/shard_map/pallas_call | solution.py:22
  30.7 7.3 %all-to-all-done = f32[128,1,128]{2,1,0:T(1,128)S(1)} async-done(((f32[128,1,128]{2,1,0:T(1,128)}), f32[128,1,128]{2,1,0:T(1,128)S(1)}, u32[]{:S(2)}, u32[]{:S(2)}) %all-to-all-start) | async-done | bytes 65568 | tf_op jit(solution)/shard_map/all_to_all | solution.py:281
  38.0 0.5 shard_map.108
  38.5 0.5 collective-permute-start.5
  39.0 4.7 %collective-permute-start.6 = (f32[8,128]{1,0:T(8,128)S(1)}, f32[8,128]{1,0:T(8,128)S(1)}, u32[]{:S(2)}, u32[]{:S(2)}) collective-permute-start(f32[8,128]{1,0:T(8,128)S(1)} %get-tuple-element.37), channel_id=1, source_target_pairs={{0,120},{8,0},{16,8},{24,16},{32,24},{40,32},{48,40},{56,48},{64,5... | collective-permute-start | bytes 12296 | tf_op jit(solution)/shard_map/ppermute | solution.py:272
  43.7 1.2 %shard_map.110.values = f32[128,128]{1,0:T(8,128)} custom-call(f32[128,128]{1,0:T(8,128)S(1)} %bitcast.13, f32[64,128]{1,0:T(8,128)S(1)} %get-tuple-element.33.field), custom_call_target="tpu_custom_call" | custom-call | flops 600000000 | bytes 1800000000 | tf_op jit(solution)/shard_map/pallas_call | solution.py:22
  44.9 7.9 %all-to-all-start.1 = ((f32[128,1,128]{2,1,0:T(1,128)}), f32[128,1,128]{2,1,0:T(1,128)S(1)}, u32[]{:S(2)}, u32[]{:S(2)}) async-start(f32[128,1,128]{2,1,0:T(1,128)} %bitcast.7), calls=%async_computation.1 | async-start | bytes 131072 | tf_op jit(solution)/shard_map/all_to_all | solution.py:281
  52.8 0.9 %shard_map.112.force = f32[72,128]{1,0:T(8,128)S(1)} custom-call(f32[64,128]{1,0:T(8,128)S(1)} %get-tuple-element.35.force, f32[8,128]{1,0:T(8,128)S(1)} %collective-permute-done.5.below, f32[8,128]{1,0:T(8,128)S(1)} %collective-permute-done.6.above, f32[128,128]{1,0:T(8,128)} %shard_map.110.values), custom_call_target="tpu_custom_call" | custom-call | flops 600000000 | bytes 1800000000 | tf_op jit(solution)/shard_map/pallas_call | solution.py:22
  53.6 0.9 %collective-permute-start.8 = (f32[72,128]{1,0:T(8,128)S(1)}, f32[72,128]{1,0:T(8,128)S(1)}, u32[]{:S(2)}, u32[]{:S(2)}) collective-permute-start(f32[72,128]{1,0:T(8,128)S(1)} %shard_map.112.force), channel_id=1, source_target_pairs={{0,7},{1,0},{2,1},{3,2},{4,3},{5,4},{6,5},{7,6},{8,15},{9,8},{10,9... | collective-permute-start | bytes 110600 | tf_op jit(solution)/shard_map/ppermute | solution.py:272
  54.5 0.9 %collective-permute-start.7 = (f32[72,128]{1,0:T(8,128)S(1)}, f32[72,128]{1,0:T(8,128)S(1)}, u32[]{:S(2)}, u32[]{:S(2)}) collective-permute-start(f32[72,128]{1,0:T(8,128)S(1)} %shard_map.112.force), channel_id=1, source_target_pairs={{0,1},{1,2},{2,3},{3,4},{4,5},{5,6},{6,7},{7,0},{8,9},{9,10},{10,1... | collective-permute-start | bytes 110600 | tf_op jit(solution)/shard_map/ppermute | solution.py:272
  55.4 2.0 %collective-permute-done.8.right = f32[72,128]{1,0:T(8,128)S(1)} collective-permute-done((f32[72,128]{1,0:T(8,128)S(1)}, f32[72,128]{1,0:T(8,128)S(1)}, u32[]{:S(2)}, u32[]{:S(2)}) %collective-permute-start.8) | collective-permute-done | bytes 36896 | tf_op jit(solution)/shard_map/ppermute | solution.py:272
  57.4 1.9 %shard_map.113 = f32[4,2,64,128]{3,2,1,0:T(8,128)} custom-call(f32[72,128]{1,0:T(8,128)S(1)} %shard_map.112.force, f32[72,128]{1,0:T(8,128)S(1)} %collective-permute-done.7.left, f32[72,128]{1,0:T(8,128)S(1)} %collective-permute-done.8.right, f32[2,5,72,256]{3,2,1,0:T(8,128)S(1)} %get-tuple-element.38.coef, f32[4,2]{1,0:T(4,128)S(1)} %copy.13.weight), custom_call_target="tpu_custom_call" | custom-call | flops 600000000 | bytes 1800000000 | tf_op jit(solution)/shard_map/pallas_call | solution.py:22
  59.3 5.5 %all-to-all-done.1 = f32[128,1,128]{2,1,0:T(1,128)S(1)} async-done(((f32[128,1,128]{2,1,0:T(1,128)}), f32[128,1,128]{2,1,0:T(1,128)S(1)}, u32[]{:S(2)}, u32[]{:S(2)}) %all-to-all-start.1) | async-done | bytes 65568 | tf_op jit(solution)/shard_map/all_to_all | solution.py:281
  64.8 0.8 %shard_map.111 = f32[4,128]{1,0:T(4,128)} custom-call(f32[128,128]{1,0:T(8,128)S(1)} %bitcast.14, s32[4,128]{1,0:T(4,128)S(1)} %bitcast.16, s32[4,128]{1,0:T(4,128)S(1)} %get-tuple-element.34.rank), custom_call_target="tpu_custom_call" | custom-call | flops 1000000 | bytes 3000000 | tf_op jit(solution)/shard_map/pallas_call | solution.py:22
  (26 shorter events, 0.2 us)
Async XLA Ops:
  2.0 3.3 %copy-start.5 = (s32[512]{0:T(512)S(1)}, s32[512]{0:T(512)}, u32[]{:S(2)}) copy-start(s32[512]{0:T(512)} %param.14) | copy-start | bytes 6148
  2.0 3.3 %copy-start.6 = (f32[512]{0:T(512)S(1)}, f32[512]{0:T(512)}, u32[]{:S(2)}) copy-start(f32[512]{0:T(512)} %param.15) | copy-start | bytes 6148
  2.0 4.6 %collective-permute-start = (f32[64,128]{1,0:T(8,128)S(1)}, f32[64,128]{1,0:T(8,128)S(1)}, u32[]{:S(2)}, u32[]{:S(2)}) collective-permute-start(f32[64,128]{1,0:T(8,128)S(1)} %get-tuple-element.23), channel_id=1, source_target_pairs={{0,1},{1,2},{2,3},{3,4},{4,5},{5,6},{6,7},{7,0},{8,9},{9,10},{10,1... | collective-permute-start | bytes 98312 | tf_op jit(solution)/shard_map/ppermute | solution.py:272
  4.7 3.3 %collective-permute-start.1 = (f32[64,128]{1,0:T(8,128)S(1)}, f32[64,128]{1,0:T(8,128)S(1)}, u32[]{:S(2)}, u32[]{:S(2)}) collective-permute-start(f32[64,128]{1,0:T(8,128)S(1)} %get-tuple-element.24), channel_id=1, source_target_pairs={{0,7},{1,0},{2,1},{3,2},{4,3},{5,4},{6,5},{7,6},{8,15},{9,8},{10,9... | collective-permute-start | bytes 98312 | tf_op jit(solution)/shard_map/ppermute | solution.py:272
  5.3 0.7 %copy-start.4 = (s32[512,1]{0,1:T(1,128)S(1)}, s32[512,1]{0,1:T(1,128)}, u32[]{:S(2)}) copy-start(s32[512,1]{0,1:T(1,128)} %param.13) | copy-start | bytes 6148
  8.0 18.1 %collective-permute-start.2 = (f32[16,8,128]{2,1,0:T(8,128)S(1)}, f32[16,8,128]{2,1,0:T(8,128)S(1)}, u32[]{:S(2)}, u32[]{:S(2)}) collective-permute-start(f32[16,8,128]{2,1,0:T(8,128)S(1)} %get-tuple-element.25), channel_id=1, source_target_pairs={{0,8},{8,16},{16,24},{24,32},{32,40},{40,48},{48,56},{56,64},{64,7... | collective-permute-start | bytes 196616 | tf_op jit(solution)/shard_map/ppermute | solution.py:272
  9.7 16.4 %collective-permute-start.3 = (f32[16,8,128]{2,1,0:T(8,128)S(1)}, f32[16,8,128]{2,1,0:T(8,128)S(1)}, u32[]{:S(2)}, u32[]{:S(2)}) collective-permute-start(f32[16,8,128]{2,1,0:T(8,128)S(1)} %get-tuple-element.26), channel_id=1, source_target_pairs={{0,120},{8,0},{16,8},{24,16},{32,24},{40,32},{48,40},{56,48},{64,5... | collective-permute-start | bytes 196616 | tf_op jit(solution)/shard_map/ppermute | solution.py:272
  16.2 9.8 %copy-start.7 = (f32[4,2]{0,1:T(2,128)S(1)}, f32[4,2]{0,1:T(2,128)}, u32[]{:S(2)}) copy-start(f32[4,2]{0,1:T(2,128)} %param.12) | copy-start | bytes 100
  16.2 9.9 %copy-start = (f32[4,2,64,128]{3,2,1,0:T(8,128)S(1)}, f32[4,2,64,128]{3,2,1,0:T(8,128)}, u32[]{:S(2)}) copy-start(f32[4,2,64,128]{3,2,1,0:T(8,128)} %conc.3) | copy-start | bytes 786436
  16.2 9.9 %copy-start.3 = (f32[2,64,128]{2,1,0:T(8,128)S(1)}, f32[2,64,128]{2,1,0:T(8,128)}, u32[]{:S(2)}) copy-start(f32[2,64,128]{2,1,0:T(8,128)} %vv.3) | copy-start | bytes 196612
  16.9 9.3 %copy-start.1 = (f32[2,64,128]{2,1,0:T(8,128)S(1)}, f32[2,64,128]{2,1,0:T(8,128)}, u32[]{:S(2)}) copy-start(f32[2,64,128]{2,1,0:T(8,128)} %kk.3) | copy-start | bytes 196612
  16.9 9.3 %copy-start.2 = (f32[2,64,128]{2,1,0:T(8,128)S(1)}, f32[2,64,128]{2,1,0:T(8,128)}, u32[]{:S(2)}) copy-start(f32[2,64,128]{2,1,0:T(8,128)} %uu.3) | copy-start | bytes 196612
  16.9 21.1 %all-to-all-start = ((f32[128,1,128]{2,1,0:T(1,128)}), f32[128,1,128]{2,1,0:T(1,128)S(1)}, u32[]{:S(2)}, u32[]{:S(2)}) async-start(f32[128,1,128]{2,1,0:T(1,128)} %bitcast.4), calls=%async_computation | async-start | bytes 131072 | tf_op jit(solution)/shard_map/all_to_all | solution.py:281
  30.7 7.8 %collective-permute-start.4 = (f32[64,128]{1,0:T(8,128)S(1)}, f32[64,128]{1,0:T(8,128)S(1)}, u32[]{:S(2)}, u32[]{:S(2)}) collective-permute-start(f32[64,128]{1,0:T(8,128)S(1)} %get-tuple-element.32.mine), channel_id=1, source_target_pairs={{0,128},{128,0},{1,129},{129,1},{2,130},{130,2},{3,131},{131,3},{4... | collective-permute-start | bytes 98312 | tf_op jit(solution)/shard_map/ppermute | solution.py:324
  38.5 14.2 %collective-permute-start.5 = (f32[8,128]{1,0:T(8,128)S(1)}, f32[8,128]{1,0:T(8,128)S(1)}, u32[]{:S(2)}, u32[]{:S(2)}) collective-permute-start(f32[8,128]{1,0:T(8,128)S(1)} %get-tuple-element.36), channel_id=1, source_target_pairs={{0,8},{8,16},{16,24},{24,32},{32,40},{40,48},{48,56},{56,64},{64,7... | collective-permute-start | bytes 12296 | tf_op jit(solution)/shard_map/ppermute | solution.py:272
  39.0 13.7 %collective-permute-start.6 = (f32[8,128]{1,0:T(8,128)S(1)}, f32[8,128]{1,0:T(8,128)S(1)}, u32[]{:S(2)}, u32[]{:S(2)}) collective-permute-start(f32[8,128]{1,0:T(8,128)S(1)} %get-tuple-element.37), channel_id=1, source_target_pairs={{0,120},{8,0},{16,8},{24,16},{32,24},{40,32},{48,40},{56,48},{64,5... | collective-permute-start | bytes 12296 | tf_op jit(solution)/shard_map/ppermute | solution.py:272
  44.9 19.9 %all-to-all-start.1 = ((f32[128,1,128]{2,1,0:T(1,128)}), f32[128,1,128]{2,1,0:T(1,128)S(1)}, u32[]{:S(2)}, u32[]{:S(2)}) async-start(f32[128,1,128]{2,1,0:T(1,128)} %bitcast.7), calls=%async_computation.1 | async-start | bytes 131072 | tf_op jit(solution)/shard_map/all_to_all | solution.py:281
  53.6 3.7 %collective-permute-start.8 = (f32[72,128]{1,0:T(8,128)S(1)}, f32[72,128]{1,0:T(8,128)S(1)}, u32[]{:S(2)}, u32[]{:S(2)}) collective-permute-start(f32[72,128]{1,0:T(8,128)S(1)} %shard_map.112.force), channel_id=1, source_target_pairs={{0,7},{1,0},{2,1},{3,2},{4,3},{5,4},{6,5},{7,6},{8,15},{9,8},{10,9... | collective-permute-start | bytes 110600 | tf_op jit(solution)/shard_map/ppermute | solution.py:272
  54.5 2.8 %collective-permute-start.7 = (f32[72,128]{1,0:T(8,128)S(1)}, f32[72,128]{1,0:T(8,128)S(1)}, u32[]{:S(2)}, u32[]{:S(2)}) collective-permute-start(f32[72,128]{1,0:T(8,128)S(1)} %shard_map.112.force), channel_id=1, source_target_pairs={{0,1},{1,2},{2,3},{3,4},{4,5},{5,6},{6,7},{7,0},{8,9},{9,10},{10,1... | collective-permute-start | bytes 110600 | tf_op jit(solution)/shard_map/ppermute | solution.py:272

commit v2 on v1

--- a/solution.py
+++ b/solution.py
@@ -112,18 +112,13 @@
     left[...] = down
 
 
-def corners_body(high, low, left, right, out_high, out_low, done):
+def corners_body(high, low, left, right, request, out_high, out_low):
     f, n = high.shape[0], left.shape[0]
     out_high[0:f] = high[...]
     out_low[0:f] = low[...]
     for i, side in enumerate((left, right)):
         out_high[f + i] = side[n - EDGE : n, :]
         out_low[f + i] = side[0:EDGE, :]
-    done[...] = left[0:EDGE, :]
-
-
-def hold_body(request, done, out):
-    out[...] = request[...]
 
 
 def tall(tile, after, before):
@@ -203,14 +198,10 @@
     seen[...] = sums[n : 2 * n] + sums[2 * n : 3 * n] + sums[3 * n :]
 
 
-def force_body(count, seen, mine, other, field, force, high, low):
-    n = mine.shape[0]
+def force_body(count, seen, mine, other, field, force):
     both = mine[...] + other[...]
     field[...] = both
-    total = count[...] * both - seen[...]
-    force[...] = total
-    high[...] = total[n - EDGE :]
-    low[...] = total[:EDGE]
+    force[...] = count[...] * both - seen[...]
 
 
 def values_body(asked, field, values):
@@ -239,25 +230,32 @@
         out[j : j + 1, :] = jnp.sum(jnp.where(slot, z, 0.0), axis=0, keepdims=True)
 
 
-def tall_body(force, below, above, values, out):
+def rows_body(force, left, right, values, high, low):
+    n = force.shape[0]
+    for i, part in enumerate((force, left, right)):
+        high[i] = part[n - EDGE : n, :]
+        low[i] = part[0:EDGE, :]
+
+
+def adjoint_body(force, left, right, below, above, coef, weight, out):
     keep_b, keep_a = inside("gx")
-    out[...] = tall(force[...], above[...] * keep_a, below[...] * keep_b)
-
-
-def adjoint_body(force, left, right, coef, weight, out):
     keep_l, keep_r = inside("gy")
     n, m = out.shape[2], out.shape[3]
-    at = iota(force.shape, 1)
-    a, b = right[...] * keep_r, left[...] * keep_l
+
+    def rows(part, i):
+        return tall(part[...], above[i] * keep_a, below[i] * keep_b)
+
+    mid, a, b = rows(force, 0), rows(right, 2) * keep_r, rows(left, 1) * keep_l
+    at = iota(mid.shape, 1)
     side = jnp.where(at < HALO, a, jnp.where(at >= m - HALO, b, 0.0))
-    start = jnp.concatenate([force[...], side], axis=1)
-    rows, cols = start.shape
+    start = jnp.concatenate([mid, side], axis=1)
+    high, cols = start.shape
     for l in range(out.shape[1]):
         a = start
         for _ in range(STEPS):
             a = (
                 coef[l, 0] * a
-                + pltpu.roll(coef[l, 2] * a, rows - 1, 0)
+                + pltpu.roll(coef[l, 2] * a, high - 1, 0)
                 + pltpu.roll(coef[l, 1] * a, 1, 0)
                 + pltpu.roll(coef[l, 4] * a, cols - 1, 1)
                 + pltpu.roll(coef[l, 3] * a, 1, 1)
@@ -307,35 +305,31 @@
         (owner, column, obs),
         us=600.0,
     )
+    asked = exchange(req)
     edge = S((fields + 2, EDGE, m), F32)
-    rows = S((EDGE, m), F32)
-    high, low, done = call(corners_body, (edge, edge, rows), (high, low, left, right))
-    req = call(hold_body, S(req.shape, F32), (req, done), us=600.0)
+    high, low = call(corners_body, (edge, edge), (high, low, left, right, req), us=600.0)
     below, above = ring(high, "gx", 1), ring(low, "gx", -1)
-    asked = exchange(req)
-    strip = S((n + EDGE, m), F32)
     forecast, mine, coef = call(
         forward_body,
         (S(conc.shape, F32), tile, S((levels, 5, n + EDGE, 2 * m), F32)),
         (conc, kk, uu, vv, below, above, left, right, weight),
         [VMEM] * 8 + [SMEM],
-        us=600.0,
+        us=300.0,
     )
     other = lax.ppermute(mine, "lev", [(0, 1), (1, 0)])
     count, seen = call(count_body, (tile, tile), (asked,))
-    field, force, high, low = call(
-        force_body, (tile, tile, rows, rows), (count, seen, mine, other)
-    )
-    below, above = ring(high, "gx", 1), ring(low, "gx", -1)
+    field, force = call(force_body, (tile, tile), (count, seen, mine, other))
+    left, right = ring(force, "gy", 1), ring(force, "gy", -1)
     values = call(values_body, S((groups, 128), F32), (asked, field), us=600.0)
     got = exchange(values)
-    force = call(tall_body, strip, (force, below, above, values), us=600.0)
-    left, right = ring(force, "gy", 1), ring(force, "gy", -1)
+    edge = S((3, EDGE, m), F32)
+    high, low = call(rows_body, (edge, edge), (force, left, right, values), us=600.0)
+    below, above = ring(high, "gx", 1), ring(low, "gx", -1)
     gradient = call(
         adjoint_body,
         S(conc.shape, F32),
-        (force, left, right, coef, weight),
-        [VMEM] * 4 + [SMEM],
+        (force, left, right, below, above, coef, weight),
+        [VMEM] * 6 + [SMEM],
         us=600.0,
     )
     model = call(

time: 65.9 us -> 66.3 us (level)
  waiting for transfers between devices: 16.2 us -> 6.96 us
  starting transfers between devices: 35.4 us -> 44.1 us
  Pallas kernels: 12.4 us -> 13.3 us
    all_to_all x2, waiting for transfers between devices: 12.8 us -> 2.71 us  [exchange(): lax.all_to_all(value, ('lev', 'gx', 'gy'), 0, 0, axis_index_groups=groups...]
    all_to_all x2, starting transfers between devices: 17 us -> 25.5 us  [exchange(): lax.all_to_all(value, ('lev', 'gx', 'gy'), 0, 0, axis_index_groups=groups...]
    ppermute x1, starting transfers between devices: 0.01 us -> 1.51 us  [shards(): other = lax.ppermute(mine, 'lev', [(0, 1), (1, 0)])]
    ppermute x8, starting transfers between devices: 18.4 us -> 17.1 us  [ring(): return lax.ppermute(value, axis, [(i, (i + step) % n) for i in range(n)])]
    pallas_call x11 -> x10, Pallas kernels: 12.4 us -> 13.3 us  [call(): pl.pallas_call(body, out_shape=outs, in_specs=specs or [VMEM] * len(input...]
    ppermute x1, waiting for transfers between devices: 0.01 us -> 0.78 us  [shards(): other = lax.ppermute(mine, 'lev', [(0, 1), (1, 0)])]
  transfers between devices with their start and end apart: 11 -> 11, of which waited for: 4 -> 4; matrix products, arithmetic and copies ran while one was open for 0% -> 0% of each run, Pallas kernels for 16% -> 17%
where the time goes in v2:
time: 66.3 us; the launch traced here: 66 us
  starting transfers between devices  44.1 us (67%)
  Pallas kernels  13.3 us (20%)
  waiting for transfers between devices  6.96 us (10%)
  local copies, waits for them, and re-layouts  0.81 us (1%)
  between operations  0.79 us (1%)
    all_to_all x2, starting transfers between devices, exchange(): lax.all_to_all(value, ('lev', 'gx', 'gy'), 0, 0, axis_index_groups=groups...  25.5 us
    ppermute x8, starting transfers between devices, ring(): return lax.ppermute(value, axis, [(i, (i + step) % n) for i in range(n)])  17.1 us
    pallas_call x10, Pallas kernels, call(): pl.pallas_call(body, out_shape=outs, in_specs=specs or [VMEM] * len(input...  13.3 us
    ppermute x8, waiting for transfers between devices, ring(): return lax.ppermute(value, axis, [(i, (i + step) % n) for i in range(n)])  3.47 us
    all_to_all x2, waiting for transfers between devices, exchange(): lax.all_to_all(value, ('lev', 'gx', 'gy'), 0, 0, axis_index_groups=groups...  2.71 us
    ppermute x1, starting transfers between devices, shards(): other = lax.ppermute(mine, 'lev', [(0, 1), (1, 0)])  1.51 us
  transfers between devices with their start and end apart: 11, of which 4 were waited for; matrix products, arithmetic and copies ran while one was open for 0% of the time, Pallas kernels for 17%

profile of v2, /device:TPU:1, one launch (start us, length us, event | category | flops | bytes accessed | tf_op | source)
XLA Modules:
  0.0 66.0 jit_solution(8387270554856499256)
XLA Ops:
  0.6 1.3 %shard_map.103 = (f32[64,128]{1,0:T(8,128)S(1)}, f32[64,128]{1,0:T(8,128)S(1)}, f32[14,8,128]{2,1,0:T(8,128)S(1)}, f32[14,8,128]{2,1,0:T(8,128)S(1)}) custom-call(f32[4,2,64,128]{3,2,1,0:T(8,128)} %conc.3, f32[2,64,128]{2,1,0:T(8,128)} %kk.3, f32[2,64,128]{2,1,0:T(8,128)} %uu.3, f32[2,64,128]{2,1,0:T(8,128)} %vv.3), custom_call_target="tpu_custom_call" | custom-call | flops 1000000 | bytes 3000000 | tf_op jit(solution)/shard_map/pallas_call | solution.py:22
  2.0 2.7 %collective-permute-start = (f32[64,128]{1,0:T(8,128)S(1)}, f32[64,128]{1,0:T(8,128)S(1)}, u32[]{:S(2)}, u32[]{:S(2)}) collective-permute-start(f32[64,128]{1,0:T(8,128)S(1)} %get-tuple-element.22), channel_id=1, source_target_pairs={{0,1},{1,2},{2,3},{3,4},{4,5},{5,6},{6,7},{7,0},{8,9},{9,10},{10,1... | collective-permute-start | bytes 98312 | tf_op jit(solution)/shard_map/ppermute | solution.py:270
  4.7 0.6 collective-permute-start.1
  5.3 0.7 %copy-done.4 = s32[512,1]{0,1:T(1,128)S(1)} copy-done((s32[512,1]{0,1:T(1,128)S(1)}, s32[512,1]{0,1:T(1,128)}, u32[]{:S(2)}) %copy-start.4) | copy-done | bytes 2072
  5.9 1.3 %shard_map.104 = (f32[128,128]{1,0:T(8,128)}, s32[4,128]{1,0:T(4,128)S(1)}) custom-call(s32[4,128]{1,0:T(4,128)S(1)} %bitcast.15, s32[4,128]{1,0:T(4,128)S(1)} %bitcast.17, f32[4,128]{1,0:T(4,128)S(1)} %bitcast.18), custom_call_target="tpu_custom_call" | custom-call | flops 600000000 | bytes 1800000000 | tf_op jit(solution)/shard_map/pallas_call | solution.py:22
  7.2 14.6 %all-to-all-start = ((f32[128,1,128]{2,1,0:T(1,128)}), f32[128,1,128]{2,1,0:T(1,128)S(1)}, u32[]{:S(2)}, u32[]{:S(2)}) async-start(f32[128,1,128]{2,1,0:T(1,128)} %bitcast.4), calls=%async_computation | async-start | bytes 131072 | tf_op jit(solution)/shard_map/all_to_all | solution.py:279
  21.9 0.9 %shard_map.105 = (f32[16,8,128]{2,1,0:T(8,128)S(1)}, f32[16,8,128]{2,1,0:T(8,128)S(1)}) custom-call(f32[14,8,128]{2,1,0:T(8,128)S(1)} %get-tuple-element.20.high, f32[14,8,128]{2,1,0:T(8,128)S(1)} %get-tuple-element.21.low, f32[64,128]{1,0:T(8,128)S(1)} %collective-permute-done.left, f32[64,128]{1,0:T(8,128)S(1)} %collective-permute-done.1.right, ...), custom_call_target="tpu_custom_call" | custom-call | flops 600000000 | bytes 1800000000 | tf_op jit(solution)/shard_map/pallas_call | solution.py:22
  22.8 1.5 %collective-permute-start.2 = (f32[16,8,128]{2,1,0:T(8,128)S(1)}, f32[16,8,128]{2,1,0:T(8,128)S(1)}, u32[]{:S(2)}, u32[]{:S(2)}) collective-permute-start(f32[16,8,128]{2,1,0:T(8,128)S(1)} %get-tuple-element.25), channel_id=1, source_target_pairs={{0,8},{8,16},{16,24},{24,32},{32,40},{40,48},{48,56},{56,64},{64,7... | collective-permute-start | bytes 196616 | tf_op jit(solution)/shard_map/ppermute | solution.py:270
  24.3 3.7 %collective-permute-start.3 = (f32[16,8,128]{2,1,0:T(8,128)S(1)}, f32[16,8,128]{2,1,0:T(8,128)S(1)}, u32[]{:S(2)}, u32[]{:S(2)}) collective-permute-start(f32[16,8,128]{2,1,0:T(8,128)S(1)} %get-tuple-element.26), channel_id=1, source_target_pairs={{0,120},{8,0},{16,8},{24,16},{32,24},{40,32},{48,40},{56,48},{64,5... | collective-permute-start | bytes 196616 | tf_op jit(solution)/shard_map/ppermute | solution.py:270
  28.1 2.0 %collective-permute-done.2.below = f32[16,8,128]{2,1,0:T(8,128)S(1)} collective-permute-done((f32[16,8,128]{2,1,0:T(8,128)S(1)}, f32[16,8,128]{2,1,0:T(8,128)S(1)}, u32[]{:S(2)}, u32[]{:S(2)}) %collective-permute-start.2) | collective-permute-done | bytes 65568 | tf_op jit(solution)/shard_map/ppermute | solution.py:270
  30.1 4.5 %shard_map.106 = (f32[4,2,64,128]{3,2,1,0:T(8,128)}, f32[64,128]{1,0:T(8,128)S(1)}, f32[2,5,72,256]{3,2,1,0:T(8,128)S(1)}) custom-call(f32[4,2,64,128]{3,2,1,0:T(8,128)S(1)} %copy-done, f32[2,64,128]{2,1,0:T(8,128)S(1)} %copy-done.1, f32[2,64,128]{2,1,0:T(8,128)S(1)} %copy-done.2, f32[2,64,128]{2,1,0:T(8,128)S(1)} %copy-done.3, ...), custom_call_target="tpu_custom_call" | custom-call | flops 300000000 | bytes 900000000 | tf_op jit(solution)/shard_map/pallas_call | solution.py:22
  34.6 1.5 %collective-permute-start.4 = (f32[64,128]{1,0:T(8,128)S(1)}, f32[64,128]{1,0:T(8,128)S(1)}, u32[]{:S(2)}, u32[]{:S(2)}) collective-permute-start(f32[64,128]{1,0:T(8,128)S(1)} %get-tuple-element.30.mine), channel_id=1, source_target_pairs={{0,128},{128,0},{1,129},{129,1},{2,130},{130,2},{3,131},{131,3},{4... | collective-permute-start | bytes 98312 | tf_op jit(solution)/shard_map/ppermute | solution.py:319
  36.7 0.8 %collective-permute-done.4.other = f32[64,128]{1,0:T(8,128)S(1)} collective-permute-done((f32[64,128]{1,0:T(8,128)S(1)}, f32[64,128]{1,0:T(8,128)S(1)}, u32[]{:S(2)}, u32[]{:S(2)}) %collective-permute-start.4) | collective-permute-done | bytes 32800 | tf_op jit(solution)/shard_map/ppermute | solution.py:319
  37.5 2.8 %collective-permute-start.6 = (f32[64,128]{1,0:T(8,128)S(1)}, f32[64,128]{1,0:T(8,128)S(1)}, u32[]{:S(2)}, u32[]{:S(2)}) collective-permute-start(f32[64,128]{1,0:T(8,128)S(1)} %get-tuple-element.33.force), channel_id=1, source_target_pairs={{0,7},{1,0},{2,1},{3,2},{4,3},{5,4},{6,5},{7,6},{8,15},{9,8},{10,9... | collective-permute-start | bytes 98312 | tf_op jit(solution)/shard_map/ppermute | solution.py:270
  40.2 0.9 %collective-permute-start.5 = (f32[64,128]{1,0:T(8,128)S(1)}, f32[64,128]{1,0:T(8,128)S(1)}, u32[]{:S(2)}, u32[]{:S(2)}) collective-permute-start(f32[64,128]{1,0:T(8,128)S(1)} %get-tuple-element.33.force), channel_id=1, source_target_pairs={{0,1},{1,2},{2,3},{3,4},{4,5},{5,6},{6,7},{7,0},{8,9},{9,10},{10,1... | collective-permute-start | bytes 98312 | tf_op jit(solution)/shard_map/ppermute | solution.py:270
  41.1 1.2 %shard_map.109.values = f32[128,128]{1,0:T(8,128)} custom-call(f32[128,128]{1,0:T(8,128)S(1)} %bitcast.13, f32[64,128]{1,0:T(8,128)S(1)} %get-tuple-element.31.field), custom_call_target="tpu_custom_call" | custom-call | flops 600000000 | bytes 1800000000 | tf_op jit(solution)/shard_map/pallas_call | solution.py:22
  42.2 10.9 %all-to-all-start.1 = ((f32[128,1,128]{2,1,0:T(1,128)}), f32[128,1,128]{2,1,0:T(1,128)S(1)}, u32[]{:S(2)}, u32[]{:S(2)}) async-start(f32[128,1,128]{2,1,0:T(1,128)} %bitcast.7), calls=%async_computation.1 | async-start | bytes 131072 | tf_op jit(solution)/shard_map/all_to_all | solution.py:279
  53.2 0.9 %shard_map.111 = (f32[3,8,128]{2,1,0:T(8,128)S(1)}, f32[3,8,128]{2,1,0:T(8,128)S(1)}) custom-call(f32[64,128]{1,0:T(8,128)S(1)} %get-tuple-element.33.force, f32[64,128]{1,0:T(8,128)S(1)} %collective-permute-done.5.left, f32[64,128]{1,0:T(8,128)S(1)} %collective-permute-done.6.right, f32[128,128]{1,0:T(8,128)} %shard_map.109.values), custom_call_target="tpu_custom_call" | custom-call | flops 600000000 | bytes 1800000000 | tf_op jit(solution)/shard_map/pallas_call | solution.py:22
  54.0 1.4 %collective-permute-start.7 = (f32[3,8,128]{2,1,0:T(8,128)S(1)}, f32[3,8,128]{2,1,0:T(8,128)S(1)}, u32[]{:S(2)}, u32[]{:S(2)}) collective-permute-start(f32[3,8,128]{2,1,0:T(8,128)S(1)} %get-tuple-element.34), channel_id=1, source_target_pairs={{0,8},{8,16},{16,24},{24,32},{32,40},{40,48},{48,56},{56,64},{64,7... | collective-permute-start | bytes 36872 | tf_op jit(solution)/shard_map/ppermute | solution.py:270
  55.4 3.7 %collective-permute-start.8 = (f32[3,8,128]{2,1,0:T(8,128)S(1)}, f32[3,8,128]{2,1,0:T(8,128)S(1)}, u32[]{:S(2)}, u32[]{:S(2)}) collective-permute-start(f32[3,8,128]{2,1,0:T(8,128)S(1)} %get-tuple-element.35), channel_id=1, source_target_pairs={{0,120},{8,0},{16,8},{24,16},{32,24},{40,32},{48,40},{56,48},{64,5... | collective-permute-start | bytes 36872 | tf_op jit(solution)/shard_map/ppermute | solution.py:270
  59.1 1.4 %collective-permute-done.7.below = f32[3,8,128]{2,1,0:T(8,128)S(1)} collective-permute-done((f32[3,8,128]{2,1,0:T(8,128)S(1)}, f32[3,8,128]{2,1,0:T(8,128)S(1)}, u32[]{:S(2)}, u32[]{:S(2)}) %collective-permute-start.7) | collective-permute-done | bytes 12320 | tf_op jit(solution)/shard_map/ppermute | solution.py:270
  60.6 1.9 %shard_map.112 = f32[4,2,64,128]{3,2,1,0:T(8,128)} custom-call(f32[64,128]{1,0:T(8,128)S(1)} %get-tuple-element.33.force, f32[64,128]{1,0:T(8,128)S(1)} %collective-permute-done.5.left, f32[64,128]{1,0:T(8,128)S(1)} %collective-permute-done.6.right, f32[3,8,128]{2,1,0:T(8,128)S(1)} %collective-permute-done.7.below, ...), custom_call_target="tpu_custom_call" | custom-call | flops 600000000 | bytes 1800000000 | tf_op jit(solution)/shard_map/pallas_call | solution.py:22
  62.5 2.7 %all-to-all-done.1 = f32[128,1,128]{2,1,0:T(1,128)S(1)} async-done(((f32[128,1,128]{2,1,0:T(1,128)}), f32[128,1,128]{2,1,0:T(1,128)S(1)}, u32[]{:S(2)}, u32[]{:S(2)}) %all-to-all-start.1) | async-done | bytes 65568 | tf_op jit(solution)/shard_map/all_to_all | solution.py:279
  65.2 0.8 %shard_map.110 = f32[4,128]{1,0:T(4,128)} custom-call(f32[128,128]{1,0:T(8,128)S(1)} %bitcast.14, s32[4,128]{1,0:T(4,128)S(1)} %bitcast.16, s32[4,128]{1,0:T(4,128)S(1)} %get-tuple-element.32.rank), custom_call_target="tpu_custom_call" | custom-call | flops 1000000 | bytes 3000000 | tf_op jit(solution)/shard_map/pallas_call | solution.py:22
  (25 shorter events, 0.7 us)
Async XLA Ops:
  2.0 3.3 %copy-start.5 = (s32[512]{0:T(512)S(1)}, s32[512]{0:T(512)}, u32[]{:S(2)}) copy-start(s32[512]{0:T(512)} %param.14) | copy-start | bytes 6148
  2.0 3.3 %copy-start.6 = (f32[512]{0:T(512)S(1)}, f32[512]{0:T(512)}, u32[]{:S(2)}) copy-start(f32[512]{0:T(512)} %param.15) | copy-start | bytes 6148
  2.0 19.8 %collective-permute-start = (f32[64,128]{1,0:T(8,128)S(1)}, f32[64,128]{1,0:T(8,128)S(1)}, u32[]{:S(2)}, u32[]{:S(2)}) collective-permute-start(f32[64,128]{1,0:T(8,128)S(1)} %get-tuple-element.22), channel_id=1, source_target_pairs={{0,1},{1,2},{2,3},{3,4},{4,5},{5,6},{6,7},{7,0},{8,9},{9,10},{10,1... | collective-permute-start | bytes 98312 | tf_op jit(solution)/shard_map/ppermute | solution.py:270
  4.7 17.2 %collective-permute-start.1 = (f32[64,128]{1,0:T(8,128)S(1)}, f32[64,128]{1,0:T(8,128)S(1)}, u32[]{:S(2)}, u32[]{:S(2)}) collective-permute-start(f32[64,128]{1,0:T(8,128)S(1)} %get-tuple-element.23), channel_id=1, source_target_pairs={{0,7},{1,0},{2,1},{3,2},{4,3},{5,4},{6,5},{7,6},{8,15},{9,8},{10,9... | collective-permute-start | bytes 98312 | tf_op jit(solution)/shard_map/ppermute | solution.py:270
  5.3 0.7 %copy-start.4 = (s32[512,1]{0,1:T(1,128)S(1)}, s32[512,1]{0,1:T(1,128)}, u32[]{:S(2)}) copy-start(s32[512,1]{0,1:T(1,128)} %param.13) | copy-start | bytes 6148
  7.2 28.9 %all-to-all-start = ((f32[128,1,128]{2,1,0:T(1,128)}), f32[128,1,128]{2,1,0:T(1,128)S(1)}, u32[]{:S(2)}, u32[]{:S(2)}) async-start(f32[128,1,128]{2,1,0:T(1,128)} %bitcast.4), calls=%async_computation | async-start | bytes 131072 | tf_op jit(solution)/shard_map/all_to_all | solution.py:279
  21.8 8.2 %copy-start = (f32[4,2,64,128]{3,2,1,0:T(8,128)S(1)}, f32[4,2,64,128]{3,2,1,0:T(8,128)}, u32[]{:S(2)}) copy-start(f32[4,2,64,128]{3,2,1,0:T(8,128)} %conc.3) | copy-start | bytes 786436
  21.9 8.2 %copy-start.1 = (f32[2,64,128]{2,1,0:T(8,128)S(1)}, f32[2,64,128]{2,1,0:T(8,128)}, u32[]{:S(2)}) copy-start(f32[2,64,128]{2,1,0:T(8,128)} %kk.3) | copy-start | bytes 196612
  21.9 8.2 %copy-start.2 = (f32[2,64,128]{2,1,0:T(8,128)S(1)}, f32[2,64,128]{2,1,0:T(8,128)}, u32[]{:S(2)}) copy-start(f32[2,64,128]{2,1,0:T(8,128)} %uu.3) | copy-start | bytes 196612
  21.9 8.2 %copy-start.3 = (f32[2,64,128]{2,1,0:T(8,128)S(1)}, f32[2,64,128]{2,1,0:T(8,128)}, u32[]{:S(2)}) copy-start(f32[2,64,128]{2,1,0:T(8,128)} %vv.3) | copy-start | bytes 196612
  22.8 5.2 %copy-start.7 = (f32[4,2]{0,1:T(2,128)S(1)}, f32[4,2]{0,1:T(2,128)}, u32[]{:S(2)}) copy-start(f32[4,2]{0,1:T(2,128)} %param.12) | copy-start | bytes 100
  22.8 7.3 %collective-permute-start.2 = (f32[16,8,128]{2,1,0:T(8,128)S(1)}, f32[16,8,128]{2,1,0:T(8,128)S(1)}, u32[]{:S(2)}, u32[]{:S(2)}) collective-permute-start(f32[16,8,128]{2,1,0:T(8,128)S(1)} %get-tuple-element.25), channel_id=1, source_target_pairs={{0,8},{8,16},{16,24},{24,32},{32,40},{40,48},{48,56},{56,64},{64,7... | collective-permute-start | bytes 196616 | tf_op jit(solution)/shard_map/ppermute | solution.py:270
  24.3 5.8 %collective-permute-start.3 = (f32[16,8,128]{2,1,0:T(8,128)S(1)}, f32[16,8,128]{2,1,0:T(8,128)S(1)}, u32[]{:S(2)}, u32[]{:S(2)}) collective-permute-start(f32[16,8,128]{2,1,0:T(8,128)S(1)} %get-tuple-element.26), channel_id=1, source_target_pairs={{0,120},{8,0},{16,8},{24,16},{32,24},{40,32},{48,40},{56,48},{64,5... | collective-permute-start | bytes 196616 | tf_op jit(solution)/shard_map/ppermute | solution.py:270
  34.6 2.8 %collective-permute-start.4 = (f32[64,128]{1,0:T(8,128)S(1)}, f32[64,128]{1,0:T(8,128)S(1)}, u32[]{:S(2)}, u32[]{:S(2)}) collective-permute-start(f32[64,128]{1,0:T(8,128)S(1)} %get-tuple-element.30.mine), channel_id=1, source_target_pairs={{0,128},{128,0},{1,129},{129,1},{2,130},{130,2},{3,131},{131,3},{4... | collective-permute-start | bytes 98312 | tf_op jit(solution)/shard_map/ppermute | solution.py:319
  37.5 15.7 %collective-permute-start.6 = (f32[64,128]{1,0:T(8,128)S(1)}, f32[64,128]{1,0:T(8,128)S(1)}, u32[]{:S(2)}, u32[]{:S(2)}) collective-permute-start(f32[64,128]{1,0:T(8,128)S(1)} %get-tuple-element.33.force), channel_id=1, source_target_pairs={{0,7},{1,0},{2,1},{3,2},{4,3},{5,4},{6,5},{7,6},{8,15},{9,8},{10,9... | collective-permute-start | bytes 98312 | tf_op jit(solution)/shard_map/ppermute | solution.py:270
  40.2 12.9 %collective-permute-start.5 = (f32[64,128]{1,0:T(8,128)S(1)}, f32[64,128]{1,0:T(8,128)S(1)}, u32[]{:S(2)}, u32[]{:S(2)}) collective-permute-start(f32[64,128]{1,0:T(8,128)S(1)} %get-tuple-element.33.force), channel_id=1, source_target_pairs={{0,1},{1,2},{2,3},{3,4},{4,5},{5,6},{6,7},{7,0},{8,9},{9,10},{10,1... | collective-permute-start | bytes 98312 | tf_op jit(solution)/shard_map/ppermute | solution.py:270
  42.2 22.9 %all-to-all-start.1 = ((f32[128,1,128]{2,1,0:T(1,128)}), f32[128,1,128]{2,1,0:T(1,128)S(1)}, u32[]{:S(2)}, u32[]{:S(2)}) async-start(f32[128,1,128]{2,1,0:T(1,128)} %bitcast.7), calls=%async_computation.1 | async-start | bytes 131072 | tf_op jit(solution)/shard_map/all_to_all | solution.py:279
  54.0 6.5 %collective-permute-start.7 = (f32[3,8,128]{2,1,0:T(8,128)S(1)}, f32[3,8,128]{2,1,0:T(8,128)S(1)}, u32[]{:S(2)}, u32[]{:S(2)}) collective-permute-start(f32[3,8,128]{2,1,0:T(8,128)S(1)} %get-tuple-element.34), channel_id=1, source_target_pairs={{0,8},{8,16},{16,24},{24,32},{32,40},{40,48},{48,56},{56,64},{64,7... | collective-permute-start | bytes 36872 | tf_op jit(solution)/shard_map/ppermute | solution.py:270
  55.4 5.1 %collective-permute-start.8 = (f32[3,8,128]{2,1,0:T(8,128)S(1)}, f32[3,8,128]{2,1,0:T(8,128)S(1)}, u32[]{:S(2)}, u32[]{:S(2)}) collective-permute-start(f32[3,8,128]{2,1,0:T(8,128)S(1)} %get-tuple-element.35), channel_id=1, source_target_pairs={{0,120},{8,0},{16,8},{24,16},{32,24},{40,32},{48,40},{56,48},{64,5... | collective-permute-start | bytes 36872 | tf_op jit(solution)/shard_map/ppermute | solution.py:270

commit v3 on v2

--- a/solution.py
+++ b/solution.py
@@ -15,15 +15,17 @@
 BF16 = jnp.bfloat16
 VMEM = pl.BlockSpec(memory_space=pltpu.VMEM)
 HBM = pl.BlockSpec(memory_space=pltpu.HBM)
+ANY = pl.BlockSpec(memory_space=pl.ANY)
 SMEM = pl.BlockSpec(memory_space=pltpu.SMEM)
 
 
-def call(body, outs, inputs, specs=None, us=1.0, scratch=()):
+def call(body, outs, inputs, specs=None, us=1.0, scratch=(), outspec=None, alias=None):
     return pl.pallas_call(
         body,
         out_shape=outs,
         in_specs=specs or [VMEM] * len(inputs),
-        out_specs=jax.tree.map(lambda _: VMEM, outs),
+        out_specs=outspec or jax.tree.map(lambda _: VMEM, outs),
+        input_output_aliases=alias or {},
         scratch_shapes=list(scratch),
         compiler_params=pltpu.CompilerParams(vmem_limit_bytes=16 << 20),
         cost_estimate=pl.CostEstimate(
@@ -50,6 +52,13 @@
 
 def iota(shape, dim):
     return lax.broadcasted_iota(jnp.int32, shape, dim)
+
+
+def tile_at(t, groups):
+    for shift in (3, 4, 3):
+        t = (t * 109 + 55) & (groups - 1)
+        t = t ^ (t >> shift)
+    return t
 
 
 def request_body(groups, owner, column, observed, req, rank):
@@ -59,8 +68,9 @@
     carry = jnp.zeros((groups, lanes), F32)
     total = jnp.zeros((groups, lanes), F32)
     blank = jnp.zeros((lanes - 2 * CAP, lanes), F32)
+    who = tile_at(iota((groups, lanes), 0), groups)
     for j in range(rows):
-        onehot = (iota((groups, lanes), 0) == owner[j : j + 1, :]).astype(F32)
+        onehot = (who == owner[j : j + 1, :]).astype(F32)
         hot = onehot.astype(BF16)
         prior = nn(hot, before) + carry
         place = jnp.sum(onehot * prior, axis=0, keepdims=True)
@@ -112,7 +122,7 @@
     left[...] = down
 
 
-def corners_body(high, low, left, right, request, out_high, out_low):
+def corners_body(high, low, left, right, out_high, out_low):
     f, n = high.shape[0], left.shape[0]
     out_high[0:f] = high[...]
     out_low[0:f] = low[...]
@@ -121,57 +131,95 @@
         out_low[f + i] = side[0:EDGE, :]
 
 
-def tall(tile, after, before):
-    first = iota(after.shape, 0) < HALO
-    return jnp.concatenate([tile, jnp.where(first, after, before)], axis=0)
-
-
-def forward_body(conc, kk, uu, vv, below, above, left, right, weight, out, column, coef):
+def spread(nat, tile, after, before):
+    n = tile.shape[0]
+    nat[0:n] = tile
+    nat[n : n + EDGE] = jnp.where(iota(after.shape, 0) < HALO, after, before)
+    step = (n + EDGE) // EDGE
+    return [nat[pl.ds(g, EDGE, stride=step), :] for g in range(step)]
+
+
+def gather(nat, parts, n):
+    for g, part in enumerate(parts):
+        nat[pl.ds(g, EDGE, stride=len(parts)), :] = part
+    return nat[0:n]
+
+
+def rows_next(x):
+    return x[1:] + [pltpu.roll(x[0], EDGE - 1, 0)]
+
+
+def rows_prev(x):
+    return [pltpu.roll(x[-1], 1, 0)] + x[:-1]
+
+
+def lanes_moved(x, side, shift, edge):
+    a = [pltpu.roll(p, shift, 1) for p in x]
+    b = [pltpu.roll(p, shift, 1) for p in side]
+    mid = [jnp.where(edge, q, p) for p, q in zip(a, b)]
+    return mid, [jnp.where(edge, p, q) for p, q in zip(a, b)]
+
+
+def halves(fn, *xs):
+    return tuple([fn(h, g, *(x[h][g] for x in xs)) for g in range(len(xs[0][0]))] for h in range(2))
+
+
+def forward_body(conc, kk, uu, vv, below, above, left, right, weight, out, column, coef, nat):
     keep_b, keep_a = inside("gx")
     keep_l, keep_r = inside("gy")
     n, m = conc.shape[2], conc.shape[3]
     tracers, levels = conc.shape[0], conc.shape[1]
     fields = (tracers + 3) * levels
+    at = iota((EDGE, m), 1)
+    last, first = at == m - 1, at == 0
 
     def rows(tile, f):
-        return tall(tile, above[f] * keep_a, below[f] * keep_b)
-
-    from_left = rows(left[...], fields) * keep_l
-    from_right = rows(right[...], fields + 1) * keep_r
-    at = iota(from_left.shape, 1)
+        return spread(nat, tile, above[f] * keep_a, below[f] * keep_b)
+
+    from_left = [p * keep_l for p in rows(left[...], fields)]
+    from_right = [p * keep_r for p in rows(right[...], fields + 1)]
 
     def wide(tile, f):
-        a = pltpu.roll(from_right, (m - HALO * f) % m, 1) if f else from_right
-        b = pltpu.roll(from_left, (m - HALO - HALO * f) % m, 1)
-        side = jnp.where(at < HALO, a, jnp.where(at >= m - HALO, b, 0.0))
-        return jnp.concatenate([rows(tile, f), side], axis=1)
-
-    total = jnp.zeros((n, m), F32)
+        side = []
+        for p, q in zip(from_left, from_right):
+            a = pltpu.roll(q, lax.rem(m - HALO * f, m), 1)
+            b = pltpu.roll(p, lax.rem(2 * m - HALO - HALO * f, m), 1)
+            side.append(jnp.where(at < HALO, a, jnp.where(at >= m - HALO, b, 0.0)))
+        return rows(tile, f), side
+
     base = tracers * levels
+    zero = tuple(jnp.zeros((EDGE, m), F32) for _ in from_left)
+    total = zero
     for l in range(levels):
-        k = wide(kk[l], base + l)
-        u = 0.5 * wide(uu[l], base + levels + l)
-        v = 0.5 * wide(vv[l], base + 2 * levels + l)
-        coef[l, 0] = 1.0 - 4.0 * k
-        coef[l, 1] = k - u
-        coef[l, 2] = k + u
-        coef[l, 3] = k - v
-        coef[l, 4] = k + v
-        for t in range(tracers):
+        k = wide(kk[l], jnp.int32(base + l))
+        u = wide(uu[l], jnp.int32(base + levels + l))
+        v = wide(vv[l], jnp.int32(base + 2 * levels + l))
+        for h in range(2):
+            for g in range(len(zero)):
+                a, b, c = k[h][g], 0.5 * u[h][g], 0.5 * v[h][g]
+                for i, value in enumerate((1.0 - 4.0 * a, a - b, a + b, a - c, a + c)):
+                    coef[l, i, h, g] = value
+
+        def one(t, total, l=l):
             c = wide(conc[t, l], t * levels + l)
-            high, cols = c.shape
             for _ in range(STEPS):
-                c = (
-                    coef[l, 0] * c
-                    + coef[l, 1] * pltpu.roll(c, high - 1, 0)
-                    + coef[l, 2] * pltpu.roll(c, 1, 0)
-                    + coef[l, 3] * pltpu.roll(c, cols - 1, 1)
-                    + coef[l, 4] * pltpu.roll(c, 1, 1)
+                e = tuple(rows_next(x) for x in c)
+                w = tuple(rows_prev(x) for x in c)
+                no = lanes_moved(*c, m - 1, last)
+                so = lanes_moved(*c, 1, first)
+                c = halves(
+                    lambda h, g, c, e, w, no, so: (
+                        coef[l, 0, h, g] * c
+                        + (coef[l, 1, h, g] * e + coef[l, 2, h, g] * w)
+                        + (coef[l, 3, h, g] * no + coef[l, 4, h, g] * so)
+                    ),
+                    c, e, w, no, so,
                 )
-            c = c[:n, :m]
-            out[t, l] = c
-            total = total + weight[t, l] * c
-    column[...] = total
+            out[t, l] = gather(nat, c[0], n)
+            return tuple(a + weight[t, l] * b for a, b in zip(total, c[0]))
+
+        total = lax.fori_loop(0, tracers, one, total)
+    column[...] = gather(nat, total, n)
 
 
 def slots(code, n, m):
@@ -222,8 +270,9 @@
     rows, lanes = owner.shape
     t = got[...].T[:CAP]
     parts = jnp.concatenate(split3(t), axis=0)
+    who = tile_at(iota((groups, lanes), 0), groups)
     for j in range(rows):
-        onehot = (iota((groups, lanes), 0) == owner[j : j + 1, :]).astype(F32)
+        onehot = (who == owner[j : j + 1, :]).astype(F32)
         z = nn(parts, onehot.astype(BF16))
         z = z[:CAP] + z[CAP : 2 * CAP] + z[2 * CAP :]
         slot = iota((CAP, lanes), 0) == rank[j : j + 1, :]
@@ -237,32 +286,40 @@
         low[i] = part[0:EDGE, :]
 
 
-def adjoint_body(force, left, right, below, above, coef, weight, out):
+def adjoint_body(force, left, right, below, above, coef, weight, out, nat):
     keep_b, keep_a = inside("gx")
     keep_l, keep_r = inside("gy")
     n, m = out.shape[2], out.shape[3]
+    at = iota((EDGE, m), 1)
+    last, first = at == m - 1, at == 0
 
     def rows(part, i):
-        return tall(part[...], above[i] * keep_a, below[i] * keep_b)
-
-    mid, a, b = rows(force, 0), rows(right, 2) * keep_r, rows(left, 1) * keep_l
-    at = iota(mid.shape, 1)
-    side = jnp.where(at < HALO, a, jnp.where(at >= m - HALO, b, 0.0))
-    start = jnp.concatenate([mid, side], axis=1)
-    high, cols = start.shape
+        return spread(nat, part[...], above[i] * keep_a, below[i] * keep_b)
+
+    mid, a, b = rows(force, 0), rows(right, 2), rows(left, 1)
+    side = [
+        jnp.where(at < HALO, p * keep_r, jnp.where(at >= m - HALO, q * keep_l, 0.0))
+        for p, q in zip(a, b)
+    ]
     for l in range(out.shape[1]):
-        a = start
+        a = (mid, side)
         for _ in range(STEPS):
-            a = (
-                coef[l, 0] * a
-                + pltpu.roll(coef[l, 2] * a, high - 1, 0)
-                + pltpu.roll(coef[l, 1] * a, 1, 0)
-                + pltpu.roll(coef[l, 4] * a, cols - 1, 1)
-                + pltpu.roll(coef[l, 3] * a, 1, 1)
+            c, w, e, s, no = (
+                halves(lambda h, g, x, i=i: coef[l, i, h, g] * x, a) for i in range(5)
             )
-        a = a[:n, :m]
+            e = tuple(rows_next(x) for x in e)
+            w = tuple(rows_prev(x) for x in w)
+            no = lanes_moved(*no, m - 1, last)
+            s = lanes_moved(*s, 1, first)
+            a = halves(lambda h, g, c, e, w, no, s: c + (e + w) + (no + s), c, e, w, no, s)
+        value = gather(nat, a[0], n)
         for t in range(out.shape[0]):
-            out[t, l] = weight[t, l] * a
+            out[t, l] = weight[t, l] * value
+
+
+def after(x, other):
+    shape = jax.ShapeDtypeStruct(x.shape, x.dtype)
+    return call(lambda *_: None, shape, (x, other), [ANY] * 2, us=600.0, outspec=ANY, alias={0: 0})
 
 
 def ring(value, axis, step):
@@ -272,10 +329,8 @@
 
 def exchange(value):
     nx, ny = lax.axis_size("gx"), lax.axis_size("gy")
-    groups = [
-        [(g ^ (2 * i // nx)) * nx * ny + i * ny + j for i in range(nx) for j in range(ny)]
-        for g in range(2)
-    ]
+    order = [tile_at(t, nx * ny) for t in range(nx * ny)]
+    groups = [[(g ^ (2 * t // (nx * ny))) * nx * ny + t for t in order] for g in range(2)]
     return lax.all_to_all(
         value, ("lev", "gx", "gy"), 0, 0, axis_index_groups=groups, tiled=True
     )
@@ -305,16 +360,17 @@
         (owner, column, obs),
         us=600.0,
     )
-    asked = exchange(req)
     edge = S((fields + 2, EDGE, m), F32)
-    high, low = call(corners_body, (edge, edge), (high, low, left, right, req), us=600.0)
+    high, low = call(corners_body, (edge, edge), (high, low, left, right))
     below, above = ring(high, "gx", 1), ring(low, "gx", -1)
+    asked = exchange(after(req, high))
     forecast, mine, coef = call(
         forward_body,
-        (S(conc.shape, F32), tile, S((levels, 5, n + EDGE, 2 * m), F32)),
+        (S(conc.shape, F32), tile, S((levels, 5, 2, (n + EDGE) // EDGE, EDGE, m), F32)),
         (conc, kk, uu, vv, below, above, left, right, weight),
         [VMEM] * 8 + [SMEM],
-        us=300.0,
+        us=600.0,
+        scratch=[pltpu.VMEM((n + EDGE, m), F32)],
     )
     other = lax.ppermute(mine, "lev", [(0, 1), (1, 0)])
     count, seen = call(count_body, (tile, tile), (asked,))
@@ -323,7 +379,7 @@
     values = call(values_body, S((groups, 128), F32), (asked, field), us=600.0)
     got = exchange(values)
     edge = S((3, EDGE, m), F32)
-    high, low = call(rows_body, (edge, edge), (force, left, right, values), us=600.0)
+    high, low = call(rows_body, (edge, edge), (force, left, right, values), [VMEM] * 3 + [ANY], us=600.0)
     below, above = ring(high, "gx", 1), ring(low, "gx", -1)
     gradient = call(
         adjoint_body,
@@ -331,6 +387,7 @@
         (force, left, right, below, above, coef, weight),
         [VMEM] * 6 + [SMEM],
         us=600.0,
+        scratch=[pltpu.VMEM((n + EDGE, m), F32)],
     )
     model = call(
         functools.partial(answer_body, groups), S(owner.shape, F32), (got, owner, rank)

time: 66.3 us -> 63.8 us (0.962)
  waiting for transfers between devices: 6.96 us -> 4.15 us
  starting transfers between devices: 44.1 us -> 45.4 us
  Pallas kernels: 13.3 us -> 12.4 us
    all_to_all x2, waiting for transfers between devices: 2.71 us -> 0.01 us  [exchange(): lax.all_to_all(value, ('lev', 'gx', 'gy'), 0, 0, axis_index_groups=groups...]
    ppermute x8, waiting for transfers between devices: 3.47 us -> 1.9 us  [ring(): return lax.ppermute(value, axis, [(i, (i + step) % n) for i in range(n)])]
    all_to_all x2, starting transfers between devices: 25.5 us -> 27.1 us  [exchange(): lax.all_to_all(value, ('lev', 'gx', 'gy'), 0, 0, axis_index_groups=groups...]
    ppermute x1, starting transfers between devices: 1.51 us -> 0.01 us  [shards(): other = lax.ppermute(mine, 'lev', [(0, 1), (1, 0)])]
    ppermute x1, waiting for transfers between devices: 0.78 us -> 2.24 us  [shards(): other = lax.ppermute(mine, 'lev', [(0, 1), (1, 0)])]
    ppermute x8, starting transfers between devices: 17.1 us -> 18.3 us  [ring(): return lax.ppermute(value, axis, [(i, (i + step) % n) for i in range(n)])]
    pallas_call x10 -> x11, Pallas kernels: 13.3 us -> 12.4 us  [call(): pl.pallas_call(body, out_shape=outs, in_specs=specs or [VMEM] * len(input...]
  transfers between devices with their start and end apart: 11 -> 11, of which waited for: 4 -> 3; matrix products, arithmetic and copies ran while one was open for 0% -> 0% of each run, Pallas kernels for 17% -> 16%
where the time goes in v3:
time: 63.8 us; the launch traced here: 63.5 us
  starting transfers between devices  45.4 us (71%)
  Pallas kernels  12.4 us (19%)
  waiting for transfers between devices  4.15 us (7%)
  local copies, waits for them, and re-layouts  0.81 us (1%)
  between operations  0.79 us (1%)
    all_to_all x2, starting transfers between devices, exchange(): lax.all_to_all(value, ('lev', 'gx', 'gy'), 0, 0, axis_index_groups=groups...  27.1 us
    ppermute x8, starting transfers between devices, ring(): return lax.ppermute(value, axis, [(i, (i + step) % n) for i in range(n)])  18.3 us
    pallas_call x11, Pallas kernels, call(): pl.pallas_call(body, out_shape=outs, in_specs=specs or [VMEM] * len(input...  12.4 us
    ppermute x1, waiting for transfers between devices, shards(): other = lax.ppermute(mine, 'lev', [(0, 1), (1, 0)])  2.24 us
    ppermute x8, waiting for transfers between devices, ring(): return lax.ppermute(value, axis, [(i, (i + step) % n) for i in range(n)])  1.9 us
  transfers between devices with their start and end apart: 11, of which 3 were waited for; matrix products, arithmetic and copies ran while one was open for 0% of the time, Pallas kernels for 16%

profile of v3, /device:TPU:1, one launch (start us, length us, event | category | flops | bytes accessed | tf_op | source)
XLA Modules:
  0.0 63.5 jit_solution(2260125309587814661)
XLA Ops:
  0.6 1.3 %shard_map.103 = (f32[64,128]{1,0:T(8,128)S(1)}, f32[64,128]{1,0:T(8,128)S(1)}, f32[14,8,128]{2,1,0:T(8,128)S(1)}, f32[14,8,128]{2,1,0:T(8,128)S(1)}) custom-call(f32[4,2,64,128]{3,2,1,0:T(8,128)} %conc.3, f32[2,64,128]{2,1,0:T(8,128)} %kk.3, f32[2,64,128]{2,1,0:T(8,128)} %uu.3, f32[2,64,128]{2,1,0:T(8,128)} %vv.3), custom_call_target="tpu_custom_call" | custom-call | flops 1000000 | bytes 3000000 | tf_op jit(solution)/shard_map/pallas_call | solution.py:23
  2.0 0.0 copy-start.5
  2.0 0.0 copy-start.6
  2.0 2.7 %collective-permute-start = (f32[64,128]{1,0:T(8,128)S(1)}, f32[64,128]{1,0:T(8,128)S(1)}, u32[]{:S(2)}, u32[]{:S(2)}) collective-permute-start(f32[64,128]{1,0:T(8,128)S(1)} %get-tuple-element.22), channel_id=1, source_target_pairs={{0,1},{1,2},{2,3},{3,4},{4,5},{5,6},{6,7},{7,0},{8,9},{9,10},{10,1... | collective-permute-start | bytes 98312 | tf_op jit(solution)/shard_map/ppermute | solution.py:327
  4.7 0.6 collective-permute-start.1
  5.3 0.7 %copy-done.4 = s32[512,1]{0,1:T(1,128)S(1)} copy-done((s32[512,1]{0,1:T(1,128)S(1)}, s32[512,1]{0,1:T(1,128)}, u32[]{:S(2)}) %copy-start.4) | copy-done | bytes 2072
  5.9 1.3 %shard_map.106 = (f32[128,128]{1,0:T(8,128)}, s32[4,128]{1,0:T(4,128)S(1)}) custom-call(s32[4,128]{1,0:T(4,128)S(1)} %bitcast.15, s32[4,128]{1,0:T(4,128)S(1)} %bitcast.17, f32[4,128]{1,0:T(4,128)S(1)} %bitcast.18), custom_call_target="tpu_custom_call" | custom-call | flops 600000000 | bytes 1800000000 | tf_op jit(solution)/shard_map/pallas_call | solution.py:23
  7.2 0.8 %collective-permute-done.1.right = f32[64,128]{1,0:T(8,128)S(1)} collective-permute-done((f32[64,128]{1,0:T(8,128)S(1)}, f32[64,128]{1,0:T(8,128)S(1)}, u32[]{:S(2)}, u32[]{:S(2)}) %collective-permute-start.1) | collective-permute-done | bytes 32800 | tf_op jit(solution)/shard_map/ppermute | solution.py:327
  8.0 8.1 %collective-permute-start.3 = (f32[16,8,128]{2,1,0:T(8,128)S(1)}, f32[16,8,128]{2,1,0:T(8,128)S(1)}, u32[]{:S(2)}, u32[]{:S(2)}) collective-permute-start(f32[16,8,128]{2,1,0:T(8,128)S(1)} %get-tuple-element.25), channel_id=1, source_target_pairs={{0,120},{8,0},{16,8},{24,16},{32,24},{40,32},{48,40},{56,48},{64,5... | collective-permute-start | bytes 196616 | tf_op jit(solution)/shard_map/ppermute | solution.py:327
  16.2 0.0 copy-start.2
  16.2 13.3 %all-to-all-start = ((f32[128,1,128]{2,1,0:T(1,128)}), f32[128,1,128]{2,1,0:T(1,128)S(1)}, u32[]{:S(2)}, u32[]{:S(2)}) async-start(f32[128,1,128]{2,1,0:T(1,128)} %bitcast.4), calls=%async_computation | async-start | bytes 131072 | tf_op jit(solution)/shard_map/all_to_all | solution.py:334
  29.5 0.1 copy.14.weight
  29.6 5.4 %shard_map.105 = (f32[4,2,64,128]{3,2,1,0:T(8,128)}, f32[64,128]{1,0:T(8,128)S(1)}, f32[2,5,2,9,8,128]{5,4,3,2,1,0:T(8,128)S(1)}) custom-call(f32[4,2,64,128]{3,2,1,0:T(8,128)S(1)} %copy-done, f32[2,64,128]{2,1,0:T(8,128)S(1)} %copy-done.1, f32[2,64,128]{2,1,0:T(8,128)S(1)} %copy-done.2, f32[2,64,128]{2,1,0:T(8,128)S(1)} %copy-done.3, ...), custom_call_target="tpu_custom_call" | custom-call | flops 600000000 | bytes 1800000000 | tf_op jit(solution)/shard_map/pallas_call | solution.py:23
  35.0 0.5 shard_map.108
  35.5 2.2 %collective-permute-done.4.other = f32[64,128]{1,0:T(8,128)S(1)} collective-permute-done((f32[64,128]{1,0:T(8,128)S(1)}, f32[64,128]{1,0:T(8,128)S(1)}, u32[]{:S(2)}, u32[]{:S(2)}) %collective-permute-start.4) | collective-permute-done | bytes 32800 | tf_op jit(solution)/shard_map/ppermute | solution.py:375
  37.8 1.3 %collective-permute-start.6 = (f32[64,128]{1,0:T(8,128)S(1)}, f32[64,128]{1,0:T(8,128)S(1)}, u32[]{:S(2)}, u32[]{:S(2)}) collective-permute-start(f32[64,128]{1,0:T(8,128)S(1)} %get-tuple-element.33.force), channel_id=1, source_target_pairs={{0,7},{1,0},{2,1},{3,2},{4,3},{5,4},{6,5},{7,6},{8,15},{9,8},{10,9... | collective-permute-start | bytes 98312 | tf_op jit(solution)/shard_map/ppermute | solution.py:327
  39.1 0.4 collective-permute-start.5
  39.6 1.2 %shard_map.110.values = f32[128,128]{1,0:T(8,128)} custom-call(f32[128,128]{1,0:T(8,128)S(1)} %bitcast.13, f32[64,128]{1,0:T(8,128)S(1)} %get-tuple-element.31.field), custom_call_target="tpu_custom_call" | custom-call | flops 600000000 | bytes 1800000000 | tf_op jit(solution)/shard_map/pallas_call | solution.py:23
  40.7 13.8 %all-to-all-start.1 = ((f32[128,1,128]{2,1,0:T(1,128)}), f32[128,1,128]{2,1,0:T(1,128)S(1)}, u32[]{:S(2)}, u32[]{:S(2)}) async-start(f32[128,1,128]{2,1,0:T(1,128)} %bitcast.7), calls=%async_computation.1 | async-start | bytes 131072 | tf_op jit(solution)/shard_map/all_to_all | solution.py:334
  54.6 0.9 %collective-permute-start.7 = (f32[3,8,128]{2,1,0:T(8,128)S(1)}, f32[3,8,128]{2,1,0:T(8,128)S(1)}, u32[]{:S(2)}, u32[]{:S(2)}) collective-permute-start(f32[3,8,128]{2,1,0:T(8,128)S(1)} %get-tuple-element.34), channel_id=1, source_target_pairs={{0,8},{8,16},{16,24},{24,32},{32,40},{40,48},{48,56},{56,64},{64,7... | collective-permute-start | bytes 36872 | tf_op jit(solution)/shard_map/ppermute | solution.py:327
  55.5 4.3 %collective-permute-start.8 = (f32[3,8,128]{2,1,0:T(8,128)S(1)}, f32[3,8,128]{2,1,0:T(8,128)S(1)}, u32[]{:S(2)}, u32[]{:S(2)}) collective-permute-start(f32[3,8,128]{2,1,0:T(8,128)S(1)} %get-tuple-element.35), channel_id=1, source_target_pairs={{0,120},{8,0},{16,8},{24,16},{32,24},{40,32},{48,40},{56,48},{64,5... | collective-permute-start | bytes 36872 | tf_op jit(solution)/shard_map/ppermute | solution.py:327
  59.7 1.1 %collective-permute-done.7.below = f32[3,8,128]{2,1,0:T(8,128)S(1)} collective-permute-done((f32[3,8,128]{2,1,0:T(8,128)S(1)}, f32[3,8,128]{2,1,0:T(8,128)S(1)}, u32[]{:S(2)}, u32[]{:S(2)}) %collective-permute-start.7) | collective-permute-done | bytes 12320 | tf_op jit(solution)/shard_map/ppermute | solution.py:327
  60.8 1.9 %shard_map.113 = f32[4,2,64,128]{3,2,1,0:T(8,128)} custom-call(f32[64,128]{1,0:T(8,128)S(1)} %get-tuple-element.33.force, f32[64,128]{1,0:T(8,128)S(1)} %collective-permute-done.5.left, f32[64,128]{1,0:T(8,128)S(1)} %collective-permute-done.6.right, f32[3,8,128]{2,1,0:T(8,128)S(1)} %collective-permute-done.7.below, ...), custom_call_target="tpu_custom_call" | custom-call | flops 600000000 | bytes 1800000000 | tf_op jit(solution)/shard_map/pallas_call | solution.py:23
  62.7 0.8 %shard_map.111 = f32[4,128]{1,0:T(4,128)} custom-call(f32[128,128]{1,0:T(8,128)S(1)} %bitcast.14, s32[4,128]{1,0:T(4,128)S(1)} %bitcast.16, s32[4,128]{1,0:T(4,128)S(1)} %get-tuple-element.32.rank), custom_call_target="tpu_custom_call" | custom-call | flops 1000000 | bytes 3000000 | tf_op jit(solution)/shard_map/pallas_call | solution.py:23
  (26 shorter events, 0.1 us)
Async XLA Ops:
  2.0 3.3 %copy-start.5 = (s32[512]{0:T(512)S(1)}, s32[512]{0:T(512)}, u32[]{:S(2)}) copy-start(s32[512]{0:T(512)} %param.14) | copy-start | bytes 6148
  2.0 3.3 %copy-start.6 = (f32[512]{0:T(512)S(1)}, f32[512]{0:T(512)}, u32[]{:S(2)}) copy-start(f32[512]{0:T(512)} %param.15) | copy-start | bytes 6148
  2.0 5.2 %collective-permute-start = (f32[64,128]{1,0:T(8,128)S(1)}, f32[64,128]{1,0:T(8,128)S(1)}, u32[]{:S(2)}, u32[]{:S(2)}) collective-permute-start(f32[64,128]{1,0:T(8,128)S(1)} %get-tuple-element.22), channel_id=1, source_target_pairs={{0,1},{1,2},{2,3},{3,4},{4,5},{5,6},{6,7},{7,0},{8,9},{9,10},{10,1... | collective-permute-start | bytes 98312 | tf_op jit(solution)/shard_map/ppermute | solution.py:327
  4.7 3.3 %collective-permute-start.1 = (f32[64,128]{1,0:T(8,128)S(1)}, f32[64,128]{1,0:T(8,128)S(1)}, u32[]{:S(2)}, u32[]{:S(2)}) collective-permute-start(f32[64,128]{1,0:T(8,128)S(1)} %get-tuple-element.23), channel_id=1, source_target_pairs={{0,7},{1,0},{2,1},{3,2},{4,3},{5,4},{6,5},{7,6},{8,15},{9,8},{10,9... | collective-permute-start | bytes 98312 | tf_op jit(solution)/shard_map/ppermute | solution.py:327
  5.3 0.7 %copy-start.4 = (s32[512,1]{0,1:T(1,128)S(1)}, s32[512,1]{0,1:T(1,128)}, u32[]{:S(2)}) copy-start(s32[512,1]{0,1:T(1,128)} %param.13) | copy-start | bytes 6148
  8.0 21.5 %collective-permute-start.3 = (f32[16,8,128]{2,1,0:T(8,128)S(1)}, f32[16,8,128]{2,1,0:T(8,128)S(1)}, u32[]{:S(2)}, u32[]{:S(2)}) collective-permute-start(f32[16,8,128]{2,1,0:T(8,128)S(1)} %get-tuple-element.25), channel_id=1, source_target_pairs={{0,120},{8,0},{16,8},{24,16},{32,24},{40,32},{48,40},{56,48},{64,5... | collective-permute-start | bytes 196616 | tf_op jit(solution)/shard_map/ppermute | solution.py:327
  16.1 13.4 %collective-permute-start.2 = (f32[16,8,128]{2,1,0:T(8,128)S(1)}, f32[16,8,128]{2,1,0:T(8,128)S(1)}, u32[]{:S(2)}, u32[]{:S(2)}) collective-permute-start(f32[16,8,128]{2,1,0:T(8,128)S(1)} %get-tuple-element.24.__1_), channel_id=1, source_target_pairs={{0,8},{8,16},{16,24},{24,32},{32,40},{40,48},{48,56},{56,64},{64,7... | collective-permute-start | bytes 196616 | tf_op jit(solution)/shard_map/ppermute | solution.py:327
  16.1 13.3 %copy-start.7 = (f32[4,2]{0,1:T(2,128)S(1)}, f32[4,2]{0,1:T(2,128)}, u32[]{:S(2)}) copy-start(f32[4,2]{0,1:T(2,128)} %param.12) | copy-start | bytes 100
  16.1 13.4 %copy-start = (f32[4,2,64,128]{3,2,1,0:T(8,128)S(1)}, f32[4,2,64,128]{3,2,1,0:T(8,128)}, u32[]{:S(2)}) copy-start(f32[4,2,64,128]{3,2,1,0:T(8,128)} %conc.3) | copy-start | bytes 786436
  16.1 13.4 %copy-start.3 = (f32[2,64,128]{2,1,0:T(8,128)S(1)}, f32[2,64,128]{2,1,0:T(8,128)}, u32[]{:S(2)}) copy-start(f32[2,64,128]{2,1,0:T(8,128)} %vv.3) | copy-start | bytes 196612
  16.2 13.4 %copy-start.1 = (f32[2,64,128]{2,1,0:T(8,128)S(1)}, f32[2,64,128]{2,1,0:T(8,128)}, u32[]{:S(2)}) copy-start(f32[2,64,128]{2,1,0:T(8,128)} %kk.3) | copy-start | bytes 196612
  16.2 13.4 %copy-start.2 = (f32[2,64,128]{2,1,0:T(8,128)S(1)}, f32[2,64,128]{2,1,0:T(8,128)}, u32[]{:S(2)}) copy-start(f32[2,64,128]{2,1,0:T(8,128)} %uu.3) | copy-start | bytes 196612
  16.2 18.8 %all-to-all-start = ((f32[128,1,128]{2,1,0:T(1,128)}), f32[128,1,128]{2,1,0:T(1,128)S(1)}, u32[]{:S(2)}, u32[]{:S(2)}) async-start(f32[128,1,128]{2,1,0:T(1,128)} %bitcast.4), calls=%async_computation | async-start | bytes 131072 | tf_op jit(solution)/shard_map/all_to_all | solution.py:334
  35.0 2.8 %collective-permute-start.4 = (f32[64,128]{1,0:T(8,128)S(1)}, f32[64,128]{1,0:T(8,128)S(1)}, u32[]{:S(2)}, u32[]{:S(2)}) collective-permute-start(f32[64,128]{1,0:T(8,128)S(1)} %get-tuple-element.30.mine), channel_id=1, source_target_pairs={{0,128},{128,0},{1,129},{129,1},{2,130},{130,2},{3,131},{131,3},{4... | collective-permute-start | bytes 98312 | tf_op jit(solution)/shard_map/ppermute | solution.py:375
  37.8 16.7 %collective-permute-start.6 = (f32[64,128]{1,0:T(8,128)S(1)}, f32[64,128]{1,0:T(8,128)S(1)}, u32[]{:S(2)}, u32[]{:S(2)}) collective-permute-start(f32[64,128]{1,0:T(8,128)S(1)} %get-tuple-element.33.force), channel_id=1, source_target_pairs={{0,7},{1,0},{2,1},{3,2},{4,3},{5,4},{6,5},{7,6},{8,15},{9,8},{10,9... | collective-permute-start | bytes 98312 | tf_op jit(solution)/shard_map/ppermute | solution.py:327
  39.1 15.4 %collective-permute-start.5 = (f32[64,128]{1,0:T(8,128)S(1)}, f32[64,128]{1,0:T(8,128)S(1)}, u32[]{:S(2)}, u32[]{:S(2)}) collective-permute-start(f32[64,128]{1,0:T(8,128)S(1)} %get-tuple-element.33.force), channel_id=1, source_target_pairs={{0,1},{1,2},{2,3},{3,4},{4,5},{5,6},{6,7},{7,0},{8,9},{9,10},{10,1... | collective-permute-start | bytes 98312 | tf_op jit(solution)/shard_map/ppermute | solution.py:327
  40.7 22.0 %all-to-all-start.1 = ((f32[128,1,128]{2,1,0:T(1,128)}), f32[128,1,128]{2,1,0:T(1,128)S(1)}, u32[]{:S(2)}, u32[]{:S(2)}) async-start(f32[128,1,128]{2,1,0:T(1,128)} %bitcast.7), calls=%async_computation.1 | async-start | bytes 131072 | tf_op jit(solution)/shard_map/all_to_all | solution.py:334
  54.6 6.2 %collective-permute-start.7 = (f32[3,8,128]{2,1,0:T(8,128)S(1)}, f32[3,8,128]{2,1,0:T(8,128)S(1)}, u32[]{:S(2)}, u32[]{:S(2)}) collective-permute-start(f32[3,8,128]{2,1,0:T(8,128)S(1)} %get-tuple-element.34), channel_id=1, source_target_pairs={{0,8},{8,16},{16,24},{24,32},{32,40},{40,48},{48,56},{56,64},{64,7... | collective-permute-start | bytes 36872 | tf_op jit(solution)/shard_map/ppermute | solution.py:327
  55.5 5.3 %collective-permute-start.8 = (f32[3,8,128]{2,1,0:T(8,128)S(1)}, f32[3,8,128]{2,1,0:T(8,128)S(1)}, u32[]{:S(2)}, u32[]{:S(2)}) collective-permute-start(f32[3,8,128]{2,1,0:T(8,128)S(1)} %get-tuple-element.35), channel_id=1, source_target_pairs={{0,120},{8,0},{16,8},{24,16},{32,24},{40,32},{48,40},{56,48},{64,5... | collective-permute-start | bytes 36872 | tf_op jit(solution)/shard_map/ppermute | solution.py:327

commit v4 on v3

v4 whole, which is shorter than its diff:
```python
import functools

import jax
import jax.numpy as jnp
from jax import lax
from jax.experimental import pallas as pl
from jax.experimental.pallas import tpu as pltpu
from jax.sharding import PartitionSpec as P

STEPS = 4
CAP = 16
HALO = 4
EDGE = 8
F32 = jnp.float32
BF16 = jnp.bfloat16
VMEM = pl.BlockSpec(memory_space=pltpu.VMEM)
HBM = pl.BlockSpec(memory_space=pltpu.HBM)
ANY = pl.BlockSpec(memory_space=pl.ANY)
SMEM = pl.BlockSpec(memory_space=pltpu.SMEM)


def call(body, outs, inputs, specs=None, us=1.0, scratch=(), outspec=None, alias=None):
    return pl.pallas_call(
        body,
        out_shape=outs,
        in_specs=specs or [VMEM] * len(inputs),
        out_specs=outspec or jax.tree.map(lambda _: VMEM, outs),
        input_output_aliases=alias or {},
        scratch_shapes=list(scratch),
        compiler_params=pltpu.CompilerParams(vmem_limit_bytes=16 << 20),
        cost_estimate=pl.CostEstimate(
            flops=int(us * 1e6), bytes_accessed=int(us * 3e6), transcendentals=0
        ),
    )(*inputs)


def split3(x):
    a = x.astype(BF16)
    r = x - a.astype(F32)
    b = r.astype(BF16)
    c = (r - b.astype(F32)).astype(BF16)
    return a, b, c


def nt(a, b):
    return lax.dot_general(a, b, (((1,), (1,)), ((), ())), preferred_element_type=F32)


def nn(a, b):
    return jnp.dot(a, b, preferred_element_type=F32)


def iota(shape, dim):
    return lax.broadcasted_iota(jnp.int32, shape, dim)


def tile_at(t, groups):
    for shift in (3, 4, 3):
        t = (t * 109 + 55) & (groups - 1)
        t = t ^ (t >> shift)
    return t


def request_body(groups, ny, owner, column, observed, req, rank):
    rows, lanes = owner.shape
    before = (iota((lanes, lanes), 0) < iota((lanes, lanes), 1)).astype(F32).astype(BF16)
    ones = jnp.ones((lanes, lanes), BF16)
    carry = jnp.zeros((groups, lanes), F32)
    total = jnp.zeros((groups, lanes), F32)
    who = tile_at(iota((groups, lanes), 0), groups)
    for j in range(rows):
        onehot = (who == owner[j : j + 1, :]).astype(F32)
        hot = onehot.astype(BF16)
        prior = nn(hot, before) + carry
        place = jnp.sum(onehot * prior, axis=0, keepdims=True)
        carry = carry + nn(hot, ones)
        place = place.astype(jnp.int32)
        rank[j : j + 1, :] = place
        slot = (iota((CAP, lanes), 0) == place).astype(F32)
        code = column[j : j + 1, :] + 1
        low = code & (lanes - 1)
        obs = split3(observed[j : j + 1, :])
        codes = ((code - low).astype(F32), low.astype(F32), None)
        parts = []
        for part, o in zip(codes, obs):
            top = jnp.zeros_like(slot) if part is None else slot * part
            parts.append(jnp.concatenate([top, slot * o.astype(F32)], axis=0).astype(BF16))
        for i, shift in enumerate((0, ny, -ny)):
            near = hot if shift == 0 else (who + shift == owner[j : j + 1, :]).astype(F32).astype(BF16)
            for part in parts:
                low_zeros = jnp.zeros((2 * CAP * i, lanes), BF16)
                high_zeros = jnp.zeros((lanes - 2 * CAP * (i + 1), lanes), BF16)
                pieces = [low_zeros] * (i > 0) + [part, high_zeros]
                total = total + nt(near, jnp.concatenate(pieces, axis=0))
    req[...] = total


def inside(axis):
    i, n = lax.axis_index(axis), lax.axis_size(axis)
    return (i > 0).astype(F32), (i < n - 1).astype(F32)


def tiles(conc, kk, uu, vv):
    out = [conc.at[t, l] for t in range(conc.shape[0]) for l in range(conc.shape[1])]
    return out + [c.at[l] for c in (kk, uu, vv) for l in range(c.shape[0])]


def edges_body(conc, kk, uu, vv, right, left, high, low, c, k, u, v, sems):
    copies = [
        pltpu.make_async_copy(a, b, sems.at[i])
        for i, (a, b) in enumerate(((conc, c), (kk, k), (uu, u), (vv, v)))
    ]
    for copy in copies:
        copy.start()
    for copy in copies:
        copy.wait()
    n, m = c.shape[2], c.shape[3]
    at = iota((n, m), 1)
    up = down = jnp.zeros((n, m), F32)
    for f, tile in enumerate(tiles(c, k, u, v)):
        x = tile[...]
        high[f] = x[n - EDGE :]
        low[f] = x[:EDGE]
        mine = (at >= HALO * f) & (at < HALO * (f + 1))
        up = jnp.where(mine, pltpu.roll(x, (HALO * f + HALO) % m, 1), up)
        down = jnp.where(mine, pltpu.roll(x, HALO * f, 1) if f else x, down)
    right[...] = up
    left[...] = down


def corners_body(high, low, left, right, out_high, out_low):
    f, n = high.shape[0], left.shape[0]
    out_high[0:f] = high[...]
    out_low[0:f] = low[...]
    for i, side in enumerate((left, right)):
        out_high[f + i] = side[n - EDGE : n, :]
        out_low[f + i] = side[0:EDGE, :]


def spread(nat, pieces):
    at = 0
    for piece in pieces:
        nat[at : at + piece.shape[0]] = piece
        at += piece.shape[0]
    step = at // EDGE
    return [nat[pl.ds(g, EDGE, stride=step), :] for g in range(step)]


def gather(nat, parts):
    for g, part in enumerate(parts):
        nat[pl.ds(g, EDGE, stride=len(parts)), :] = part
    return nat


def halo(after, before):
    return jnp.where(iota(after.shape, 0) < HALO, after, before)


def ends():
    at = iota((EDGE, 128), 1)
    return at == 127, at == 0


def shifted(mid, side, up):
    last, first = ends()
    a, b = (pltpu.roll(x, 127 if up else 1, 1) for x in (mid, side))
    edge = last if up else first
    return jnp.where(edge, b, a), jnp.where(edge, a, b)


def ring_rows(load, g, steps):
    after = load(g + 1) if g + 1 < steps else pltpu.roll(load(0), EDGE - 1, 0)
    before = load(g - 1) if g else pltpu.roll(load(steps - 1), 1, 0)
    return after, before


def forward_step(state, old, new, fields, coef, steps):
    for g in range(steps):
        k = [[coef(i, h, g) for i in range(5)] for h in range(2)]
        for f in fields:
            mid = state[old, f, 0, g], state[old, f, 1, g]
            north, south = shifted(*mid, True), shifted(*mid, False)
            for h in range(2):
                e, w = ring_rows(lambda i: state[old, f, h, i], g, steps)
                state[new, f, h, g] = (
                    k[h][0] * mid[h]
                    + (k[h][1] * e + k[h][2] * w)
                    + (k[h][3] * north[h] + k[h][4] * south[h])
                )


def adjoint_step(state, old, new, f, coef, steps):
    for g in range(steps):
        mid = state[old, f, 0, g], state[old, f, 1, g]
        north = shifted(*(coef(4, h, g) * mid[h] for h in range(2)), True)
        south = shifted(*(coef(3, h, g) * mid[h] for h in range(2)), False)
        for h in range(2):
            e = ring_rows(lambda i: coef(2, h, i) * state[old, f, h, i], g, steps)[0]
            w = ring_rows(lambda i: coef(1, h, i) * state[old, f, h, i], g, steps)[1]
            state[new, f, h, g] = coef(0, h, g) * mid[h] + (e + w) + (north[h] + south[h])


def sides(left, right, f):
    at = iota((EDGE, 128), 1)
    out = []
    for p, q in zip(left, right):
        a = pltpu.roll(q, lax.rem(128 - HALO * f, 128), 1)
        b = pltpu.roll(p, lax.rem(256 - HALO - HALO * f, 128), 1)
        out.append(jnp.where(at < HALO, a, jnp.where(at >= 128 - HALO, b, 0.0)))
    return out


def store_coefs(coef, l, k, u, v):
    for h in range(2):
        for g in range(len(k[0])):
            a, b, c = k[h][g], 0.5 * u[h][g], 0.5 * v[h][g]
            for i, value in enumerate((1.0 - 4.0 * a, a - b, a + b, a - c, a + c)):
                coef[l, i, h, g] = value


def column_body(conc, kk, uu, vv, below, above, left, right, weight, column, coef, state, nat):
    keep_b, keep_a = inside("gx")
    keep_l, keep_r = inside("gy")
    n = conc.shape[2]
    tracers, levels = conc.shape[0], conc.shape[1]
    base = tracers * levels
    steps = (n + 2 * EDGE) // EDGE

    def pieces(tile, f):
        return tile, above[f] * keep_a, below[f] * keep_b

    from_left = [p * keep_l for p in spread(nat.at[0], pieces(left[...], base + 3 * levels))]
    from_right = [p * keep_r for p in spread(nat.at[1], pieces(right[...], base + 3 * levels + 1))]
    for l in range(levels):
        fs = [t * levels + l for t in range(tracers)]
        ws = [weight[t, l] for t in range(tracers)]
        parts = [pieces(conc[t, l], f) for t, f in enumerate(fs)]
        mixed = [sum(w * p[i] for w, p in zip(ws, parts)) for i in range(3)]
        mid = spread(nat.at[2 + l], mixed)
        side = [sum(w * x for w, x in zip(ws, xs)) for xs in zip(*(sides(from_left, from_right, f) for f in fs))]
        for g in range(steps):
            state[0, l, 0, g] = mid[g]
            state[0, l, 1, g] = side[g]
        wide = []
        for i, c in enumerate((kk, uu, vv)):
            f = base + i * levels + l
            wide.append((spread(nat.at[4 + 3 * l + i], pieces(c[l], f)), sides(from_left, from_right, f)))
        store_coefs(coef, l, *wide)
    for s in range(STEPS):
        for l in range(levels):
            forward_step(state, s % 2, 1 - s % 2, (l,), lambda i, h, g: coef[l, i, h, g], steps)
    total = gather(nat.at[0], [sum(state[STEPS % 2, l, 0, g] for l in range(levels)) for g in range(steps)])
    column[0:n] = total[0:n]
    column[n : n + EDGE] = halo(total[n : n + EDGE], total[n + EDGE : n + 2 * EDGE])


def forward_body(conc, kk, uu, vv, below, above, left, right, out, coef, state, nat):
    keep_b, keep_a = inside("gx")
    keep_l, keep_r = inside("gy")
    n = conc.shape[2]
    tracers, levels = conc.shape[0], conc.shape[1]
    base = tracers * levels
    steps = (n + EDGE) // EDGE

    def pieces(tile, f):
        return tile, halo(above[f] * keep_a, below[f] * keep_b)

    from_left = [p * keep_l for p in spread(nat.at[0], pieces(left[...], base + 3 * levels))]
    from_right = [p * keep_r for p in spread(nat.at[1], pieces(right[...], base + 3 * levels + 1))]

    def one(l, carry):
        wide = []
        for i, c in enumerate((kk, uu, vv)):
            f = base + i * levels + l
            wide.append((spread(nat.at[2 + i], pieces(c[l], f)), sides(from_left, from_right, f)))
        store_coefs(coef, l, *wide)
        for t in range(tracers):
            f = t * levels + l
            mid, side = spread(nat.at[5 + t], pieces(conc[t, l], f)), sides(from_left, from_right, f)
            for g in range(steps):
                state[0, t, 0, g] = mid[g]
                state[0, t, 1, g] = side[g]
        for s in range(STEPS):
            forward_step(state, s % 2, 1 - s % 2, range(tracers), lambda i, h, g: coef[l, i, h, g], steps)
        for t in range(tracers):
            value = gather(nat.at[5 + t], [state[STEPS % 2, t, 0, g] for g in range(steps)])
            out[t, l] = value[0:n]
        return carry

    lax.fori_loop(0, levels, one, 0)


def slots(code, first, n, m):
    where = code.astype(jnp.int32) - 1
    x, y = (where >> (m.bit_length() - 1)) - first, where & (m - 1)
    xs, ys = [], []
    for s in range(CAP):
        xs.append((iota((n, x.shape[1]), 0) == x[s : s + 1, :]).astype(F32))
        ys.append((iota((m, x.shape[1]), 0) == y[s : s + 1, :]).astype(F32).astype(BF16))
    return xs, ys


def force_body(asked, mine, other, values, force):
    n, m = mine.shape[0] - EDGE, mine.shape[1]
    t = asked[...].T
    sums = jnp.zeros((4 * n, m), F32)
    rims = jnp.zeros((4 * EDGE, m), F32)
    for i in range(3):
        part = t[2 * CAP * i : 2 * CAP * (i + 1)]
        obs = [o.astype(F32) for o in split3(part[CAP:])]
        if i == 0:
            xs, ys = slots(part[:CAP], 0, n, m)
        else:
            xs, ys = slots(part[:CAP], 0 if i == 1 else n - EDGE, EDGE, m)
            rim = iota((EDGE, m), 0)
            keep = ((rim < HALO) if i == 1 else (rim >= HALO)).astype(F32)
            xs = [x * keep for x in xs]
        for s in range(CAP):
            lhs = [xs[s]] + [xs[s] * o[s : s + 1, :] for o in obs]
            got = nt(jnp.concatenate(lhs, axis=0).astype(BF16), ys[s])
            if i == 0:
                sums = sums + got
            else:
                rims = rims + got
    for at, rows, tall in ((0, n, sums), (n, EDGE, rims)):
        count = tall[:rows]
        seen = tall[rows : 2 * rows] + tall[2 * rows : 3 * rows] + tall[3 * rows :]
        where = slice(at, at + rows)
        force[where] = count * (mine[where] + other[where]) - seen


def values_body(asked, mine, other, values):
    n, m = mine.shape[0] - EDGE, mine.shape[1]
    field = mine[0:n] + other[0:n]
    t = asked[...].T
    xs, ys = slots(t[:CAP], 0, n, m)
    fields = jnp.concatenate(split3(field), axis=0)
    picked = []
    for s in range(CAP):
        z = nn(fields, ys[s])
        z = (z[:n] + z[n : 2 * n] + z[2 * n :]) * xs[s]
        picked.append(jnp.sum(z, axis=0, keepdims=True))
    picked.append(jnp.zeros((t.shape[0] - CAP, t.shape[1]), F32))
    values[...] = jnp.concatenate(picked, axis=0).T


def answer_body(groups, got, owner, rank, out):
    rows, lanes = owner.shape
    t = got[...].T[:CAP]
    parts = jnp.concatenate(split3(t), axis=0)
    who = tile_at(iota((groups, lanes), 0), groups)
    for j in range(rows):
        onehot = (who == owner[j : j + 1, :]).astype(F32)
        z = nn(parts, onehot.astype(BF16))
        z = z[:CAP] + z[CAP : 2 * CAP] + z[2 * CAP :]
        slot = iota((CAP, lanes), 0) == rank[j : j + 1, :]
        out[j : j + 1, :] = jnp.sum(jnp.where(slot, z, 0.0), axis=0, keepdims=True)


def adjoint_body(force, left, right, coef, weight, out, state, nat):
    keep_l, keep_r = inside("gy")
    n, m = out.shape[2], out.shape[3]
    at = iota((EDGE, m), 1)
    mid, a, b = (spread(nat.at[i], (x[...],)) for i, x in enumerate((force, right, left)))
    levels = out.shape[1]
    steps = len(mid)
    for g in range(steps):
        side = jnp.where(at < HALO, a[g] * keep_r, jnp.where(at >= m - HALO, b[g] * keep_l, 0.0))
        for l in range(levels):
            state[0, l, 0, g] = mid[g]
            state[0, l, 1, g] = side
    for s in range(STEPS):
        for l in range(levels):
            adjoint_step(state, s % 2, 1 - s % 2, l, lambda i, h, g: coef[l, i, h, g], steps)
    for l in range(levels):
        value = gather(nat.at[3 + l], [state[STEPS % 2, l, 0, g] for g in range(steps)])
        for t in range(out.shape[0]):
            out[t, l] = weight[t, l] * value[0:n]


def after(x, other):
    shape = jax.ShapeDtypeStruct(x.shape, x.dtype)
    return call(lambda *_: None, shape, (x, other), [ANY] * 2, us=600.0, outspec=ANY, alias={0: 0})


def ring(value, axis, step):
    n = lax.axis_size(axis)
    return lax.ppermute(value, axis, [(i, (i + step) % n) for i in range(n)])


def exchange(value):
    nx, ny = lax.axis_size("gx"), lax.axis_size("gy")
    order = [tile_at(t, nx * ny) for t in range(nx * ny)]
    groups = [[(g ^ (2 * t // (nx * ny))) * nx * ny + t for t in order] for g in range(2)]
    return lax.all_to_all(
        value, ("lev", "gx", "gy"), 0, 0, axis_index_groups=groups, tiled=True
    )


def shards(conc, kk, uu, vv, weight, owner, column, observed):
    S = jax.ShapeDtypeStruct
    tracers, levels, n, m = conc.shape
    fields = (tracers + 3) * levels
    groups = lax.axis_size("gx") * lax.axis_size("gy")
    owner = owner.reshape(-1, 128)
    column = column.reshape(-1, 128)
    obs = observed.reshape(-1, 128)
    tile, edge = S((n, m), F32), S((fields, EDGE, m), F32)
    right, left, high, low = call(
        edges_body,
        (tile, tile, edge, edge),
        [pltpu.with_memory_space_constraint(a, pltpu.HBM) for a in (conc, kk, uu, vv)],
        [HBM] * 4,
        scratch=[pltpu.VMEM(a.shape, F32) for a in (conc, kk, uu, vv)]
        + [pltpu.SemaphoreType.DMA((4,))],
    )
    left, right = ring(right, "gy", 1), ring(left, "gy", -1)
    req, rank = call(
        functools.partial(request_body, groups, lax.axis_size("gy")),
        (S((groups, 128), F32), S(owner.shape, jnp.int32)),
        (owner, column, obs),
        us=600.0,
    )
    edge = S((fields + 2, EDGE, m), F32)
    high, low = call(corners_body, (edge, edge), (high, low, left, right))
    below, above = ring(high, "gx", 1), ring(low, "gx", -1)
    asked = exchange(after(req, high))
    inputs = (conc, kk, uu, vv, below, above, left, right)
    strip = S((n + EDGE, m), F32)
    more, some = (n + 2 * EDGE) // EDGE, (n + EDGE) // EDGE
    mine = call(
        column_body,
        strip,
        (*inputs, weight),
        [VMEM] * 8 + [SMEM],
        us=600.0,
        scratch=[
            pltpu.VMEM((levels, 5, 2, more, EDGE, m), F32),
            pltpu.VMEM((2, levels, 2, more, EDGE, m), F32),
            pltpu.VMEM((4 + 3 * levels, n + 2 * EDGE, m), F32),
        ],
    )
    other = lax.ppermute(mine, "lev", [(0, 1), (1, 0)])
    forecast, coef = call(
        forward_body,
        (S(conc.shape, F32), S((levels, 5, 2, some, EDGE, m), F32)),
        inputs,
        us=600.0,
        scratch=[
            pltpu.VMEM((2, tracers, 2, some, EDGE, m), F32),
            pltpu.VMEM((5 + tracers, n + EDGE, m), F32),
        ],
    )
    values = call(values_body, S((groups, 128), F32), (asked, mine, other), us=600.0)
    got = exchange(values)
    force = call(
        force_body, strip, (asked, mine, other, values), [VMEM] * 3 + [ANY], us=600.0
    )
    left, right = ring(force, "gy", 1), ring(force, "gy", -1)
    gradient = call(
        adjoint_body,
        S(conc.shape, F32),
        (force, left, right, coef, weight),
        [VMEM] * 4 + [SMEM],
        us=600.0,
        scratch=[
            pltpu.VMEM((2, levels, 2, some, EDGE, m), F32),
            pltpu.VMEM((3 + levels, n + EDGE, m), F32),
        ],
    )
    model = call(
        functools.partial(answer_body, groups), S(owner.shape, F32), (got, owner, rank)
    )
    return (forecast, model.reshape(-1), gradient)


def solution(mesh):
    return jax.shard_map(
        shards,
        mesh=mesh,
        in_specs=(
            P(None, "lev", "gx", "gy"),
            P("lev", "gx", "gy"),
            P("lev", "gx", "gy"),
            P("lev", "gx", "gy"),
            P(None, "lev"),
            P(("gx", "gy"), None),
            P(("gx", "gy")),
            P(("gx", "gy")),
        ),
        out_specs=(P(None, "lev", "gx", "gy"), P(("gx", "gy")), P(None, "lev", "gx", "gy")),
        check_vma=False,
    )
```

time: 63.8 us -> 58.2 us (0.912)
  starting transfers between devices: 45.4 us -> 41.1 us
  Pallas kernels: 12.4 us -> 11.6 us
    ppermute x8 -> x6, starting transfers between devices: 18.3 us -> 13.2 us  [ring(): return lax.ppermute(value, axis, [(i, (i + step) % n) for i in range(n)])]
    ppermute x8 -> x6, waiting for transfers between devices: 1.9 us -> 0.28 us  [ring(): return lax.ppermute(value, axis, [(i, (i + step) % n) for i in range(n)])]
    ppermute x1, waiting for transfers between devices: 2.24 us -> 3.09 us  [shards(): other = lax.ppermute(mine, 'lev', [(0, 1), (1, 0)])]
    pallas_call x11 -> x10, Pallas kernels: 12.4 us -> 11.6 us  [call(): pl.pallas_call(body, out_shape=outs, in_specs=specs or [VMEM] * len(input...]
    all_to_all x2, starting transfers between devices: 27.1 us -> 27.8 us  [exchange(): lax.all_to_all(value, ('lev', 'gx', 'gy'), 0, 0, axis_index_groups=groups...]
  transfers between devices with their start and end apart: 11 -> 9, of which waited for: 3 -> 3; matrix products, arithmetic and copies ran while one was open for 0% -> 0% of each run, Pallas kernels for 16% -> 14%
where the time goes in v4:
time: 58.2 us; the launch traced here: 58 us
  starting transfers between devices  41.1 us (71%)
  Pallas kernels  11.6 us (20%)
  waiting for transfers between devices  3.75 us (6%)
  local copies, waits for them, and re-layouts  0.81 us (1%)
  between operations  0.76 us (1%)
    all_to_all x2, starting transfers between devices, exchange(): lax.all_to_all(value, ('lev', 'gx', 'gy'), 0, 0, axis_index_groups=groups...  27.8 us
    ppermute x6, starting transfers between devices, ring(): return lax.ppermute(value, axis, [(i, (i + step) % n) for i in range(n)])  13.2 us
    pallas_call x10, Pallas kernels, call(): pl.pallas_call(body, out_shape=outs, in_specs=specs or [VMEM] * len(input...  11.6 us
    ppermute x1, waiting for transfers between devices, shards(): other = lax.ppermute(mine, 'lev', [(0, 1), (1, 0)])  3.09 us
  transfers between devices with their start and end apart: 9, of which 3 were waited for; matrix products, arithmetic and copies ran while one was open for 0% of the time, Pallas kernels for 14%

profile of v4, /device:TPU:1, one launch (start us, length us, event | category | flops | bytes accessed | tf_op | source)
XLA Modules:
  0.0 58.0 jit_solution(12079538218509449280)
XLA Ops:
  0.6 1.3 %shard_map.103 = (f32[64,128]{1,0:T(8,128)S(1)}, f32[64,128]{1,0:T(8,128)S(1)}, f32[14,8,128]{2,1,0:T(8,128)S(1)}, f32[14,8,128]{2,1,0:T(8,128)S(1)}) custom-call(f32[4,2,64,128]{3,2,1,0:T(8,128)} %conc.5, f32[2,64,128]{2,1,0:T(8,128)} %kk.5, f32[2,64,128]{2,1,0:T(8,128)} %uu.5, f32[2,64,128]{2,1,0:T(8,128)} %vv.5), custom_call_target="tpu_custom_call" | custom-call | flops 1000000 | bytes 3000000 | tf_op jit(solution)/shard_map/pallas_call | solution.py:23
  2.0 0.0 copy-start.5
  2.0 2.7 %collective-permute-start = (f32[64,128]{1,0:T(8,128)S(1)}, f32[64,128]{1,0:T(8,128)S(1)}, u32[]{:S(2)}, u32[]{:S(2)}) collective-permute-start(f32[64,128]{1,0:T(8,128)S(1)} %get-tuple-element.15), channel_id=1, source_target_pairs={{0,1},{1,2},{2,3},{3,4},{4,5},{5,6},{6,7},{7,0},{8,9},{9,10},{10,1... | collective-permute-start | bytes 98312 | tf_op jit(solution)/shard_map/ppermute | solution.py:388
  4.7 0.6 collective-permute-start.1
  5.3 0.7 %copy-done.4 = s32[512,1]{0,1:T(1,128)S(1)} copy-done((s32[512,1]{0,1:T(1,128)S(1)}, s32[512,1]{0,1:T(1,128)}, u32[]{:S(2)}) %copy-start.4) | copy-done | bytes 2072
  5.9 1.8 %shard_map.106 = (f32[128,128]{1,0:T(8,128)}, s32[4,128]{1,0:T(4,128)S(1)}) custom-call(s32[4,128]{1,0:T(4,128)S(1)} %bitcast.15, s32[4,128]{1,0:T(4,128)S(1)} %bitcast.17, f32[4,128]{1,0:T(4,128)S(1)} %bitcast.18), custom_call_target="tpu_custom_call" | custom-call | flops 600000000 | bytes 1800000000 | tf_op jit(solution)/shard_map/pallas_call | solution.py:23
  7.8 0.3 collective-permute-done.1.right
  8.0 8.1 %collective-permute-start.3 = (f32[16,8,128]{2,1,0:T(8,128)S(1)}, f32[16,8,128]{2,1,0:T(8,128)S(1)}, u32[]{:S(2)}, u32[]{:S(2)}) collective-permute-start(f32[16,8,128]{2,1,0:T(8,128)S(1)} %get-tuple-element.18), channel_id=1, source_target_pairs={{0,120},{8,0},{16,8},{24,16},{32,24},{40,32},{48,40},{56,48},{64,5... | collective-permute-start | bytes 196616 | tf_op jit(solution)/shard_map/ppermute | solution.py:388
  16.2 0.0 copy-start.1
  16.2 0.0 copy-start.2
  16.2 13.8 %all-to-all-start = ((f32[128,1,128]{2,1,0:T(1,128)}), f32[128,1,128]{2,1,0:T(1,128)S(1)}, u32[]{:S(2)}, u32[]{:S(2)}) async-start(f32[128,1,128]{2,1,0:T(1,128)} %bitcast.4), calls=%async_computation | async-start | bytes 131072 | tf_op jit(solution)/shard_map/all_to_all | solution.py:395
  30.1 0.1 copy.15.weight
  30.2 1.3 %shard_map.108.mine = f32[72,128]{1,0:T(8,128)S(1)} custom-call(f32[4,2,64,128]{3,2,1,0:T(8,128)S(1)} %copy-done, f32[2,64,128]{2,1,0:T(8,128)S(1)} %copy-done.1, f32[2,64,128]{2,1,0:T(8,128)S(1)} %copy-done.2, f32[2,64,128]{2,1,0:T(8,128)S(1)} %copy-done.3, f32[16,8,128]{2,1,0:T(8,128)S(1)} %collective-permute-done.2.below, ...), custom_call_target="tpu_custom_call" | custom-call | flops 600000000 | bytes 1800000000 | tf_op jit(solution)/shard_map/pallas_call | solution.py:23
  31.5 0.1 collective-permute-start.4
  31.6 3.1 %collective-permute-done.4.other = f32[72,128]{1,0:T(8,128)S(1)} collective-permute-done((f32[72,128]{1,0:T(8,128)S(1)}, f32[72,128]{1,0:T(8,128)S(1)}, u32[]{:S(2)}, u32[]{:S(2)}) %collective-permute-start.4) | collective-permute-done | bytes 36896 | tf_op jit(solution)/shard_map/ppermute | solution.py:443
  34.7 0.4 all-to-all-done
  35.1 1.2 %shard_map.109.values = f32[128,128]{1,0:T(8,128)} custom-call(f32[128,128]{1,0:T(8,128)S(1)} %bitcast.13, f32[72,128]{1,0:T(8,128)S(1)} %shard_map.108.mine, f32[72,128]{1,0:T(8,128)S(1)} %collective-permute-done.4.other), custom_call_target="tpu_custom_call" | custom-call | flops 600000000 | bytes 1800000000 | tf_op jit(solution)/shard_map/pallas_call | solution.py:23
  36.2 14.0 %all-to-all-start.1 = ((f32[128,1,128]{2,1,0:T(1,128)}), f32[128,1,128]{2,1,0:T(1,128)S(1)}, u32[]{:S(2)}, u32[]{:S(2)}) async-start(f32[128,1,128]{2,1,0:T(1,128)} %bitcast.7), calls=%async_computation.1 | async-start | bytes 131072 | tf_op jit(solution)/shard_map/all_to_all | solution.py:395
  50.2 1.0 %shard_map.111.force = f32[72,128]{1,0:T(8,128)S(1)} custom-call(f32[128,128]{1,0:T(8,128)S(1)} %bitcast.14, f32[72,128]{1,0:T(8,128)S(1)} %shard_map.108.mine, f32[72,128]{1,0:T(8,128)S(1)} %collective-permute-done.4.other, f32[128,128]{1,0:T(8,128)} %shard_map.109.values), custom_call_target="tpu_custom_call" | custom-call | flops 600000000 | bytes 1800000000 | tf_op jit(solution)/shard_map/pallas_call | solution.py:23
  51.2 0.2 collective-permute-start.6
  51.4 1.6 %collective-permute-start.5 = (f32[72,128]{1,0:T(8,128)S(1)}, f32[72,128]{1,0:T(8,128)S(1)}, u32[]{:S(2)}, u32[]{:S(2)}) collective-permute-start(f32[72,128]{1,0:T(8,128)S(1)} %shard_map.111.force), channel_id=1, source_target_pairs={{0,1},{1,2},{2,3},{3,4},{4,5},{5,6},{6,7},{7,0},{8,9},{9,10},{10,1... | collective-permute-start | bytes 110600 | tf_op jit(solution)/shard_map/ppermute | solution.py:388
  53.0 2.5 %shard_map.105 = (f32[4,2,64,128]{3,2,1,0:T(8,128)}, f32[2,5,2,9,8,128]{5,4,3,2,1,0:T(8,128)S(1)}) custom-call(f32[4,2,64,128]{3,2,1,0:T(8,128)S(1)} %copy-done, f32[2,64,128]{2,1,0:T(8,128)S(1)} %copy-done.1, f32[2,64,128]{2,1,0:T(8,128)S(1)} %copy-done.2, f32[2,64,128]{2,1,0:T(8,128)S(1)} %copy-done.3, f32[16,8,128]{2,1,0:T(8,128)S(1)} %collective-permute-done.2.below, ...), custom_call_target="tpu_custom_call" | custom-call | flops 600000000 | bytes 1800000000 | tf_op jit(solution)/shard_map/pallas_call | solution.py:23
  55.5 1.7 %shard_map.112 = f32[4,2,64,128]{3,2,1,0:T(8,128)} custom-call(f32[72,128]{1,0:T(8,128)S(1)} %shard_map.111.force, f32[72,128]{1,0:T(8,128)S(1)} %collective-permute-done.5.left, f32[72,128]{1,0:T(8,128)S(1)} %collective-permute-done.6.right, f32[2,5,2,9,8,128]{5,4,3,2,1,0:T(8,128)S(1)} %get-tuple-element.22.coef, f32[4,2]{1,0:T(4,128)S(1)} %copy.15.weight), custom_call_target="tpu_custom_call" | custom-call | flops 600000000 | bytes 1800000000 | tf_op jit(solution)/shard_map/pallas_call | solution.py:23
  57.2 0.8 %shard_map.110 = f32[4,128]{1,0:T(4,128)} custom-call(f32[128,128]{1,0:T(8,128)S(1)} %bitcast.12, s32[4,128]{1,0:T(4,128)S(1)} %bitcast.16, s32[4,128]{1,0:T(4,128)S(1)} %get-tuple-element.21.rank), custom_call_target="tpu_custom_call" | custom-call | flops 1000000 | bytes 3000000 | tf_op jit(solution)/shard_map/pallas_call | solution.py:23
  (21 shorter events, 0.1 us)
Async XLA Ops:
  2.0 3.3 %copy-start.5 = (s32[512]{0:T(512)S(1)}, s32[512]{0:T(512)}, u32[]{:S(2)}) copy-start(s32[512]{0:T(512)} %param.14) | copy-start | bytes 6148
  2.0 3.3 %copy-start.6 = (f32[512]{0:T(512)S(1)}, f32[512]{0:T(512)}, u32[]{:S(2)}) copy-start(f32[512]{0:T(512)} %param.15) | copy-start | bytes 6148
  2.0 5.8 %collective-permute-start = (f32[64,128]{1,0:T(8,128)S(1)}, f32[64,128]{1,0:T(8,128)S(1)}, u32[]{:S(2)}, u32[]{:S(2)}) collective-permute-start(f32[64,128]{1,0:T(8,128)S(1)} %get-tuple-element.15), channel_id=1, source_target_pairs={{0,1},{1,2},{2,3},{3,4},{4,5},{5,6},{6,7},{7,0},{8,9},{9,10},{10,1... | collective-permute-start | bytes 98312 | tf_op jit(solution)/shard_map/ppermute | solution.py:388
  4.7 3.3 %collective-permute-start.1 = (f32[64,128]{1,0:T(8,128)S(1)}, f32[64,128]{1,0:T(8,128)S(1)}, u32[]{:S(2)}, u32[]{:S(2)}) collective-permute-start(f32[64,128]{1,0:T(8,128)S(1)} %get-tuple-element.16), channel_id=1, source_target_pairs={{0,7},{1,0},{2,1},{3,2},{4,3},{5,4},{6,5},{7,6},{8,15},{9,8},{10,9... | collective-permute-start | bytes 98312 | tf_op jit(solution)/shard_map/ppermute | solution.py:388
  5.3 0.7 %copy-start.4 = (s32[512,1]{0,1:T(1,128)S(1)}, s32[512,1]{0,1:T(1,128)}, u32[]{:S(2)}) copy-start(s32[512,1]{0,1:T(1,128)} %param.13) | copy-start | bytes 6148
  8.0 22.1 %collective-permute-start.3 = (f32[16,8,128]{2,1,0:T(8,128)S(1)}, f32[16,8,128]{2,1,0:T(8,128)S(1)}, u32[]{:S(2)}, u32[]{:S(2)}) collective-permute-start(f32[16,8,128]{2,1,0:T(8,128)S(1)} %get-tuple-element.18), channel_id=1, source_target_pairs={{0,120},{8,0},{16,8},{24,16},{32,24},{40,32},{48,40},{56,48},{64,5... | collective-permute-start | bytes 196616 | tf_op jit(solution)/shard_map/ppermute | solution.py:388
  16.1 14.0 %collective-permute-start.2 = (f32[16,8,128]{2,1,0:T(8,128)S(1)}, f32[16,8,128]{2,1,0:T(8,128)S(1)}, u32[]{:S(2)}, u32[]{:S(2)}) collective-permute-start(f32[16,8,128]{2,1,0:T(8,128)S(1)} %get-tuple-element.17.__1_), channel_id=1, source_target_pairs={{0,8},{8,16},{16,24},{24,32},{32,40},{40,48},{48,56},{56,64},{64,7... | collective-permute-start | bytes 196616 | tf_op jit(solution)/shard_map/ppermute | solution.py:388
  16.1 13.9 %copy-start.7 = (f32[4,2]{0,1:T(2,128)S(1)}, f32[4,2]{0,1:T(2,128)}, u32[]{:S(2)}) copy-start(f32[4,2]{0,1:T(2,128)} %param.12) | copy-start | bytes 100
  16.1 14.0 %copy-start = (f32[4,2,64,128]{3,2,1,0:T(8,128)S(1)}, f32[4,2,64,128]{3,2,1,0:T(8,128)}, u32[]{:S(2)}) copy-start(f32[4,2,64,128]{3,2,1,0:T(8,128)} %conc.5) | copy-start | bytes 786436
  16.1 14.0 %copy-start.3 = (f32[2,64,128]{2,1,0:T(8,128)S(1)}, f32[2,64,128]{2,1,0:T(8,128)}, u32[]{:S(2)}) copy-start(f32[2,64,128]{2,1,0:T(8,128)} %vv.5) | copy-start | bytes 196612
  16.2 14.0 %copy-start.1 = (f32[2,64,128]{2,1,0:T(8,128)S(1)}, f32[2,64,128]{2,1,0:T(8,128)}, u32[]{:S(2)}) copy-start(f32[2,64,128]{2,1,0:T(8,128)} %kk.5) | copy-start | bytes 196612
  16.2 14.0 %copy-start.2 = (f32[2,64,128]{2,1,0:T(8,128)S(1)}, f32[2,64,128]{2,1,0:T(8,128)}, u32[]{:S(2)}) copy-start(f32[2,64,128]{2,1,0:T(8,128)} %uu.5) | copy-start | bytes 196612
  16.2 18.9 %all-to-all-start = ((f32[128,1,128]{2,1,0:T(1,128)}), f32[128,1,128]{2,1,0:T(1,128)S(1)}, u32[]{:S(2)}, u32[]{:S(2)}) async-start(f32[128,1,128]{2,1,0:T(1,128)} %bitcast.4), calls=%async_computation | async-start | bytes 131072 | tf_op jit(solution)/shard_map/all_to_all | solution.py:395
  31.5 3.2 %collective-permute-start.4 = (f32[72,128]{1,0:T(8,128)S(1)}, f32[72,128]{1,0:T(8,128)S(1)}, u32[]{:S(2)}, u32[]{:S(2)}) collective-permute-start(f32[72,128]{1,0:T(8,128)S(1)} %shard_map.108.mine), channel_id=1, source_target_pairs={{0,128},{128,0},{1,129},{129,1},{2,130},{130,2},{3,131},{131,3},{4... | collective-permute-start | bytes 110600 | tf_op jit(solution)/shard_map/ppermute | solution.py:443
  36.2 20.9 %all-to-all-start.1 = ((f32[128,1,128]{2,1,0:T(1,128)}), f32[128,1,128]{2,1,0:T(1,128)S(1)}, u32[]{:S(2)}, u32[]{:S(2)}) async-start(f32[128,1,128]{2,1,0:T(1,128)} %bitcast.7), calls=%async_computation.1 | async-start | bytes 131072 | tf_op jit(solution)/shard_map/all_to_all | solution.py:395
  51.2 4.3 %collective-permute-start.6 = (f32[72,128]{1,0:T(8,128)S(1)}, f32[72,128]{1,0:T(8,128)S(1)}, u32[]{:S(2)}, u32[]{:S(2)}) collective-permute-start(f32[72,128]{1,0:T(8,128)S(1)} %shard_map.111.force), channel_id=1, source_target_pairs={{0,7},{1,0},{2,1},{3,2},{4,3},{5,4},{6,5},{7,6},{8,15},{9,8},{10,9... | collective-permute-start | bytes 110600 | tf_op jit(solution)/shard_map/ppermute | solution.py:388
  51.4 4.1 %collective-permute-start.5 = (f32[72,128]{1,0:T(8,128)S(1)}, f32[72,128]{1,0:T(8,128)S(1)}, u32[]{:S(2)}, u32[]{:S(2)}) collective-permute-start(f32[72,128]{1,0:T(8,128)S(1)} %shard_map.111.force), channel_id=1, source_target_pairs={{0,1},{1,2},{2,3},{3,4},{4,5},{5,6},{6,7},{7,0},{8,9},{9,10},{10,1... | collective-permute-start | bytes 110600 | tf_op jit(solution)/shard_map/ppermute | solution.py:388

commit v5 on v4

--- a/solution.py
+++ b/solution.py
@@ -64,34 +64,33 @@
 def request_body(groups, ny, owner, column, observed, req, rank):
     rows, lanes = owner.shape
     before = (iota((lanes, lanes), 0) < iota((lanes, lanes), 1)).astype(F32).astype(BF16)
-    ones = jnp.ones((lanes, lanes), BF16)
+    sums = jnp.concatenate([before, jnp.ones((lanes, lanes), BF16)], axis=1)
     carry = jnp.zeros((groups, lanes), F32)
-    total = jnp.zeros((groups, lanes), F32)
     who = tile_at(iota((groups, lanes), 0), groups)
+    own = [owner[j : j + 1, :] for j in range(rows)]
+    values = []
     for j in range(rows):
-        onehot = (who == owner[j : j + 1, :]).astype(F32)
-        hot = onehot.astype(BF16)
-        prior = nn(hot, before) + carry
-        place = jnp.sum(onehot * prior, axis=0, keepdims=True)
-        carry = carry + nn(hot, ones)
+        onehot = (who == own[j]).astype(F32)
+        got = nn(onehot.astype(BF16), sums)
+        place = jnp.sum(onehot * (got[:, :lanes] + carry), axis=0, keepdims=True)
+        carry = carry + got[:, lanes:]
         place = place.astype(jnp.int32)
         rank[j : j + 1, :] = place
         slot = (iota((CAP, lanes), 0) == place).astype(F32)
         code = column[j : j + 1, :] + 1
         low = code & (lanes - 1)
-        obs = split3(observed[j : j + 1, :])
-        codes = ((code - low).astype(F32), low.astype(F32), None)
-        parts = []
-        for part, o in zip(codes, obs):
-            top = jnp.zeros_like(slot) if part is None else slot * part
-            parts.append(jnp.concatenate([top, slot * o.astype(F32)], axis=0).astype(BF16))
-        for i, shift in enumerate((0, ny, -ny)):
-            near = hot if shift == 0 else (who + shift == owner[j : j + 1, :]).astype(F32).astype(BF16)
-            for part in parts:
-                low_zeros = jnp.zeros((2 * CAP * i, lanes), BF16)
-                high_zeros = jnp.zeros((lanes - 2 * CAP * (i + 1), lanes), BF16)
-                pieces = [low_zeros] * (i > 0) + [part, high_zeros]
-                total = total + nt(near, jnp.concatenate(pieces, axis=0))
+        o1, o2, o3 = (o.astype(F32) for o in split3(observed[j : j + 1, :]))
+        pieces = ((code - low).astype(F32), o1, low.astype(F32), o2, 0.0, o3, 0.0, 0.0)
+        values.append(jnp.concatenate([slot * p for p in pieces], axis=0).astype(BF16))
+    values = jnp.concatenate(values, axis=1)
+    at = iota((groups, lanes), 1)
+    total = jnp.zeros((groups, lanes), F32)
+    for i, shift in enumerate((0, ny, -ny)):
+        near = jnp.concatenate([(who + shift == o).astype(F32).astype(BF16) for o in own], axis=1)
+        got = nt(near, values)
+        moved = [pltpu.roll(got, (2 * CAP * (i + 4 - p)) % lanes, 1) for p in range(3)]
+        mine = (at >= 2 * CAP * i) & (at < 2 * CAP * (i + 1))
+        total = jnp.where(mine, moved[0] + moved[1] + moved[2], total)
     req[...] = total
 
 
@@ -105,10 +104,12 @@
     return out + [c.at[l] for c in (kk, uu, vv) for l in range(c.shape[0])]
 
 
-def edges_body(conc, kk, uu, vv, right, left, high, low, c, k, u, v, sems):
+def edges_body(conc, kk, uu, vv, own, col, obs, right, left, high, low, own_v, col_v, obs_v, c, k, u, v, sems):
     copies = [
         pltpu.make_async_copy(a, b, sems.at[i])
-        for i, (a, b) in enumerate(((conc, c), (kk, k), (uu, u), (vv, v)))
+        for i, (a, b) in enumerate(
+            ((conc, c), (kk, k), (uu, u), (vv, v), (own, own_v), (col, col_v), (obs, obs_v))
+        )
     ]
     for copy in copies:
         copy.start()
@@ -329,7 +330,7 @@
         force[where] = count * (mine[where] + other[where]) - seen
 
 
-def values_body(asked, mine, other, values):
+def values_body(asked, mine, other, coef, values):
     n, m = mine.shape[0] - EDGE, mine.shape[1]
     field = mine[0:n] + other[0:n]
     t = asked[...].T
@@ -406,25 +407,27 @@
     column = column.reshape(-1, 128)
     obs = observed.reshape(-1, 128)
     tile, edge = S((n, m), F32), S((fields, EDGE, m), F32)
-    right, left, high, low = call(
+    sounding = (owner, column, obs)
+    right, left, high, low, *sounding = call(
         edges_body,
-        (tile, tile, edge, edge),
-        [pltpu.with_memory_space_constraint(a, pltpu.HBM) for a in (conc, kk, uu, vv)],
-        [HBM] * 4,
+        (tile, tile, edge, edge, *(S(a.shape, a.dtype) for a in sounding)),
+        [pltpu.with_memory_space_constraint(a, pltpu.HBM) for a in (conc, kk, uu, vv, *sounding)],
+        [HBM] * 7,
         scratch=[pltpu.VMEM(a.shape, F32) for a in (conc, kk, uu, vv)]
-        + [pltpu.SemaphoreType.DMA((4,))],
-    )
+        + [pltpu.SemaphoreType.DMA((7,))],
+    )
+    owner = sounding[0]
     left, right = ring(right, "gy", 1), ring(left, "gy", -1)
     req, rank = call(
         functools.partial(request_body, groups, lax.axis_size("gy")),
         (S((groups, 128), F32), S(owner.shape, jnp.int32)),
-        (owner, column, obs),
+        tuple(sounding),
         us=600.0,
     )
     edge = S((fields + 2, EDGE, m), F32)
     high, low = call(corners_body, (edge, edge), (high, low, left, right))
-    below, above = ring(high, "gx", 1), ring(low, "gx", -1)
-    asked = exchange(after(req, high))
+    above, below = ring(low, "gx", -1), ring(high, "gx", 1)
+    asked = exchange(after(req, low))
     inputs = (conc, kk, uu, vv, below, above, left, right)
     strip = S((n + EDGE, m), F32)
     more, some = (n + 2 * EDGE) // EDGE, (n + EDGE) // EDGE
@@ -451,7 +454,13 @@
             pltpu.VMEM((5 + tracers, n + EDGE, m), F32),
         ],
     )
-    values = call(values_body, S((groups, 128), F32), (asked, mine, other), us=600.0)
+    values = call(
+        values_body,
+        S((groups, 128), F32),
+        (asked, mine, other, coef),
+        [VMEM] * 3 + [ANY],
+        us=600.0,
+    )
     got = exchange(values)
     force = call(
         force_body, strip, (asked, mine, other, values), [VMEM] * 3 + [ANY], us=600.0

time: 58.2 us -> 55.3 us (0.950)
  starting transfers between devices: 41.1 us -> 38.7 us
  local copies, waits for them, and re-layouts: 0.81 us -> 0.11 us
  waiting for transfers between devices: 3.75 us -> 4.42 us
    ppermute x6, waiting for transfers between devices: 0.28 us -> 3.5 us  [ring(): return lax.ppermute(value, axis, [(i, (i + step) % n) for i in range(n)])]
    ppermute x1, waiting for transfers between devices: 3.09 us -> 0.53 us  [shards(): other = lax.ppermute(mine, 'lev', [(0, 1), (1, 0)])]
    all_to_all x2, starting transfers between devices: 27.8 us -> 25.4 us  [exchange(): lax.all_to_all(value, ('lev', 'gx', 'gy'), 0, 0, axis_index_groups=groups...]
    unnamed x17 -> x11, local copies, waits for them, and re-layouts: 0.81 us -> 0.11 us
  transfers between devices with their start and end apart: 9 -> 9, of which waited for: 3 -> 4; matrix products, arithmetic and copies ran while one was open for 0% -> 0% of each run, Pallas kernels for 14% -> 14%
where the time goes in v5:
time: 55.3 us; the launch traced here: 55.1 us
  starting transfers between devices  38.7 us (70%)
  Pallas kernels  11.1 us (20%)
  waiting for transfers between devices  4.42 us (8%)
  between operations  0.73 us (1%)
    all_to_all x2, starting transfers between devices, exchange(): lax.all_to_all(value, ('lev', 'gx', 'gy'), 0, 0, axis_index_groups=groups...  25.4 us
    ppermute x6, starting transfers between devices, ring(): return lax.ppermute(value, axis, [(i, (i + step) % n) for i in range(n)])  13.3 us
    pallas_call x10, Pallas kernels, call(): pl.pallas_call(body, out_shape=outs, in_specs=specs or [VMEM] * len(input...  11.1 us
    ppermute x6, waiting for transfers between devices, ring(): return lax.ppermute(value, axis, [(i, (i + step) % n) for i in range(n)])  3.5 us
  transfers between devices with their start and end apart: 9, of which 4 were waited for; matrix products, arithmetic and copies ran while one was open for 0% of the time, Pallas kernels for 14%

profile of v5, /device:TPU:1, one launch (start us, length us, event | category | flops | bytes accessed | tf_op | source)
XLA Modules:
  0.0 55.1 jit_solution(6525928553360249847)
XLA Ops:
  0.6 1.3 %shard_map.103 = (f32[64,128]{1,0:T(8,128)S(1)}, f32[64,128]{1,0:T(8,128)S(1)}, f32[14,8,128]{2,1,0:T(8,128)S(1)}, f32[14,8,128]{2,1,0:T(8,128)S(1)}, s32[4,128]...) custom-call(f32[4,2,64,128]{3,2,1,0:T(8,128)} %conc.5, f32[2,64,128]{2,1,0:T(8,128)} %kk.5, ...), custom_call_target="tpu_custom_call" | custom-call | flops 1000000 | bytes 3000000 | tf_op jit(solution)/shard_map/pallas_call | solution.py:23
  2.0 2.7 %collective-permute-start = (f32[64,128]{1,0:T(8,128)S(1)}, f32[64,128]{1,0:T(8,128)S(1)}, u32[]{:S(2)}, u32[]{:S(2)}) collective-permute-start(f32[64,128]{1,0:T(8,128)S(1)} %get-tuple-element.18), channel_id=1, source_target_pairs={{0,1},{1,2},{2,3},{3,4},{4,5},{5,6},{6,7},{7,0},{8,9},{9,10},{10,1... | collective-permute-start | bytes 98312 | tf_op jit(solution)/shard_map/ppermute | solution.py:389
  4.7 0.6 %collective-permute-start.1 = (f32[64,128]{1,0:T(8,128)S(1)}, f32[64,128]{1,0:T(8,128)S(1)}, u32[]{:S(2)}, u32[]{:S(2)}) collective-permute-start(f32[64,128]{1,0:T(8,128)S(1)} %get-tuple-element.19), channel_id=1, source_target_pairs={{0,7},{1,0},{2,1},{3,2},{4,3},{5,4},{6,5},{7,6},{8,15},{9,8},{10,9... | collective-permute-start | bytes 98312 | tf_op jit(solution)/shard_map/ppermute | solution.py:389
  5.3 1.2 %shard_map.106 = (f32[128,128]{1,0:T(8,128)}, s32[4,128]{1,0:T(4,128)S(1)}) custom-call(s32[4,128]{1,0:T(4,128)S(1)} %get-tuple-element.23.owner, s32[4,128]{1,0:T(4,128)S(1)} %get-tuple-element.24.column, f32[4,128]{1,0:T(4,128)S(1)} %get-tuple-element.25.observed), custom_call_target="tpu_custom_call" | custom-call | flops 600000000 | bytes 1800000000 | tf_op jit(solution)/shard_map/pallas_call | solution.py:23
  6.5 0.0 collective-permute-done.left
  6.5 1.5 %collective-permute-done.1.right = f32[64,128]{1,0:T(8,128)S(1)} collective-permute-done((f32[64,128]{1,0:T(8,128)S(1)}, f32[64,128]{1,0:T(8,128)S(1)}, u32[]{:S(2)}, u32[]{:S(2)}) %collective-permute-start.1) | collective-permute-done | bytes 32800 | tf_op jit(solution)/shard_map/ppermute | solution.py:389
  8.0 1.7 %collective-permute-start.2 = (f32[16,8,128]{2,1,0:T(8,128)S(1)}, f32[16,8,128]{2,1,0:T(8,128)S(1)}, u32[]{:S(2)}, u32[]{:S(2)}) collective-permute-start(f32[16,8,128]{2,1,0:T(8,128)S(1)} %get-tuple-element.20), channel_id=1, source_target_pairs={{0,8},{8,16},{16,24},{24,32},{32,40},{40,48},{48,56},{56,64},{64,7... | collective-permute-start | bytes 196616 | tf_op jit(solution)/shard_map/ppermute | solution.py:389
  9.8 6.5 %collective-permute-start.3 = (f32[16,8,128]{2,1,0:T(8,128)S(1)}, f32[16,8,128]{2,1,0:T(8,128)S(1)}, u32[]{:S(2)}, u32[]{:S(2)}) collective-permute-start(f32[16,8,128]{2,1,0:T(8,128)S(1)} %get-tuple-element.21.__1_), channel_id=1, source_target_pairs={{0,120},{8,0},{16,8},{24,16},{32,24},{40,32},{48,40},{56,48},{64,5... | collective-permute-start | bytes 196616 | tf_op jit(solution)/shard_map/ppermute | solution.py:389
  16.3 0.0 copy-start.2
  16.3 11.4 %all-to-all-start = ((f32[128,1,128]{2,1,0:T(1,128)}), f32[128,1,128]{2,1,0:T(1,128)S(1)}, u32[]{:S(2)}, u32[]{:S(2)}) async-start(f32[128,1,128]{2,1,0:T(1,128)} %bitcast.4), calls=%async_computation | async-start | bytes 131072 | tf_op jit(solution)/shard_map/all_to_all | solution.py:396
  27.7 0.1 copy.15.weight
  27.8 1.3 %shard_map.108.mine = f32[72,128]{1,0:T(8,128)S(1)} custom-call(f32[4,2,64,128]{3,2,1,0:T(8,128)S(1)} %copy-done, f32[2,64,128]{2,1,0:T(8,128)S(1)} %copy-done.1, f32[2,64,128]{2,1,0:T(8,128)S(1)} %copy-done.2, f32[2,64,128]{2,1,0:T(8,128)S(1)} %copy-done.3, f32[16,8,128]{2,1,0:T(8,128)S(1)} %collective-permute-done.2.below, ...), custom_call_target="tpu_custom_call" | custom-call | flops 600000000 | bytes 1800000000 | tf_op jit(solution)/shard_map/pallas_call | solution.py:23
  29.1 0.1 collective-permute-start.4
  29.2 2.6 %shard_map.105 = (f32[4,2,64,128]{3,2,1,0:T(8,128)}, f32[2,5,2,9,8,128]{5,4,3,2,1,0:T(8,128)S(1)}) custom-call(f32[4,2,64,128]{3,2,1,0:T(8,128)S(1)} %copy-done, f32[2,64,128]{2,1,0:T(8,128)S(1)} %copy-done.1, f32[2,64,128]{2,1,0:T(8,128)S(1)} %copy-done.2, f32[2,64,128]{2,1,0:T(8,128)S(1)} %copy-done.3, f32[16,8,128]{2,1,0:T(8,128)S(1)} %collective-permute-done.2.below, ...), custom_call_target="tpu_custom_call" | custom-call | flops 600000000 | bytes 1800000000 | tf_op jit(solution)/shard_map/pallas_call | solution.py:23
  31.8 0.5 collective-permute-done.4.other
  32.3 0.4 all-to-all-done
  32.7 1.2 %shard_map.109.values = f32[128,128]{1,0:T(8,128)} custom-call(f32[128,128]{1,0:T(8,128)S(1)} %bitcast.13, f32[72,128]{1,0:T(8,128)S(1)} %shard_map.108.mine, f32[72,128]{1,0:T(8,128)S(1)} %collective-permute-done.4.other, f32[2,5,2,9,8,128]{5,4,3,2,1,0:T(8,128)S(1)} %get-tuple-element.27.coef), custom_call_target="tpu_custom_call" | custom-call | flops 600000000 | bytes 1800000000 | tf_op jit(solution)/shard_map/pallas_call | solution.py:23
  33.9 14.0 %all-to-all-start.1 = ((f32[128,1,128]{2,1,0:T(1,128)}), f32[128,1,128]{2,1,0:T(1,128)S(1)}, u32[]{:S(2)}, u32[]{:S(2)}) async-start(f32[128,1,128]{2,1,0:T(1,128)} %bitcast.7), calls=%async_computation.1 | async-start | bytes 131072 | tf_op jit(solution)/shard_map/all_to_all | solution.py:396
  47.8 1.0 %shard_map.111.force = f32[72,128]{1,0:T(8,128)S(1)} custom-call(f32[128,128]{1,0:T(8,128)S(1)} %bitcast.14, f32[72,128]{1,0:T(8,128)S(1)} %shard_map.108.mine, f32[72,128]{1,0:T(8,128)S(1)} %collective-permute-done.4.other, f32[128,128]{1,0:T(8,128)} %shard_map.109.values), custom_call_target="tpu_custom_call" | custom-call | flops 600000000 | bytes 1800000000 | tf_op jit(solution)/shard_map/pallas_call | solution.py:23
  48.8 0.2 collective-permute-start.6
  49.0 1.6 %collective-permute-start.5 = (f32[72,128]{1,0:T(8,128)S(1)}, f32[72,128]{1,0:T(8,128)S(1)}, u32[]{:S(2)}, u32[]{:S(2)}) collective-permute-start(f32[72,128]{1,0:T(8,128)S(1)} %shard_map.111.force), channel_id=1, source_target_pairs={{0,1},{1,2},{2,3},{3,4},{4,5},{5,6},{6,7},{7,0},{8,9},{9,10},{10,1... | collective-permute-start | bytes 110600 | tf_op jit(solution)/shard_map/ppermute | solution.py:389
  50.6 2.0 %collective-permute-done.6.right = f32[72,128]{1,0:T(8,128)S(1)} collective-permute-done((f32[72,128]{1,0:T(8,128)S(1)}, f32[72,128]{1,0:T(8,128)S(1)}, u32[]{:S(2)}, u32[]{:S(2)}) %collective-permute-start.6) | collective-permute-done | bytes 36896 | tf_op jit(solution)/shard_map/ppermute | solution.py:389
  52.6 1.7 %shard_map.112 = f32[4,2,64,128]{3,2,1,0:T(8,128)} custom-call(f32[72,128]{1,0:T(8,128)S(1)} %shard_map.111.force, f32[72,128]{1,0:T(8,128)S(1)} %collective-permute-done.5.left, f32[72,128]{1,0:T(8,128)S(1)} %collective-permute-done.6.right, f32[2,5,2,9,8,128]{5,4,3,2,1,0:T(8,128)S(1)} %get-tuple-element.27.coef, f32[4,2]{1,0:T(4,128)S(1)} %copy.15.weight), custom_call_target="tpu_custom_call" | custom-call | flops 600000000 | bytes 1800000000 | tf_op jit(solution)/shard_map/pallas_call | solution.py:23
  54.3 0.8 %shard_map.110 = f32[4,128]{1,0:T(4,128)} custom-call(f32[128,128]{1,0:T(8,128)S(1)} %bitcast.12, s32[4,128]{1,0:T(4,128)S(1)} %get-tuple-element.23.owner, s32[4,128]{1,0:T(4,128)S(1)} %get-tuple-element.28.rank), custom_call_target="tpu_custom_call" | custom-call | flops 1000000 | bytes 3000000 | tf_op jit(solution)/shard_map/pallas_call | solution.py:23
  (15 shorter events, 0.0 us)
Async XLA Ops:
  2.0 4.5 %collective-permute-start = (f32[64,128]{1,0:T(8,128)S(1)}, f32[64,128]{1,0:T(8,128)S(1)}, u32[]{:S(2)}, u32[]{:S(2)}) collective-permute-start(f32[64,128]{1,0:T(8,128)S(1)} %get-tuple-element.18), channel_id=1, source_target_pairs={{0,1},{1,2},{2,3},{3,4},{4,5},{5,6},{6,7},{7,0},{8,9},{9,10},{10,1... | collective-permute-start | bytes 98312 | tf_op jit(solution)/shard_map/ppermute | solution.py:389
  4.7 3.3 %collective-permute-start.1 = (f32[64,128]{1,0:T(8,128)S(1)}, f32[64,128]{1,0:T(8,128)S(1)}, u32[]{:S(2)}, u32[]{:S(2)}) collective-permute-start(f32[64,128]{1,0:T(8,128)S(1)} %get-tuple-element.19), channel_id=1, source_target_pairs={{0,7},{1,0},{2,1},{3,2},{4,3},{5,4},{6,5},{7,6},{8,15},{9,8},{10,9... | collective-permute-start | bytes 98312 | tf_op jit(solution)/shard_map/ppermute | solution.py:389
  8.0 19.8 %collective-permute-start.2 = (f32[16,8,128]{2,1,0:T(8,128)S(1)}, f32[16,8,128]{2,1,0:T(8,128)S(1)}, u32[]{:S(2)}, u32[]{:S(2)}) collective-permute-start(f32[16,8,128]{2,1,0:T(8,128)S(1)} %get-tuple-element.20), channel_id=1, source_target_pairs={{0,8},{8,16},{16,24},{24,32},{32,40},{40,48},{48,56},{56,64},{64,7... | collective-permute-start | bytes 196616 | tf_op jit(solution)/shard_map/ppermute | solution.py:389
  9.8 18.0 %collective-permute-start.3 = (f32[16,8,128]{2,1,0:T(8,128)S(1)}, f32[16,8,128]{2,1,0:T(8,128)S(1)}, u32[]{:S(2)}, u32[]{:S(2)}) collective-permute-start(f32[16,8,128]{2,1,0:T(8,128)S(1)} %get-tuple-element.21.__1_), channel_id=1, source_target_pairs={{0,120},{8,0},{16,8},{24,16},{32,24},{40,32},{48,40},{56,48},{64,5... | collective-permute-start | bytes 196616 | tf_op jit(solution)/shard_map/ppermute | solution.py:389
  16.2 11.4 %copy-start.4 = (f32[4,2]{0,1:T(2,128)S(1)}, f32[4,2]{0,1:T(2,128)}, u32[]{:S(2)}) copy-start(f32[4,2]{0,1:T(2,128)} %param.12) | copy-start | bytes 100
  16.2 11.6 %copy-start = (f32[4,2,64,128]{3,2,1,0:T(8,128)S(1)}, f32[4,2,64,128]{3,2,1,0:T(8,128)}, u32[]{:S(2)}) copy-start(f32[4,2,64,128]{3,2,1,0:T(8,128)} %conc.5) | copy-start | bytes 786436
  16.2 11.6 %copy-start.3 = (f32[2,64,128]{2,1,0:T(8,128)S(1)}, f32[2,64,128]{2,1,0:T(8,128)}, u32[]{:S(2)}) copy-start(f32[2,64,128]{2,1,0:T(8,128)} %vv.5) | copy-start | bytes 196612
  16.2 11.6 %copy-start.1 = (f32[2,64,128]{2,1,0:T(8,128)S(1)}, f32[2,64,128]{2,1,0:T(8,128)}, u32[]{:S(2)}) copy-start(f32[2,64,128]{2,1,0:T(8,128)} %kk.5) | copy-start | bytes 196612
  16.3 11.6 %copy-start.2 = (f32[2,64,128]{2,1,0:T(8,128)S(1)}, f32[2,64,128]{2,1,0:T(8,128)}, u32[]{:S(2)}) copy-start(f32[2,64,128]{2,1,0:T(8,128)} %uu.5) | copy-start | bytes 196612
  16.3 16.4 %all-to-all-start = ((f32[128,1,128]{2,1,0:T(1,128)}), f32[128,1,128]{2,1,0:T(1,128)S(1)}, u32[]{:S(2)}, u32[]{:S(2)}) async-start(f32[128,1,128]{2,1,0:T(1,128)} %bitcast.4), calls=%async_computation | async-start | bytes 131072 | tf_op jit(solution)/shard_map/all_to_all | solution.py:396
  29.1 3.2 %collective-permute-start.4 = (f32[72,128]{1,0:T(8,128)S(1)}, f32[72,128]{1,0:T(8,128)S(1)}, u32[]{:S(2)}, u32[]{:S(2)}) collective-permute-start(f32[72,128]{1,0:T(8,128)S(1)} %shard_map.108.mine), channel_id=1, source_target_pairs={{0,128},{128,0},{1,129},{129,1},{2,130},{130,2},{3,131},{131,3},{4... | collective-permute-start | bytes 110600 | tf_op jit(solution)/shard_map/ppermute | solution.py:446
  33.9 20.4 %all-to-all-start.1 = ((f32[128,1,128]{2,1,0:T(1,128)}), f32[128,1,128]{2,1,0:T(1,128)S(1)}, u32[]{:S(2)}, u32[]{:S(2)}) async-start(f32[128,1,128]{2,1,0:T(1,128)} %bitcast.7), calls=%async_computation.1 | async-start | bytes 131072 | tf_op jit(solution)/shard_map/all_to_all | solution.py:396
  48.8 3.8 %collective-permute-start.6 = (f32[72,128]{1,0:T(8,128)S(1)}, f32[72,128]{1,0:T(8,128)S(1)}, u32[]{:S(2)}, u32[]{:S(2)}) collective-permute-start(f32[72,128]{1,0:T(8,128)S(1)} %shard_map.111.force), channel_id=1, source_target_pairs={{0,7},{1,0},{2,1},{3,2},{4,3},{5,4},{6,5},{7,6},{8,15},{9,8},{10,9... | collective-permute-start | bytes 110600 | tf_op jit(solution)/shard_map/ppermute | solution.py:389
  49.0 3.6 %collective-permute-start.5 = (f32[72,128]{1,0:T(8,128)S(1)}, f32[72,128]{1,0:T(8,128)S(1)}, u32[]{:S(2)}, u32[]{:S(2)}) collective-permute-start(f32[72,128]{1,0:T(8,128)S(1)} %shard_map.111.force), channel_id=1, source_target_pairs={{0,1},{1,2},{2,3},{3,4},{4,5},{5,6},{6,7},{7,0},{8,9},{9,10},{10,1... | collective-permute-start | bytes 110600 | tf_op jit(solution)/shard_map/ppermute | solution.py:389

commit v6 on v5

--- a/solution.py
+++ b/solution.py
@@ -56,7 +56,7 @@
 
 def tile_at(t, groups):
     for shift in (3, 4, 3):
-        t = (t * 109 + 55) & (groups - 1)
+        t = (t * 45 + 3) & (groups - 1)
         t = t ^ (t >> shift)
     return t
 
@@ -294,17 +294,14 @@
 def slots(code, first, n, m):
     where = code.astype(jnp.int32) - 1
     x, y = (where >> (m.bit_length() - 1)) - first, where & (m - 1)
-    xs, ys = [], []
-    for s in range(CAP):
-        xs.append((iota((n, x.shape[1]), 0) == x[s : s + 1, :]).astype(F32))
-        ys.append((iota((m, x.shape[1]), 0) == y[s : s + 1, :]).astype(F32).astype(BF16))
-    return xs, ys
+    xs = [(iota((n, m), 0) == x[s : s + 1, :]).astype(F32) for s in range(CAP)]
+    ys = [(iota((m, m), 0) == y[s : s + 1, :]).astype(F32).astype(BF16) for s in range(CAP)]
+    return xs, jnp.concatenate(ys, axis=1)
 
 
 def force_body(asked, mine, other, values, force):
     n, m = mine.shape[0] - EDGE, mine.shape[1]
     t = asked[...].T
-    sums = jnp.zeros((4 * n, m), F32)
     rims = jnp.zeros((4 * EDGE, m), F32)
     for i in range(3):
         part = t[2 * CAP * i : 2 * CAP * (i + 1)]
@@ -316,13 +313,15 @@
             rim = iota((EDGE, m), 0)
             keep = ((rim < HALO) if i == 1 else (rim >= HALO)).astype(F32)
             xs = [x * keep for x in xs]
-        for s in range(CAP):
-            lhs = [xs[s]] + [xs[s] * o[s : s + 1, :] for o in obs]
-            got = nt(jnp.concatenate(lhs, axis=0).astype(BF16), ys[s])
-            if i == 0:
-                sums = sums + got
-            else:
-                rims = rims + got
+        lhs = [
+            jnp.concatenate([x] + [x * o[s : s + 1, :] for o in obs], axis=0).astype(BF16)
+            for s, x in enumerate(xs)
+        ]
+        got = nt(jnp.concatenate(lhs, axis=1), ys)
+        if i == 0:
+            sums = got
+        else:
+            rims = rims + got
     for at, rows, tall in ((0, n, sums), (n, EDGE, rims)):
         count = tall[:rows]
         seen = tall[rows : 2 * rows] + tall[2 * rows : 3 * rows] + tall[3 * rows :]
@@ -336,11 +335,11 @@
     t = asked[...].T
     xs, ys = slots(t[:CAP], 0, n, m)
     fields = jnp.concatenate(split3(field), axis=0)
-    picked = []
-    for s in range(CAP):
-        z = nn(fields, ys[s])
-        z = (z[:n] + z[n : 2 * n] + z[2 * n :]) * xs[s]
-        picked.append(jnp.sum(z, axis=0, keepdims=True))
+    got = nn(fields, ys)
+    got = got[:n] + got[n : 2 * n] + got[2 * n :]
+    picked = [
+        jnp.sum(got[:, m * s : m * (s + 1)] * xs[s], axis=0, keepdims=True) for s in range(CAP)
+    ]
     picked.append(jnp.zeros((t.shape[0] - CAP, t.shape[1]), F32))
     values[...] = jnp.concatenate(picked, axis=0).T
 
@@ -350,12 +349,13 @@
     t = got[...].T[:CAP]
     parts = jnp.concatenate(split3(t), axis=0)
     who = tile_at(iota((groups, lanes), 0), groups)
+    hot = [(who == owner[j : j + 1, :]).astype(F32).astype(BF16) for j in range(rows)]
+    z = nn(parts, jnp.concatenate(hot, axis=1))
+    z = z[:CAP] + z[CAP : 2 * CAP] + z[2 * CAP :]
     for j in range(rows):
-        onehot = (who == owner[j : j + 1, :]).astype(F32)
-        z = nn(parts, onehot.astype(BF16))
-        z = z[:CAP] + z[CAP : 2 * CAP] + z[2 * CAP :]
         slot = iota((CAP, lanes), 0) == rank[j : j + 1, :]
-        out[j : j + 1, :] = jnp.sum(jnp.where(slot, z, 0.0), axis=0, keepdims=True)
+        mine = z[:, lanes * j : lanes * (j + 1)]
+        out[j : j + 1, :] = jnp.sum(jnp.where(slot, mine, 0.0), axis=0, keepdims=True)
 
 
 def adjoint_body(force, left, right, coef, weight, out, state, nat):

time: 55.3 us -> 53.7 us (0.971)
  starting transfers between devices: 38.7 us -> 36.6 us
  waiting for transfers between devices: 4.42 us -> 5.15 us
    all_to_all x2, starting transfers between devices: 25.4 us -> 23.2 us  [exchange(): lax.all_to_all(value, ('lev', 'gx', 'gy'), 0, 0, axis_index_groups=groups...]
    all_to_all x2, waiting for transfers between devices: 0.38 us -> 1.14 us  [exchange(): lax.all_to_all(value, ('lev', 'gx', 'gy'), 0, 0, axis_index_groups=groups...]
where the time goes in v6:
time: 53.7 us; the launch traced here: 53.5 us
  starting transfers between devices  36.6 us (68%)
  Pallas kernels  10.9 us (20%)
  waiting for transfers between devices  5.15 us (10%)
  between operations  0.73 us (1%)
    all_to_all x2, starting transfers between devices, exchange(): lax.all_to_all(value, ('lev', 'gx', 'gy'), 0, 0, axis_index_groups=groups...  23.2 us
    ppermute x6, starting transfers between devices, ring(): return lax.ppermute(value, axis, [(i, (i + step) % n) for i in range(n)])  13.2 us
    pallas_call x10, Pallas kernels, call(): pl.pallas_call(body, out_shape=outs, in_specs=specs or [VMEM] * len(input...  10.9 us
    ppermute x6, waiting for transfers between devices, ring(): return lax.ppermute(value, axis, [(i, (i + step) % n) for i in range(n)])  3.47 us
    all_to_all x2, waiting for transfers between devices, exchange(): lax.all_to_all(value, ('lev', 'gx', 'gy'), 0, 0, axis_index_groups=groups...  1.14 us
  transfers between devices with their start and end apart: 9, of which 4 were waited for; matrix products, arithmetic and copies ran while one was open for 0% of the time, Pallas kernels for 14%

profile of v6, /device:TPU:1, one launch (start us, length us, event | category | flops | bytes accessed | tf_op | source)
XLA Modules:
  0.0 53.5 jit_solution(14448283219775784843)
XLA Ops:
  0.6 1.3 %shard_map.103 = (f32[64,128]{1,0:T(8,128)S(1)}, f32[64,128]{1,0:T(8,128)S(1)}, f32[14,8,128]{2,1,0:T(8,128)S(1)}, f32[14,8,128]{2,1,0:T(8,128)S(1)}, s32[4,128]...) custom-call(f32[4,2,64,128]{3,2,1,0:T(8,128)} %conc.5, f32[2,64,128]{2,1,0:T(8,128)} %kk.5, ...), custom_call_target="tpu_custom_call" | custom-call | flops 1000000 | bytes 3000000 | tf_op jit(solution)/shard_map/pallas_call | solution.py:23
  2.0 2.7 %collective-permute-start = (f32[64,128]{1,0:T(8,128)S(1)}, f32[64,128]{1,0:T(8,128)S(1)}, u32[]{:S(2)}, u32[]{:S(2)}) collective-permute-start(f32[64,128]{1,0:T(8,128)S(1)} %get-tuple-element.18), channel_id=1, source_target_pairs={{0,1},{1,2},{2,3},{3,4},{4,5},{5,6},{6,7},{7,0},{8,9},{9,10},{10,1... | collective-permute-start | bytes 98312 | tf_op jit(solution)/shard_map/ppermute | solution.py:389
  4.7 0.6 %collective-permute-start.1 = (f32[64,128]{1,0:T(8,128)S(1)}, f32[64,128]{1,0:T(8,128)S(1)}, u32[]{:S(2)}, u32[]{:S(2)}) collective-permute-start(f32[64,128]{1,0:T(8,128)S(1)} %get-tuple-element.19), channel_id=1, source_target_pairs={{0,7},{1,0},{2,1},{3,2},{4,3},{5,4},{6,5},{7,6},{8,15},{9,8},{10,9... | collective-permute-start | bytes 98312 | tf_op jit(solution)/shard_map/ppermute | solution.py:389
  5.3 1.2 %shard_map.106 = (f32[128,128]{1,0:T(8,128)}, s32[4,128]{1,0:T(4,128)S(1)}) custom-call(s32[4,128]{1,0:T(4,128)S(1)} %get-tuple-element.23.owner, s32[4,128]{1,0:T(4,128)S(1)} %get-tuple-element.24.column, f32[4,128]{1,0:T(4,128)S(1)} %get-tuple-element.25.observed), custom_call_target="tpu_custom_call" | custom-call | flops 600000000 | bytes 1800000000 | tf_op jit(solution)/shard_map/pallas_call | solution.py:23
  6.5 0.0 collective-permute-done.left
  6.5 1.5 %collective-permute-done.1.right = f32[64,128]{1,0:T(8,128)S(1)} collective-permute-done((f32[64,128]{1,0:T(8,128)S(1)}, f32[64,128]{1,0:T(8,128)S(1)}, u32[]{:S(2)}, u32[]{:S(2)}) %collective-permute-start.1) | collective-permute-done | bytes 32800 | tf_op jit(solution)/shard_map/ppermute | solution.py:389
  8.0 1.7 %collective-permute-start.2 = (f32[16,8,128]{2,1,0:T(8,128)S(1)}, f32[16,8,128]{2,1,0:T(8,128)S(1)}, u32[]{:S(2)}, u32[]{:S(2)}) collective-permute-start(f32[16,8,128]{2,1,0:T(8,128)S(1)} %get-tuple-element.20), channel_id=1, source_target_pairs={{0,8},{8,16},{16,24},{24,32},{32,40},{40,48},{48,56},{56,64},{64,7... | collective-permute-start | bytes 196616 | tf_op jit(solution)/shard_map/ppermute | solution.py:389
  9.8 6.5 %collective-permute-start.3 = (f32[16,8,128]{2,1,0:T(8,128)S(1)}, f32[16,8,128]{2,1,0:T(8,128)S(1)}, u32[]{:S(2)}, u32[]{:S(2)}) collective-permute-start(f32[16,8,128]{2,1,0:T(8,128)S(1)} %get-tuple-element.21.__1_), channel_id=1, source_target_pairs={{0,120},{8,0},{16,8},{24,16},{32,24},{40,32},{48,40},{56,48},{64,5... | collective-permute-start | bytes 196616 | tf_op jit(solution)/shard_map/ppermute | solution.py:389
  16.3 0.0 copy-start.2
  16.3 10.5 %all-to-all-start = ((f32[128,1,128]{2,1,0:T(1,128)}), f32[128,1,128]{2,1,0:T(1,128)S(1)}, u32[]{:S(2)}, u32[]{:S(2)}) async-start(f32[128,1,128]{2,1,0:T(1,128)} %bitcast.4), calls=%async_computation | async-start | bytes 131072 | tf_op jit(solution)/shard_map/all_to_all | solution.py:396
  26.7 0.1 copy.15.weight
  26.9 1.3 %shard_map.108.mine = f32[72,128]{1,0:T(8,128)S(1)} custom-call(f32[4,2,64,128]{3,2,1,0:T(8,128)S(1)} %copy-done, f32[2,64,128]{2,1,0:T(8,128)S(1)} %copy-done.1, f32[2,64,128]{2,1,0:T(8,128)S(1)} %copy-done.2, f32[2,64,128]{2,1,0:T(8,128)S(1)} %copy-done.3, f32[16,8,128]{2,1,0:T(8,128)S(1)} %collective-permute-done.2.below, ...), custom_call_target="tpu_custom_call" | custom-call | flops 600000000 | bytes 1800000000 | tf_op jit(solution)/shard_map/pallas_call | solution.py:23
  28.2 0.1 collective-permute-start.4
  28.3 2.6 %shard_map.105 = (f32[4,2,64,128]{3,2,1,0:T(8,128)}, f32[2,5,2,9,8,128]{5,4,3,2,1,0:T(8,128)S(1)}) custom-call(f32[4,2,64,128]{3,2,1,0:T(8,128)S(1)} %copy-done, f32[2,64,128]{2,1,0:T(8,128)S(1)} %copy-done.1, f32[2,64,128]{2,1,0:T(8,128)S(1)} %copy-done.2, f32[2,64,128]{2,1,0:T(8,128)S(1)} %copy-done.3, f32[16,8,128]{2,1,0:T(8,128)S(1)} %collective-permute-done.2.below, ...), custom_call_target="tpu_custom_call" | custom-call | flops 600000000 | bytes 1800000000 | tf_op jit(solution)/shard_map/pallas_call | solution.py:23
  30.8 0.5 %collective-permute-done.4.other = f32[72,128]{1,0:T(8,128)S(1)} collective-permute-done((f32[72,128]{1,0:T(8,128)S(1)}, f32[72,128]{1,0:T(8,128)S(1)}, u32[]{:S(2)}, u32[]{:S(2)}) %collective-permute-start.4) | collective-permute-done | bytes 36896 | tf_op jit(solution)/shard_map/ppermute | solution.py:446
  31.4 1.1 %all-to-all-done = f32[128,1,128]{2,1,0:T(1,128)S(1)} async-done(((f32[128,1,128]{2,1,0:T(1,128)}), f32[128,1,128]{2,1,0:T(1,128)S(1)}, u32[]{:S(2)}, u32[]{:S(2)}) %all-to-all-start) | async-done | bytes 65568 | tf_op jit(solution)/shard_map/all_to_all | solution.py:396
  32.5 1.2 %shard_map.109.values = f32[128,128]{1,0:T(8,128)} custom-call(f32[128,128]{1,0:T(8,128)S(1)} %bitcast.13, f32[72,128]{1,0:T(8,128)S(1)} %shard_map.108.mine, f32[72,128]{1,0:T(8,128)S(1)} %collective-permute-done.4.other, f32[2,5,2,9,8,128]{5,4,3,2,1,0:T(8,128)S(1)} %get-tuple-element.27.coef), custom_call_target="tpu_custom_call" | custom-call | flops 600000000 | bytes 1800000000 | tf_op jit(solution)/shard_map/pallas_call | solution.py:23
  33.7 12.8 %all-to-all-start.1 = ((f32[128,1,128]{2,1,0:T(1,128)}), f32[128,1,128]{2,1,0:T(1,128)S(1)}, u32[]{:S(2)}, u32[]{:S(2)}) async-start(f32[128,1,128]{2,1,0:T(1,128)} %bitcast.7), calls=%async_computation.1 | async-start | bytes 131072 | tf_op jit(solution)/shard_map/all_to_all | solution.py:396
  46.5 0.8 %shard_map.111.force = f32[72,128]{1,0:T(8,128)S(1)} custom-call(f32[128,128]{1,0:T(8,128)S(1)} %bitcast.14, f32[72,128]{1,0:T(8,128)S(1)} %shard_map.108.mine, f32[72,128]{1,0:T(8,128)S(1)} %collective-permute-done.4.other, f32[128,128]{1,0:T(8,128)} %shard_map.109.values), custom_call_target="tpu_custom_call" | custom-call | flops 600000000 | bytes 1800000000 | tf_op jit(solution)/shard_map/pallas_call | solution.py:23
  47.3 0.0 collective-permute-start.6
  47.3 1.7 %collective-permute-start.5 = (f32[72,128]{1,0:T(8,128)S(1)}, f32[72,128]{1,0:T(8,128)S(1)}, u32[]{:S(2)}, u32[]{:S(2)}) collective-permute-start(f32[72,128]{1,0:T(8,128)S(1)} %shard_map.111.force), channel_id=1, source_target_pairs={{0,1},{1,2},{2,3},{3,4},{4,5},{5,6},{6,7},{7,0},{8,9},{9,10},{10,1... | collective-permute-start | bytes 110600 | tf_op jit(solution)/shard_map/ppermute | solution.py:389
  49.0 2.0 %collective-permute-done.6.right = f32[72,128]{1,0:T(8,128)S(1)} collective-permute-done((f32[72,128]{1,0:T(8,128)S(1)}, f32[72,128]{1,0:T(8,128)S(1)}, u32[]{:S(2)}, u32[]{:S(2)}) %collective-permute-start.6) | collective-permute-done | bytes 36896 | tf_op jit(solution)/shard_map/ppermute | solution.py:389
  51.0 1.7 %shard_map.112 = f32[4,2,64,128]{3,2,1,0:T(8,128)} custom-call(f32[72,128]{1,0:T(8,128)S(1)} %shard_map.111.force, f32[72,128]{1,0:T(8,128)S(1)} %collective-permute-done.5.left, f32[72,128]{1,0:T(8,128)S(1)} %collective-permute-done.6.right, f32[2,5,2,9,8,128]{5,4,3,2,1,0:T(8,128)S(1)} %get-tuple-element.27.coef, f32[4,2]{1,0:T(4,128)S(1)} %copy.15.weight), custom_call_target="tpu_custom_call" | custom-call | flops 600000000 | bytes 1800000000 | tf_op jit(solution)/shard_map/pallas_call | solution.py:23
  52.7 0.8 %shard_map.110 = f32[4,128]{1,0:T(4,128)} custom-call(f32[128,128]{1,0:T(8,128)S(1)} %bitcast.12, s32[4,128]{1,0:T(4,128)S(1)} %get-tuple-element.23.owner, s32[4,128]{1,0:T(4,128)S(1)} %get-tuple-element.28.rank), custom_call_target="tpu_custom_call" | custom-call | flops 1000000 | bytes 3000000 | tf_op jit(solution)/shard_map/pallas_call | solution.py:23
  (15 shorter events, 0.0 us)
Async XLA Ops:
  2.0 4.5 %collective-permute-start = (f32[64,128]{1,0:T(8,128)S(1)}, f32[64,128]{1,0:T(8,128)S(1)}, u32[]{:S(2)}, u32[]{:S(2)}) collective-permute-start(f32[64,128]{1,0:T(8,128)S(1)} %get-tuple-element.18), channel_id=1, source_target_pairs={{0,1},{1,2},{2,3},{3,4},{4,5},{5,6},{6,7},{7,0},{8,9},{9,10},{10,1... | collective-permute-start | bytes 98312 | tf_op jit(solution)/shard_map/ppermute | solution.py:389
  4.7 3.3 %collective-permute-start.1 = (f32[64,128]{1,0:T(8,128)S(1)}, f32[64,128]{1,0:T(8,128)S(1)}, u32[]{:S(2)}, u32[]{:S(2)}) collective-permute-start(f32[64,128]{1,0:T(8,128)S(1)} %get-tuple-element.19), channel_id=1, source_target_pairs={{0,7},{1,0},{2,1},{3,2},{4,3},{5,4},{6,5},{7,6},{8,15},{9,8},{10,9... | collective-permute-start | bytes 98312 | tf_op jit(solution)/shard_map/ppermute | solution.py:389
  8.0 18.8 %collective-permute-start.2 = (f32[16,8,128]{2,1,0:T(8,128)S(1)}, f32[16,8,128]{2,1,0:T(8,128)S(1)}, u32[]{:S(2)}, u32[]{:S(2)}) collective-permute-start(f32[16,8,128]{2,1,0:T(8,128)S(1)} %get-tuple-element.20), channel_id=1, source_target_pairs={{0,8},{8,16},{16,24},{24,32},{32,40},{40,48},{48,56},{56,64},{64,7... | collective-permute-start | bytes 196616 | tf_op jit(solution)/shard_map/ppermute | solution.py:389
  9.8 17.1 %collective-permute-start.3 = (f32[16,8,128]{2,1,0:T(8,128)S(1)}, f32[16,8,128]{2,1,0:T(8,128)S(1)}, u32[]{:S(2)}, u32[]{:S(2)}) collective-permute-start(f32[16,8,128]{2,1,0:T(8,128)S(1)} %get-tuple-element.21.__1_), channel_id=1, source_target_pairs={{0,120},{8,0},{16,8},{24,16},{32,24},{40,32},{48,40},{56,48},{64,5... | collective-permute-start | bytes 196616 | tf_op jit(solution)/shard_map/ppermute | solution.py:389
  16.2 10.5 %copy-start.4 = (f32[4,2]{0,1:T(2,128)S(1)}, f32[4,2]{0,1:T(2,128)}, u32[]{:S(2)}) copy-start(f32[4,2]{0,1:T(2,128)} %param.12) | copy-start | bytes 100
  16.2 10.6 %copy-start = (f32[4,2,64,128]{3,2,1,0:T(8,128)S(1)}, f32[4,2,64,128]{3,2,1,0:T(8,128)}, u32[]{:S(2)}) copy-start(f32[4,2,64,128]{3,2,1,0:T(8,128)} %conc.5) | copy-start | bytes 786436
  16.2 10.6 %copy-start.3 = (f32[2,64,128]{2,1,0:T(8,128)S(1)}, f32[2,64,128]{2,1,0:T(8,128)}, u32[]{:S(2)}) copy-start(f32[2,64,128]{2,1,0:T(8,128)} %vv.5) | copy-start | bytes 196612
  16.2 10.6 %copy-start.1 = (f32[2,64,128]{2,1,0:T(8,128)S(1)}, f32[2,64,128]{2,1,0:T(8,128)}, u32[]{:S(2)}) copy-start(f32[2,64,128]{2,1,0:T(8,128)} %kk.5) | copy-start | bytes 196612
  16.3 10.6 %copy-start.2 = (f32[2,64,128]{2,1,0:T(8,128)S(1)}, f32[2,64,128]{2,1,0:T(8,128)}, u32[]{:S(2)}) copy-start(f32[2,64,128]{2,1,0:T(8,128)} %uu.5) | copy-start | bytes 196612
  16.3 16.3 %all-to-all-start = ((f32[128,1,128]{2,1,0:T(1,128)}), f32[128,1,128]{2,1,0:T(1,128)S(1)}, u32[]{:S(2)}, u32[]{:S(2)}) async-start(f32[128,1,128]{2,1,0:T(1,128)} %bitcast.4), calls=%async_computation | async-start | bytes 131072 | tf_op jit(solution)/shard_map/all_to_all | solution.py:396
  28.2 3.2 %collective-permute-start.4 = (f32[72,128]{1,0:T(8,128)S(1)}, f32[72,128]{1,0:T(8,128)S(1)}, u32[]{:S(2)}, u32[]{:S(2)}) collective-permute-start(f32[72,128]{1,0:T(8,128)S(1)} %shard_map.108.mine), channel_id=1, source_target_pairs={{0,128},{128,0},{1,129},{129,1},{2,130},{130,2},{3,131},{131,3},{4... | collective-permute-start | bytes 110600 | tf_op jit(solution)/shard_map/ppermute | solution.py:446
  33.7 19.0 %all-to-all-start.1 = ((f32[128,1,128]{2,1,0:T(1,128)}), f32[128,1,128]{2,1,0:T(1,128)S(1)}, u32[]{:S(2)}, u32[]{:S(2)}) async-start(f32[128,1,128]{2,1,0:T(1,128)} %bitcast.7), calls=%async_computation.1 | async-start | bytes 131072 | tf_op jit(solution)/shard_map/all_to_all | solution.py:396
  47.3 3.7 %collective-permute-start.6 = (f32[72,128]{1,0:T(8,128)S(1)}, f32[72,128]{1,0:T(8,128)S(1)}, u32[]{:S(2)}, u32[]{:S(2)}) collective-permute-start(f32[72,128]{1,0:T(8,128)S(1)} %shard_map.111.force), channel_id=1, source_target_pairs={{0,7},{1,0},{2,1},{3,2},{4,3},{5,4},{6,5},{7,6},{8,15},{9,8},{10,9... | collective-permute-start | bytes 110600 | tf_op jit(solution)/shard_map/ppermute | solution.py:389
  47.3 3.7 %collective-permute-start.5 = (f32[72,128]{1,0:T(8,128)S(1)}, f32[72,128]{1,0:T(8,128)S(1)}, u32[]{:S(2)}, u32[]{:S(2)}) collective-permute-start(f32[72,128]{1,0:T(8,128)S(1)} %shard_map.111.force), channel_id=1, source_target_pairs={{0,1},{1,2},{2,3},{3,4},{4,5},{5,6},{6,7},{7,0},{8,9},{9,10},{10,1... | collective-permute-start | bytes 110600 | tf_op jit(solution)/shard_map/ppermute | solution.py:389

commit v7 on v6

--- a/solution.py
+++ b/solution.py
@@ -358,7 +358,7 @@
         out[j : j + 1, :] = jnp.sum(jnp.where(slot, mine, 0.0), axis=0, keepdims=True)
 
 
-def adjoint_body(force, left, right, coef, weight, out, state, nat):
+def adjoint_body(force, left, right, coef, weight, model, out, state, nat):
     keep_l, keep_r = inside("gy")
     n, m = out.shape[2], out.shape[3]
     at = iota((EDGE, m), 1)
@@ -466,19 +466,22 @@
         force_body, strip, (asked, mine, other, values), [VMEM] * 3 + [ANY], us=600.0
     )
     left, right = ring(force, "gy", 1), ring(force, "gy", -1)
+    model = call(
+        functools.partial(answer_body, groups),
+        S(owner.shape, F32),
+        (got, owner, rank),
+        us=600.0,
+    )
     gradient = call(
         adjoint_body,
         S(conc.shape, F32),
-        (force, left, right, coef, weight),
-        [VMEM] * 4 + [SMEM],
+        (force, left, right, coef, weight, pltpu.with_memory_space_constraint(model, pltpu.HBM)),
+        [VMEM] * 4 + [SMEM, HBM],
         us=600.0,
         scratch=[
             pltpu.VMEM((2, levels, 2, some, EDGE, m), F32),
             pltpu.VMEM((3 + levels, n + EDGE, m), F32),
         ],
-    )
-    model = call(
-        functools.partial(answer_body, groups), S(owner.shape, F32), (got, owner, rank)
     )
     return (forecast, model.reshape(-1), gradient)
 

time: 53.7 us -> 54.9 us (1.022)
  waiting for transfers between devices: 5.15 us -> 6.46 us
    all_to_all x2, waiting for transfers between devices: 1.14 us -> 4.37 us  [exchange(): lax.all_to_all(value, ('lev', 'gx', 'gy'), 0, 0, axis_index_groups=groups...]
    ppermute x6, waiting for transfers between devices: 3.47 us -> 1.52 us  [ring(): return lax.ppermute(value, axis, [(i, (i + step) % n) for i in range(n)])]
  transfers between devices with their start and end apart: 9 -> 9, of which waited for: 4 -> 4; matrix products, arithmetic and copies ran while one was open for 0% -> 0% of each run, Pallas kernels for 14% -> 12%
where the time goes in v7:
time: 54.9 us; the launch traced here: 54.7 us
  starting transfers between devices  36.6 us (67%)
  Pallas kernels  10.9 us (20%)
  waiting for transfers between devices  6.46 us (12%)
  between operations  0.73 us (1%)
    all_to_all x2, starting transfers between devices, exchange(): lax.all_to_all(value, ('lev', 'gx', 'gy'), 0, 0, axis_index_groups=groups...  23.2 us
    ppermute x6, starting transfers between devices, ring(): return lax.ppermute(value, axis, [(i, (i + step) % n) for i in range(n)])  13.2 us
    pallas_call x10, Pallas kernels, call(): pl.pallas_call(body, out_shape=outs, in_specs=specs or [VMEM] * len(input...  10.9 us
    all_to_all x2, waiting for transfers between devices, exchange(): lax.all_to_all(value, ('lev', 'gx', 'gy'), 0, 0, axis_index_groups=groups...  4.37 us
    ppermute x6, waiting for transfers between devices, ring(): return lax.ppermute(value, axis, [(i, (i + step) % n) for i in range(n)])  1.52 us
  transfers between devices with their start and end apart: 9, of which 4 were waited for; matrix products, arithmetic and copies ran while one was open for 0% of the time, Pallas kernels for 12%

profile of v7, /device:TPU:1, one launch (start us, length us, event | category | flops | bytes accessed | tf_op | source)
XLA Modules:
  0.0 54.7 jit_solution(1738571359518394671)
XLA Ops:
  0.6 1.3 %shard_map.103 = (f32[64,128]{1,0:T(8,128)S(1)}, f32[64,128]{1,0:T(8,128)S(1)}, f32[14,8,128]{2,1,0:T(8,128)S(1)}, f32[14,8,128]{2,1,0:T(8,128)S(1)}, s32[4,128]...) custom-call(f32[4,2,64,128]{3,2,1,0:T(8,128)} %conc.5, f32[2,64,128]{2,1,0:T(8,128)} %kk.5, ...), custom_call_target="tpu_custom_call" | custom-call | flops 1000000 | bytes 3000000 | tf_op jit(solution)/shard_map/pallas_call | solution.py:23
  2.0 2.7 %collective-permute-start = (f32[64,128]{1,0:T(8,128)S(1)}, f32[64,128]{1,0:T(8,128)S(1)}, u32[]{:S(2)}, u32[]{:S(2)}) collective-permute-start(f32[64,128]{1,0:T(8,128)S(1)} %get-tuple-element.18), channel_id=1, source_target_pairs={{0,1},{1,2},{2,3},{3,4},{4,5},{5,6},{6,7},{7,0},{8,9},{9,10},{10,1... | collective-permute-start | bytes 98312 | tf_op jit(solution)/shard_map/ppermute | solution.py:389
  4.7 0.6 %collective-permute-start.1 = (f32[64,128]{1,0:T(8,128)S(1)}, f32[64,128]{1,0:T(8,128)S(1)}, u32[]{:S(2)}, u32[]{:S(2)}) collective-permute-start(f32[64,128]{1,0:T(8,128)S(1)} %get-tuple-element.19), channel_id=1, source_target_pairs={{0,7},{1,0},{2,1},{3,2},{4,3},{5,4},{6,5},{7,6},{8,15},{9,8},{10,9... | collective-permute-start | bytes 98312 | tf_op jit(solution)/shard_map/ppermute | solution.py:389
  5.3 1.2 %shard_map.106 = (f32[128,128]{1,0:T(8,128)}, s32[4,128]{1,0:T(4,128)S(1)}) custom-call(s32[4,128]{1,0:T(4,128)S(1)} %get-tuple-element.23.owner, s32[4,128]{1,0:T(4,128)S(1)} %get-tuple-element.24.column, f32[4,128]{1,0:T(4,128)S(1)} %get-tuple-element.25.observed), custom_call_target="tpu_custom_call" | custom-call | flops 600000000 | bytes 1800000000 | tf_op jit(solution)/shard_map/pallas_call | solution.py:23
  6.5 0.0 collective-permute-done.left
  6.5 1.5 %collective-permute-done.1.right = f32[64,128]{1,0:T(8,128)S(1)} collective-permute-done((f32[64,128]{1,0:T(8,128)S(1)}, f32[64,128]{1,0:T(8,128)S(1)}, u32[]{:S(2)}, u32[]{:S(2)}) %collective-permute-start.1) | collective-permute-done | bytes 32800 | tf_op jit(solution)/shard_map/ppermute | solution.py:389
  8.0 1.7 %collective-permute-start.2 = (f32[16,8,128]{2,1,0:T(8,128)S(1)}, f32[16,8,128]{2,1,0:T(8,128)S(1)}, u32[]{:S(2)}, u32[]{:S(2)}) collective-permute-start(f32[16,8,128]{2,1,0:T(8,128)S(1)} %get-tuple-element.20), channel_id=1, source_target_pairs={{0,8},{8,16},{16,24},{24,32},{32,40},{40,48},{48,56},{56,64},{64,7... | collective-permute-start | bytes 196616 | tf_op jit(solution)/shard_map/ppermute | solution.py:389
  9.8 6.5 %collective-permute-start.3 = (f32[16,8,128]{2,1,0:T(8,128)S(1)}, f32[16,8,128]{2,1,0:T(8,128)S(1)}, u32[]{:S(2)}, u32[]{:S(2)}) collective-permute-start(f32[16,8,128]{2,1,0:T(8,128)S(1)} %get-tuple-element.21.__1_), channel_id=1, source_target_pairs={{0,120},{8,0},{16,8},{24,16},{32,24},{40,32},{48,40},{56,48},{64,5... | collective-permute-start | bytes 196616 | tf_op jit(solution)/shard_map/ppermute | solution.py:389
  16.3 0.0 copy-start.2
  16.3 10.5 %all-to-all-start = ((f32[128,1,128]{2,1,0:T(1,128)}), f32[128,1,128]{2,1,0:T(1,128)S(1)}, u32[]{:S(2)}, u32[]{:S(2)}) async-start(f32[128,1,128]{2,1,0:T(1,128)} %bitcast.4), calls=%async_computation | async-start | bytes 131072 | tf_op jit(solution)/shard_map/all_to_all | solution.py:396
  26.7 0.1 copy.15.weight
  26.9 1.3 %shard_map.108.mine = f32[72,128]{1,0:T(8,128)S(1)} custom-call(f32[4,2,64,128]{3,2,1,0:T(8,128)S(1)} %copy-done, f32[2,64,128]{2,1,0:T(8,128)S(1)} %copy-done.1, f32[2,64,128]{2,1,0:T(8,128)S(1)} %copy-done.2, f32[2,64,128]{2,1,0:T(8,128)S(1)} %copy-done.3, f32[16,8,128]{2,1,0:T(8,128)S(1)} %collective-permute-done.2.below, ...), custom_call_target="tpu_custom_call" | custom-call | flops 600000000 | bytes 1800000000 | tf_op jit(solution)/shard_map/pallas_call | solution.py:23
  28.2 0.1 collective-permute-start.4
  28.3 2.5 %shard_map.105 = (f32[4,2,64,128]{3,2,1,0:T(8,128)}, f32[2,5,2,9,8,128]{5,4,3,2,1,0:T(8,128)S(1)}) custom-call(f32[4,2,64,128]{3,2,1,0:T(8,128)S(1)} %copy-done, f32[2,64,128]{2,1,0:T(8,128)S(1)} %copy-done.1, f32[2,64,128]{2,1,0:T(8,128)S(1)} %copy-done.2, f32[2,64,128]{2,1,0:T(8,128)S(1)} %copy-done.3, f32[16,8,128]{2,1,0:T(8,128)S(1)} %collective-permute-done.2.below, ...), custom_call_target="tpu_custom_call" | custom-call | flops 600000000 | bytes 1800000000 | tf_op jit(solution)/shard_map/pallas_call | solution.py:23
  30.8 0.6 %collective-permute-done.4.other = f32[72,128]{1,0:T(8,128)S(1)} collective-permute-done((f32[72,128]{1,0:T(8,128)S(1)}, f32[72,128]{1,0:T(8,128)S(1)}, u32[]{:S(2)}, u32[]{:S(2)}) %collective-permute-start.4) | collective-permute-done | bytes 36896 | tf_op jit(solution)/shard_map/ppermute | solution.py:446
  31.4 1.1 %all-to-all-done = f32[128,1,128]{2,1,0:T(1,128)S(1)} async-done(((f32[128,1,128]{2,1,0:T(1,128)}), f32[128,1,128]{2,1,0:T(1,128)S(1)}, u32[]{:S(2)}, u32[]{:S(2)}) %all-to-all-start) | async-done | bytes 65568 | tf_op jit(solution)/shard_map/all_to_all | solution.py:396
  32.5 1.2 %shard_map.109.values = f32[128,128]{1,0:T(8,128)} custom-call(f32[128,128]{1,0:T(8,128)S(1)} %bitcast.12, f32[72,128]{1,0:T(8,128)S(1)} %shard_map.108.mine, f32[72,128]{1,0:T(8,128)S(1)} %collective-permute-done.4.other, f32[2,5,2,9,8,128]{5,4,3,2,1,0:T(8,128)S(1)} %get-tuple-element.27.coef), custom_call_target="tpu_custom_call" | custom-call | flops 600000000 | bytes 1800000000 | tf_op jit(solution)/shard_map/pallas_call | solution.py:23
  33.7 12.8 %all-to-all-start.1 = ((f32[128,1,128]{2,1,0:T(1,128)}), f32[128,1,128]{2,1,0:T(1,128)S(1)}, u32[]{:S(2)}, u32[]{:S(2)}) async-start(f32[128,1,128]{2,1,0:T(1,128)} %bitcast.7), calls=%async_computation.1 | async-start | bytes 131072 | tf_op jit(solution)/shard_map/all_to_all | solution.py:396
  46.5 0.8 %shard_map.111.force = f32[72,128]{1,0:T(8,128)S(1)} custom-call(f32[128,128]{1,0:T(8,128)S(1)} %bitcast.13, f32[72,128]{1,0:T(8,128)S(1)} %shard_map.108.mine, f32[72,128]{1,0:T(8,128)S(1)} %collective-permute-done.4.other, f32[128,128]{1,0:T(8,128)} %shard_map.109.values), custom_call_target="tpu_custom_call" | custom-call | flops 600000000 | bytes 1800000000 | tf_op jit(solution)/shard_map/pallas_call | solution.py:23
  47.3 0.0 collective-permute-start.6
  47.3 1.7 %collective-permute-start.5 = (f32[72,128]{1,0:T(8,128)S(1)}, f32[72,128]{1,0:T(8,128)S(1)}, u32[]{:S(2)}, u32[]{:S(2)}) collective-permute-start(f32[72,128]{1,0:T(8,128)S(1)} %shard_map.111.force), channel_id=1, source_target_pairs={{0,1},{1,2},{2,3},{3,4},{4,5},{5,6},{6,7},{7,0},{8,9},{9,10},{10,1... | collective-permute-start | bytes 110600 | tf_op jit(solution)/shard_map/ppermute | solution.py:389
  49.0 3.2 %all-to-all-done.1 = f32[128,1,128]{2,1,0:T(1,128)S(1)} async-done(((f32[128,1,128]{2,1,0:T(1,128)}), f32[128,1,128]{2,1,0:T(1,128)S(1)}, u32[]{:S(2)}, u32[]{:S(2)}) %all-to-all-start.1) | async-done | bytes 65568 | tf_op jit(solution)/shard_map/all_to_all | solution.py:396
  52.3 0.8 %shard_map.110.model = f32[4,128]{1,0:T(4,128)} custom-call(f32[128,128]{1,0:T(8,128)S(1)} %bitcast.14, s32[4,128]{1,0:T(4,128)S(1)} %get-tuple-element.23.owner, s32[4,128]{1,0:T(4,128)S(1)} %get-tuple-element.28.rank), custom_call_target="tpu_custom_call" | custom-call | flops 600000000 | bytes 1800000000 | tf_op jit(solution)/shard_map/pallas_call | solution.py:23
  53.0 1.7 %shard_map.112 = f32[4,2,64,128]{3,2,1,0:T(8,128)} custom-call(f32[72,128]{1,0:T(8,128)S(1)} %shard_map.111.force, f32[72,128]{1,0:T(8,128)S(1)} %collective-permute-done.5.left, f32[72,128]{1,0:T(8,128)S(1)} %collective-permute-done.6.right, f32[2,5,2,9,8,128]{5,4,3,2,1,0:T(8,128)S(1)} %get-tuple-element.27.coef, f32[4,2]{1,0:T(4,128)S(1)} %copy.15.weight, ...), custom_call_target="tpu_custom_call" | custom-call | flops 600000000 | bytes 1800000000 | tf_op jit(solution)/shard_map/pallas_call | solution.py:23
  (15 shorter events, 0.0 us)
Async XLA Ops:
  2.0 4.5 %collective-permute-start = (f32[64,128]{1,0:T(8,128)S(1)}, f32[64,128]{1,0:T(8,128)S(1)}, u32[]{:S(2)}, u32[]{:S(2)}) collective-permute-start(f32[64,128]{1,0:T(8,128)S(1)} %get-tuple-element.18), channel_id=1, source_target_pairs={{0,1},{1,2},{2,3},{3,4},{4,5},{5,6},{6,7},{7,0},{8,9},{9,10},{10,1... | collective-permute-start | bytes 98312 | tf_op jit(solution)/shard_map/ppermute | solution.py:389
  4.7 3.3 %collective-permute-start.1 = (f32[64,128]{1,0:T(8,128)S(1)}, f32[64,128]{1,0:T(8,128)S(1)}, u32[]{:S(2)}, u32[]{:S(2)}) collective-permute-start(f32[64,128]{1,0:T(8,128)S(1)} %get-tuple-element.19), channel_id=1, source_target_pairs={{0,7},{1,0},{2,1},{3,2},{4,3},{5,4},{6,5},{7,6},{8,15},{9,8},{10,9... | collective-permute-start | bytes 98312 | tf_op jit(solution)/shard_map/ppermute | solution.py:389
  8.0 18.8 %collective-permute-start.2 = (f32[16,8,128]{2,1,0:T(8,128)S(1)}, f32[16,8,128]{2,1,0:T(8,128)S(1)}, u32[]{:S(2)}, u32[]{:S(2)}) collective-permute-start(f32[16,8,128]{2,1,0:T(8,128)S(1)} %get-tuple-element.20), channel_id=1, source_target_pairs={{0,8},{8,16},{16,24},{24,32},{32,40},{40,48},{48,56},{56,64},{64,7... | collective-permute-start | bytes 196616 | tf_op jit(solution)/shard_map/ppermute | solution.py:389
  9.8 17.1 %collective-permute-start.3 = (f32[16,8,128]{2,1,0:T(8,128)S(1)}, f32[16,8,128]{2,1,0:T(8,128)S(1)}, u32[]{:S(2)}, u32[]{:S(2)}) collective-permute-start(f32[16,8,128]{2,1,0:T(8,128)S(1)} %get-tuple-element.21.__1_), channel_id=1, source_target_pairs={{0,120},{8,0},{16,8},{24,16},{32,24},{40,32},{48,40},{56,48},{64,5... | collective-permute-start | bytes 196616 | tf_op jit(solution)/shard_map/ppermute | solution.py:389
  16.2 10.5 %copy-start.4 = (f32[4,2]{0,1:T(2,128)S(1)}, f32[4,2]{0,1:T(2,128)}, u32[]{:S(2)}) copy-start(f32[4,2]{0,1:T(2,128)} %param.12) | copy-start | bytes 100
  16.2 10.6 %copy-start = (f32[4,2,64,128]{3,2,1,0:T(8,128)S(1)}, f32[4,2,64,128]{3,2,1,0:T(8,128)}, u32[]{:S(2)}) copy-start(f32[4,2,64,128]{3,2,1,0:T(8,128)} %conc.5) | copy-start | bytes 786436
  16.2 10.6 %copy-start.3 = (f32[2,64,128]{2,1,0:T(8,128)S(1)}, f32[2,64,128]{2,1,0:T(8,128)}, u32[]{:S(2)}) copy-start(f32[2,64,128]{2,1,0:T(8,128)} %vv.5) | copy-start | bytes 196612
  16.2 10.6 %copy-start.1 = (f32[2,64,128]{2,1,0:T(8,128)S(1)}, f32[2,64,128]{2,1,0:T(8,128)}, u32[]{:S(2)}) copy-start(f32[2,64,128]{2,1,0:T(8,128)} %kk.5) | copy-start | bytes 196612
  16.3 10.6 %copy-start.2 = (f32[2,64,128]{2,1,0:T(8,128)S(1)}, f32[2,64,128]{2,1,0:T(8,128)}, u32[]{:S(2)}) copy-start(f32[2,64,128]{2,1,0:T(8,128)} %uu.5) | copy-start | bytes 196612
  16.3 16.3 %all-to-all-start = ((f32[128,1,128]{2,1,0:T(1,128)}), f32[128,1,128]{2,1,0:T(1,128)S(1)}, u32[]{:S(2)}, u32[]{:S(2)}) async-start(f32[128,1,128]{2,1,0:T(1,128)} %bitcast.4), calls=%async_computation | async-start | bytes 131072 | tf_op jit(solution)/shard_map/all_to_all | solution.py:396
  28.2 3.2 %collective-permute-start.4 = (f32[72,128]{1,0:T(8,128)S(1)}, f32[72,128]{1,0:T(8,128)S(1)}, u32[]{:S(2)}, u32[]{:S(2)}) collective-permute-start(f32[72,128]{1,0:T(8,128)S(1)} %shard_map.108.mine), channel_id=1, source_target_pairs={{0,128},{128,0},{1,129},{129,1},{2,130},{130,2},{3,131},{131,3},{4... | collective-permute-start | bytes 110600 | tf_op jit(solution)/shard_map/ppermute | solution.py:446
  33.7 18.6 %all-to-all-start.1 = ((f32[128,1,128]{2,1,0:T(1,128)}), f32[128,1,128]{2,1,0:T(1,128)S(1)}, u32[]{:S(2)}, u32[]{:S(2)}) async-start(f32[128,1,128]{2,1,0:T(1,128)} %bitcast.7), calls=%async_computation.1 | async-start | bytes 131072 | tf_op jit(solution)/shard_map/all_to_all | solution.py:396
  47.3 5.8 %collective-permute-start.6 = (f32[72,128]{1,0:T(8,128)S(1)}, f32[72,128]{1,0:T(8,128)S(1)}, u32[]{:S(2)}, u32[]{:S(2)}) collective-permute-start(f32[72,128]{1,0:T(8,128)S(1)} %shard_map.111.force), channel_id=1, source_target_pairs={{0,7},{1,0},{2,1},{3,2},{4,3},{5,4},{6,5},{7,6},{8,15},{9,8},{10,9... | collective-permute-start | bytes 110600 | tf_op jit(solution)/shard_map/ppermute | solution.py:389
  47.3 5.7 %collective-permute-start.5 = (f32[72,128]{1,0:T(8,128)S(1)}, f32[72,128]{1,0:T(8,128)S(1)}, u32[]{:S(2)}, u32[]{:S(2)}) collective-permute-start(f32[72,128]{1,0:T(8,128)S(1)} %shard_map.111.force), channel_id=1, source_target_pairs={{0,1},{1,2},{2,3},{3,4},{4,5},{5,6},{6,7},{7,0},{8,9},{9,10},{10,1... | collective-permute-start | bytes 110600 | tf_op jit(solution)/shard_map/ppermute | solution.py:389

commit v8 on v6

--- a/solution.py
+++ b/solution.py
@@ -55,8 +55,8 @@
 
 
 def tile_at(t, groups):
-    for shift in (3, 4, 3):
-        t = (t * 45 + 3) & (groups - 1)
+    for shift in (4, 3, 2):
+        t = (t * 71 + 16) & (groups - 1)
         t = t ^ (t >> shift)
     return t
 

time: 53.7 us -> 56.6 us (1.054)
  starting transfers between devices: 36.6 us -> 41.2 us
  waiting for transfers between devices: 5.15 us -> 3.4 us
    all_to_all x2, starting transfers between devices: 23.2 us -> 27.9 us  [exchange(): lax.all_to_all(value, ('lev', 'gx', 'gy'), 0, 0, axis_index_groups=groups...]
    all_to_all x2, waiting for transfers between devices: 1.14 us -> 0.01 us  [exchange(): lax.all_to_all(value, ('lev', 'gx', 'gy'), 0, 0, axis_index_groups=groups...]
  transfers between devices with their start and end apart: 9 -> 9, of which waited for: 4 -> 3; matrix products, arithmetic and copies ran while one was open for 0% -> 0% of each run, Pallas kernels for 14% -> 13%
where the time goes in v8:
time: 56.6 us; the launch traced here: 56.4 us
  starting transfers between devices  41.2 us (73%)
  Pallas kernels  10.9 us (19%)
  waiting for transfers between devices  3.4 us (6%)
  between operations  0.73 us (1%)
    all_to_all x2, starting transfers between devices, exchange(): lax.all_to_all(value, ('lev', 'gx', 'gy'), 0, 0, axis_index_groups=groups...  27.9 us
    ppermute x6, starting transfers between devices, ring(): return lax.ppermute(value, axis, [(i, (i + step) % n) for i in range(n)])  13.2 us
    pallas_call x10, Pallas kernels, call(): pl.pallas_call(body, out_shape=outs, in_specs=specs or [VMEM] * len(input...  10.9 us
    ppermute x6, waiting for transfers between devices, ring(): return lax.ppermute(value, axis, [(i, (i + step) % n) for i in range(n)])  3.16 us
  transfers between devices with their start and end apart: 9, of which 3 were waited for; matrix products, arithmetic and copies ran while one was open for 0% of the time, Pallas kernels for 13%

profile of v8, /device:TPU:1, one launch (start us, length us, event | category | flops | bytes accessed | tf_op | source)
XLA Modules:
  0.0 56.4 jit_solution(18381668363009477825)
XLA Ops:
  0.6 1.3 %shard_map.103 = (f32[64,128]{1,0:T(8,128)S(1)}, f32[64,128]{1,0:T(8,128)S(1)}, f32[14,8,128]{2,1,0:T(8,128)S(1)}, f32[14,8,128]{2,1,0:T(8,128)S(1)}, s32[4,128]...) custom-call(f32[4,2,64,128]{3,2,1,0:T(8,128)} %conc.5, f32[2,64,128]{2,1,0:T(8,128)} %kk.5, ...), custom_call_target="tpu_custom_call" | custom-call | flops 1000000 | bytes 3000000 | tf_op jit(solution)/shard_map/pallas_call | solution.py:23
  2.0 2.7 %collective-permute-start = (f32[64,128]{1,0:T(8,128)S(1)}, f32[64,128]{1,0:T(8,128)S(1)}, u32[]{:S(2)}, u32[]{:S(2)}) collective-permute-start(f32[64,128]{1,0:T(8,128)S(1)} %get-tuple-element.18), channel_id=1, source_target_pairs={{0,1},{1,2},{2,3},{3,4},{4,5},{5,6},{6,7},{7,0},{8,9},{9,10},{10,1... | collective-permute-start | bytes 98312 | tf_op jit(solution)/shard_map/ppermute | solution.py:389
  4.7 0.6 %collective-permute-start.1 = (f32[64,128]{1,0:T(8,128)S(1)}, f32[64,128]{1,0:T(8,128)S(1)}, u32[]{:S(2)}, u32[]{:S(2)}) collective-permute-start(f32[64,128]{1,0:T(8,128)S(1)} %get-tuple-element.19), channel_id=1, source_target_pairs={{0,7},{1,0},{2,1},{3,2},{4,3},{5,4},{6,5},{7,6},{8,15},{9,8},{10,9... | collective-permute-start | bytes 98312 | tf_op jit(solution)/shard_map/ppermute | solution.py:389
  5.3 1.2 %shard_map.106 = (f32[128,128]{1,0:T(8,128)}, s32[4,128]{1,0:T(4,128)S(1)}) custom-call(s32[4,128]{1,0:T(4,128)S(1)} %get-tuple-element.23.owner, s32[4,128]{1,0:T(4,128)S(1)} %get-tuple-element.24.column, f32[4,128]{1,0:T(4,128)S(1)} %get-tuple-element.25.observed), custom_call_target="tpu_custom_call" | custom-call | flops 600000000 | bytes 1800000000 | tf_op jit(solution)/shard_map/pallas_call | solution.py:23
  6.5 0.0 collective-permute-done.left
  6.5 1.5 %collective-permute-done.1.right = f32[64,128]{1,0:T(8,128)S(1)} collective-permute-done((f32[64,128]{1,0:T(8,128)S(1)}, f32[64,128]{1,0:T(8,128)S(1)}, u32[]{:S(2)}, u32[]{:S(2)}) %collective-permute-start.1) | collective-permute-done | bytes 32800 | tf_op jit(solution)/shard_map/ppermute | solution.py:389
  8.0 1.7 %collective-permute-start.2 = (f32[16,8,128]{2,1,0:T(8,128)S(1)}, f32[16,8,128]{2,1,0:T(8,128)S(1)}, u32[]{:S(2)}, u32[]{:S(2)}) collective-permute-start(f32[16,8,128]{2,1,0:T(8,128)S(1)} %get-tuple-element.20), channel_id=1, source_target_pairs={{0,8},{8,16},{16,24},{24,32},{32,40},{40,48},{48,56},{56,64},{64,7... | collective-permute-start | bytes 196616 | tf_op jit(solution)/shard_map/ppermute | solution.py:389
  9.8 6.5 %collective-permute-start.3 = (f32[16,8,128]{2,1,0:T(8,128)S(1)}, f32[16,8,128]{2,1,0:T(8,128)S(1)}, u32[]{:S(2)}, u32[]{:S(2)}) collective-permute-start(f32[16,8,128]{2,1,0:T(8,128)S(1)} %get-tuple-element.21.__1_), channel_id=1, source_target_pairs={{0,120},{8,0},{16,8},{24,16},{32,24},{40,32},{48,40},{56,48},{64,5... | collective-permute-start | bytes 196616 | tf_op jit(solution)/shard_map/ppermute | solution.py:389
  16.3 0.0 copy-start.2
  16.3 13.4 %all-to-all-start = ((f32[128,1,128]{2,1,0:T(1,128)}), f32[128,1,128]{2,1,0:T(1,128)S(1)}, u32[]{:S(2)}, u32[]{:S(2)}) async-start(f32[128,1,128]{2,1,0:T(1,128)} %bitcast.4), calls=%async_computation | async-start | bytes 131072 | tf_op jit(solution)/shard_map/all_to_all | solution.py:396
  29.7 0.1 copy.15.weight
  29.9 1.3 %shard_map.108.mine = f32[72,128]{1,0:T(8,128)S(1)} custom-call(f32[4,2,64,128]{3,2,1,0:T(8,128)S(1)} %copy-done, f32[2,64,128]{2,1,0:T(8,128)S(1)} %copy-done.1, f32[2,64,128]{2,1,0:T(8,128)S(1)} %copy-done.2, f32[2,64,128]{2,1,0:T(8,128)S(1)} %copy-done.3, f32[16,8,128]{2,1,0:T(8,128)S(1)} %collective-permute-done.2.below, ...), custom_call_target="tpu_custom_call" | custom-call | flops 600000000 | bytes 1800000000 | tf_op jit(solution)/shard_map/pallas_call | solution.py:23
  31.2 0.1 collective-permute-start.4
  31.3 2.6 %shard_map.105 = (f32[4,2,64,128]{3,2,1,0:T(8,128)}, f32[2,5,2,9,8,128]{5,4,3,2,1,0:T(8,128)S(1)}) custom-call(f32[4,2,64,128]{3,2,1,0:T(8,128)S(1)} %copy-done, f32[2,64,128]{2,1,0:T(8,128)S(1)} %copy-done.1, f32[2,64,128]{2,1,0:T(8,128)S(1)} %copy-done.2, f32[2,64,128]{2,1,0:T(8,128)S(1)} %copy-done.3, f32[16,8,128]{2,1,0:T(8,128)S(1)} %collective-permute-done.2.below, ...), custom_call_target="tpu_custom_call" | custom-call | flops 600000000 | bytes 1800000000 | tf_op jit(solution)/shard_map/pallas_call | solution.py:23
  33.8 0.2 collective-permute-done.4.other
  34.1 1.2 %shard_map.109.values = f32[128,128]{1,0:T(8,128)} custom-call(f32[128,128]{1,0:T(8,128)S(1)} %bitcast.13, f32[72,128]{1,0:T(8,128)S(1)} %shard_map.108.mine, f32[72,128]{1,0:T(8,128)S(1)} %collective-permute-done.4.other, f32[2,5,2,9,8,128]{5,4,3,2,1,0:T(8,128)S(1)} %get-tuple-element.27.coef), custom_call_target="tpu_custom_call" | custom-call | flops 600000000 | bytes 1800000000 | tf_op jit(solution)/shard_map/pallas_call | solution.py:23
  35.2 14.5 %all-to-all-start.1 = ((f32[128,1,128]{2,1,0:T(1,128)}), f32[128,1,128]{2,1,0:T(1,128)S(1)}, u32[]{:S(2)}, u32[]{:S(2)}) async-start(f32[128,1,128]{2,1,0:T(1,128)} %bitcast.7), calls=%async_computation.1 | async-start | bytes 131072 | tf_op jit(solution)/shard_map/all_to_all | solution.py:396
  49.7 0.8 %shard_map.111.force = f32[72,128]{1,0:T(8,128)S(1)} custom-call(f32[128,128]{1,0:T(8,128)S(1)} %bitcast.14, f32[72,128]{1,0:T(8,128)S(1)} %shard_map.108.mine, f32[72,128]{1,0:T(8,128)S(1)} %collective-permute-done.4.other, f32[128,128]{1,0:T(8,128)} %shard_map.109.values), custom_call_target="tpu_custom_call" | custom-call | flops 600000000 | bytes 1800000000 | tf_op jit(solution)/shard_map/pallas_call | solution.py:23
  50.5 0.9 %collective-permute-start.6 = (f32[72,128]{1,0:T(8,128)S(1)}, f32[72,128]{1,0:T(8,128)S(1)}, u32[]{:S(2)}, u32[]{:S(2)}) collective-permute-start(f32[72,128]{1,0:T(8,128)S(1)} %shard_map.111.force), channel_id=1, source_target_pairs={{0,7},{1,0},{2,1},{3,2},{4,3},{5,4},{6,5},{7,6},{8,15},{9,8},{10,9... | collective-permute-start | bytes 110600 | tf_op jit(solution)/shard_map/ppermute | solution.py:389
  51.4 0.8 %collective-permute-start.5 = (f32[72,128]{1,0:T(8,128)S(1)}, f32[72,128]{1,0:T(8,128)S(1)}, u32[]{:S(2)}, u32[]{:S(2)}) collective-permute-start(f32[72,128]{1,0:T(8,128)S(1)} %shard_map.111.force), channel_id=1, source_target_pairs={{0,1},{1,2},{2,3},{3,4},{4,5},{5,6},{6,7},{7,0},{8,9},{9,10},{10,1... | collective-permute-start | bytes 110600 | tf_op jit(solution)/shard_map/ppermute | solution.py:389
  52.3 1.6 %collective-permute-done.6.right = f32[72,128]{1,0:T(8,128)S(1)} collective-permute-done((f32[72,128]{1,0:T(8,128)S(1)}, f32[72,128]{1,0:T(8,128)S(1)}, u32[]{:S(2)}, u32[]{:S(2)}) %collective-permute-start.6) | collective-permute-done | bytes 36896 | tf_op jit(solution)/shard_map/ppermute | solution.py:389
  53.9 1.7 %shard_map.112 = f32[4,2,64,128]{3,2,1,0:T(8,128)} custom-call(f32[72,128]{1,0:T(8,128)S(1)} %shard_map.111.force, f32[72,128]{1,0:T(8,128)S(1)} %collective-permute-done.5.left, f32[72,128]{1,0:T(8,128)S(1)} %collective-permute-done.6.right, f32[2,5,2,9,8,128]{5,4,3,2,1,0:T(8,128)S(1)} %get-tuple-element.27.coef, f32[4,2]{1,0:T(4,128)S(1)} %copy.15.weight), custom_call_target="tpu_custom_call" | custom-call | flops 600000000 | bytes 1800000000 | tf_op jit(solution)/shard_map/pallas_call | solution.py:23
  55.6 0.0 all-to-all-done.1
  55.6 0.8 %shard_map.110 = f32[4,128]{1,0:T(4,128)} custom-call(f32[128,128]{1,0:T(8,128)S(1)} %bitcast.12, s32[4,128]{1,0:T(4,128)S(1)} %get-tuple-element.23.owner, s32[4,128]{1,0:T(4,128)S(1)} %get-tuple-element.28.rank), custom_call_target="tpu_custom_call" | custom-call | flops 1000000 | bytes 3000000 | tf_op jit(solution)/shard_map/pallas_call | solution.py:23
  (15 shorter events, 0.0 us)
Async XLA Ops:
  2.0 4.5 %collective-permute-start = (f32[64,128]{1,0:T(8,128)S(1)}, f32[64,128]{1,0:T(8,128)S(1)}, u32[]{:S(2)}, u32[]{:S(2)}) collective-permute-start(f32[64,128]{1,0:T(8,128)S(1)} %get-tuple-element.18), channel_id=1, source_target_pairs={{0,1},{1,2},{2,3},{3,4},{4,5},{5,6},{6,7},{7,0},{8,9},{9,10},{10,1... | collective-permute-start | bytes 98312 | tf_op jit(solution)/shard_map/ppermute | solution.py:389
  4.7 3.3 %collective-permute-start.1 = (f32[64,128]{1,0:T(8,128)S(1)}, f32[64,128]{1,0:T(8,128)S(1)}, u32[]{:S(2)}, u32[]{:S(2)}) collective-permute-start(f32[64,128]{1,0:T(8,128)S(1)} %get-tuple-element.19), channel_id=1, source_target_pairs={{0,7},{1,0},{2,1},{3,2},{4,3},{5,4},{6,5},{7,6},{8,15},{9,8},{10,9... | collective-permute-start | bytes 98312 | tf_op jit(solution)/shard_map/ppermute | solution.py:389
  8.0 21.8 %collective-permute-start.2 = (f32[16,8,128]{2,1,0:T(8,128)S(1)}, f32[16,8,128]{2,1,0:T(8,128)S(1)}, u32[]{:S(2)}, u32[]{:S(2)}) collective-permute-start(f32[16,8,128]{2,1,0:T(8,128)S(1)} %get-tuple-element.20), channel_id=1, source_target_pairs={{0,8},{8,16},{16,24},{24,32},{32,40},{40,48},{48,56},{56,64},{64,7... | collective-permute-start | bytes 196616 | tf_op jit(solution)/shard_map/ppermute | solution.py:389
  9.8 20.1 %collective-permute-start.3 = (f32[16,8,128]{2,1,0:T(8,128)S(1)}, f32[16,8,128]{2,1,0:T(8,128)S(1)}, u32[]{:S(2)}, u32[]{:S(2)}) collective-permute-start(f32[16,8,128]{2,1,0:T(8,128)S(1)} %get-tuple-element.21.__1_), channel_id=1, source_target_pairs={{0,120},{8,0},{16,8},{24,16},{32,24},{40,32},{48,40},{56,48},{64,5... | collective-permute-start | bytes 196616 | tf_op jit(solution)/shard_map/ppermute | solution.py:389
  16.2 13.5 %copy-start.4 = (f32[4,2]{0,1:T(2,128)S(1)}, f32[4,2]{0,1:T(2,128)}, u32[]{:S(2)}) copy-start(f32[4,2]{0,1:T(2,128)} %param.12) | copy-start | bytes 100
  16.2 13.6 %copy-start = (f32[4,2,64,128]{3,2,1,0:T(8,128)S(1)}, f32[4,2,64,128]{3,2,1,0:T(8,128)}, u32[]{:S(2)}) copy-start(f32[4,2,64,128]{3,2,1,0:T(8,128)} %conc.5) | copy-start | bytes 786436
  16.2 13.6 %copy-start.3 = (f32[2,64,128]{2,1,0:T(8,128)S(1)}, f32[2,64,128]{2,1,0:T(8,128)}, u32[]{:S(2)}) copy-start(f32[2,64,128]{2,1,0:T(8,128)} %vv.5) | copy-start | bytes 196612
  16.2 13.6 %copy-start.1 = (f32[2,64,128]{2,1,0:T(8,128)S(1)}, f32[2,64,128]{2,1,0:T(8,128)}, u32[]{:S(2)}) copy-start(f32[2,64,128]{2,1,0:T(8,128)} %kk.5) | copy-start | bytes 196612
  16.3 13.6 %copy-start.2 = (f32[2,64,128]{2,1,0:T(8,128)S(1)}, f32[2,64,128]{2,1,0:T(8,128)}, u32[]{:S(2)}) copy-start(f32[2,64,128]{2,1,0:T(8,128)} %uu.5) | copy-start | bytes 196612
  16.3 17.8 %all-to-all-start = ((f32[128,1,128]{2,1,0:T(1,128)}), f32[128,1,128]{2,1,0:T(1,128)S(1)}, u32[]{:S(2)}, u32[]{:S(2)}) async-start(f32[128,1,128]{2,1,0:T(1,128)} %bitcast.4), calls=%async_computation | async-start | bytes 131072 | tf_op jit(solution)/shard_map/all_to_all | solution.py:396
  31.2 2.9 %collective-permute-start.4 = (f32[72,128]{1,0:T(8,128)S(1)}, f32[72,128]{1,0:T(8,128)S(1)}, u32[]{:S(2)}, u32[]{:S(2)}) collective-permute-start(f32[72,128]{1,0:T(8,128)S(1)} %shard_map.108.mine), channel_id=1, source_target_pairs={{0,128},{128,0},{1,129},{129,1},{2,130},{130,2},{3,131},{131,3},{4... | collective-permute-start | bytes 110600 | tf_op jit(solution)/shard_map/ppermute | solution.py:446
  35.2 20.4 %all-to-all-start.1 = ((f32[128,1,128]{2,1,0:T(1,128)}), f32[128,1,128]{2,1,0:T(1,128)S(1)}, u32[]{:S(2)}, u32[]{:S(2)}) async-start(f32[128,1,128]{2,1,0:T(1,128)} %bitcast.7), calls=%async_computation.1 | async-start | bytes 131072 | tf_op jit(solution)/shard_map/all_to_all | solution.py:396
  50.5 3.4 %collective-permute-start.6 = (f32[72,128]{1,0:T(8,128)S(1)}, f32[72,128]{1,0:T(8,128)S(1)}, u32[]{:S(2)}, u32[]{:S(2)}) collective-permute-start(f32[72,128]{1,0:T(8,128)S(1)} %shard_map.111.force), channel_id=1, source_target_pairs={{0,7},{1,0},{2,1},{3,2},{4,3},{5,4},{6,5},{7,6},{8,15},{9,8},{10,9... | collective-permute-start | bytes 110600 | tf_op jit(solution)/shard_map/ppermute | solution.py:389
  51.4 2.5 %collective-permute-start.5 = (f32[72,128]{1,0:T(8,128)S(1)}, f32[72,128]{1,0:T(8,128)S(1)}, u32[]{:S(2)}, u32[]{:S(2)}) collective-permute-start(f32[72,128]{1,0:T(8,128)S(1)} %shard_map.111.force), channel_id=1, source_target_pairs={{0,1},{1,2},{2,3},{3,4},{4,5},{5,6},{6,7},{7,0},{8,9},{9,10},{10,1... | collective-permute-start | bytes 110600 | tf_op jit(solution)/shard_map/ppermute | solution.py:389

commit v9 on v6

--- a/solution.py
+++ b/solution.py
@@ -358,7 +358,7 @@
         out[j : j + 1, :] = jnp.sum(jnp.where(slot, mine, 0.0), axis=0, keepdims=True)
 
 
-def adjoint_body(force, left, right, coef, weight, out, state, nat):
+def adjoint_body(force, left, right, coef, weight, out, state, nat, made, sems):
     keep_l, keep_r = inside("gy")
     n, m = out.shape[2], out.shape[3]
     at = iota((EDGE, m), 1)
@@ -376,7 +376,11 @@
     for l in range(levels):
         value = gather(nat.at[3 + l], [state[STEPS % 2, l, 0, g] for g in range(steps)])
         for t in range(out.shape[0]):
-            out[t, l] = weight[t, l] * value[0:n]
+            made[t, l] = weight[t, l] * value[0:n]
+            pltpu.make_async_copy(made.at[t, l], out.at[t, l], sems.at[t, l]).start()
+    for l in range(levels):
+        for t in range(out.shape[0]):
+            pltpu.make_async_copy(made.at[t, l], out.at[t, l], sems.at[t, l]).wait()
 
 
 def after(x, other):
@@ -387,6 +391,16 @@
 def ring(value, axis, step):
     n = lax.axis_size(axis)
     return lax.ppermute(value, axis, [(i, (i + step) % n) for i in range(n)])
+
+
+def long_ring(value, step):
+    n = lax.axis_size("gx")
+    pairs = []
+    for l in range(2):
+        for i in range(n):
+            to = i + step
+            pairs.append((l * n + i, l * n + to if 0 <= to < n else (1 - l) * n + to % n))
+    return lax.ppermute(value, ("lev", "gx"), pairs)
 
 
 def exchange(value):
@@ -426,7 +440,7 @@
     )
     edge = S((fields + 2, EDGE, m), F32)
     high, low = call(corners_body, (edge, edge), (high, low, left, right))
-    above, below = ring(low, "gx", -1), ring(high, "gx", 1)
+    above, below = long_ring(low, -1), long_ring(high, 1)
     asked = exchange(after(req, low))
     inputs = (conc, kk, uu, vv, below, above, left, right)
     strip = S((n + EDGE, m), F32)
@@ -475,7 +489,10 @@
         scratch=[
             pltpu.VMEM((2, levels, 2, some, EDGE, m), F32),
             pltpu.VMEM((3 + levels, n + EDGE, m), F32),
+            pltpu.VMEM(conc.shape, F32),
+            pltpu.SemaphoreType.DMA((tracers, levels)),
         ],
+        outspec=HBM,
     )
     model = call(
         functools.partial(answer_body, groups), S(owner.shape, F32), (got, owner, rank)

time: 53.7 us -> 53.7 us (level)
    ppermute x6 -> x4, starting transfers between devices: 13.2 us -> 5.04 us  [ring(): return lax.ppermute(value, axis, [(i, (i + step) % n) for i in range(n)])]
    ppermute x0 -> x2, starting transfers between devices: none -> 7.94 us  [long_ring(): return lax.ppermute(value, ('lev', 'gx'), pairs)]
    ppermute x6 -> x4, waiting for transfers between devices: 3.47 us -> 3.47 us  [ring(): return lax.ppermute(value, axis, [(i, (i + step) % n) for i in range(n)])]
where the time goes in v9:
time: 53.7 us; the launch traced here: 53.5 us
  starting transfers between devices  36.6 us (68%)
  Pallas kernels  10.9 us (20%)
  waiting for transfers between devices  5.15 us (10%)
  between operations  0.75 us (1%)
    all_to_all x2, starting transfers between devices, exchange(): lax.all_to_all(value, ('lev', 'gx', 'gy'), 0, 0, axis_index_groups=groups...  23.5 us
    pallas_call x10, Pallas kernels, call(): pl.pallas_call(body, out_shape=outs, in_specs=specs or [VMEM] * len(input...  10.9 us
    ppermute x2, starting transfers between devices, long_ring(): return lax.ppermute(value, ('lev', 'gx'), pairs)  7.94 us
    ppermute x4, starting transfers between devices, ring(): return lax.ppermute(value, axis, [(i, (i + step) % n) for i in range(n)])  5.04 us
    ppermute x4, waiting for transfers between devices, ring(): return lax.ppermute(value, axis, [(i, (i + step) % n) for i in range(n)])  3.47 us
    all_to_all x2, waiting for transfers between devices, exchange(): lax.all_to_all(value, ('lev', 'gx', 'gy'), 0, 0, axis_index_groups=groups...  1.14 us
  transfers between devices with their start and end apart: 9, of which 4 were waited for; matrix products, arithmetic and copies ran while one was open for 0% of the time, Pallas kernels for 14%

profile of v9, /device:TPU:1, one launch (start us, length us, event | category | flops | bytes accessed | tf_op | source)
XLA Modules:
  0.0 53.5 jit_solution(14794842076019228832)
XLA Ops:
  0.6 1.3 %shard_map.103 = (f32[64,128]{1,0:T(8,128)S(1)}, f32[64,128]{1,0:T(8,128)S(1)}, f32[14,8,128]{2,1,0:T(8,128)S(1)}, f32[14,8,128]{2,1,0:T(8,128)S(1)}, s32[4,128]...) custom-call(f32[4,2,64,128]{3,2,1,0:T(8,128)} %conc.5, f32[2,64,128]{2,1,0:T(8,128)} %kk.5, ...), custom_call_target="tpu_custom_call" | custom-call | flops 1000000 | bytes 3000000 | tf_op jit(solution)/shard_map/pallas_call | solution.py:23
  2.0 2.7 %collective-permute-start = (f32[64,128]{1,0:T(8,128)S(1)}, f32[64,128]{1,0:T(8,128)S(1)}, u32[]{:S(2)}, u32[]{:S(2)}) collective-permute-start(f32[64,128]{1,0:T(8,128)S(1)} %get-tuple-element.18), channel_id=1, source_target_pairs={{0,1},{1,2},{2,3},{3,4},{4,5},{5,6},{6,7},{7,0},{8,9},{9,10},{10,1... | collective-permute-start | bytes 98312 | tf_op jit(solution)/shard_map/ppermute | solution.py:393
  4.7 0.6 %collective-permute-start.1 = (f32[64,128]{1,0:T(8,128)S(1)}, f32[64,128]{1,0:T(8,128)S(1)}, u32[]{:S(2)}, u32[]{:S(2)}) collective-permute-start(f32[64,128]{1,0:T(8,128)S(1)} %get-tuple-element.19), channel_id=1, source_target_pairs={{0,7},{1,0},{2,1},{3,2},{4,3},{5,4},{6,5},{7,6},{8,15},{9,8},{10,9... | collective-permute-start | bytes 98312 | tf_op jit(solution)/shard_map/ppermute | solution.py:393
  5.3 1.2 %shard_map.106 = (f32[128,128]{1,0:T(8,128)}, s32[4,128]{1,0:T(4,128)S(1)}) custom-call(s32[4,128]{1,0:T(4,128)S(1)} %get-tuple-element.23.owner, s32[4,128]{1,0:T(4,128)S(1)} %get-tuple-element.24.column, f32[4,128]{1,0:T(4,128)S(1)} %get-tuple-element.25.observed), custom_call_target="tpu_custom_call" | custom-call | flops 600000000 | bytes 1800000000 | tf_op jit(solution)/shard_map/pallas_call | solution.py:23
  6.5 0.0 collective-permute-done.left
  6.5 1.5 %collective-permute-done.1.right = f32[64,128]{1,0:T(8,128)S(1)} collective-permute-done((f32[64,128]{1,0:T(8,128)S(1)}, f32[64,128]{1,0:T(8,128)S(1)}, u32[]{:S(2)}, u32[]{:S(2)}) %collective-permute-start.1) | collective-permute-done | bytes 32800 | tf_op jit(solution)/shard_map/ppermute | solution.py:393
  8.0 1.7 %collective-permute-start.2 = (f32[16,8,128]{2,1,0:T(8,128)S(1)}, f32[16,8,128]{2,1,0:T(8,128)S(1)}, u32[]{:S(2)}, u32[]{:S(2)}) collective-permute-start(f32[16,8,128]{2,1,0:T(8,128)S(1)} %get-tuple-element.20), channel_id=1, source_target_pairs={{0,8},{8,16},{16,24},{24,32},{32,40},{40,48},{48,56},{56,64},{64,7... | collective-permute-start | bytes 196616 | tf_op jit(solution)/shard_map/ppermute | solution.py:403
  9.8 6.2 %collective-permute-start.3 = (f32[16,8,128]{2,1,0:T(8,128)S(1)}, f32[16,8,128]{2,1,0:T(8,128)S(1)}, u32[]{:S(2)}, u32[]{:S(2)}) collective-permute-start(f32[16,8,128]{2,1,0:T(8,128)S(1)} %get-tuple-element.21.__1_), channel_id=1, source_target_pairs={{0,248},{8,0},{16,8},{24,16},{32,24},{40,32},{48,40},{56,48},{64,5... | collective-permute-start | bytes 196616 | tf_op jit(solution)/shard_map/ppermute | solution.py:403
  16.0 0.0 copy-start.2
  16.0 10.7 %all-to-all-start = ((f32[128,1,128]{2,1,0:T(1,128)}), f32[128,1,128]{2,1,0:T(1,128)S(1)}, u32[]{:S(2)}, u32[]{:S(2)}) async-start(f32[128,1,128]{2,1,0:T(1,128)} %bitcast.4), calls=%async_computation | async-start | bytes 131072 | tf_op jit(solution)/shard_map/all_to_all | solution.py:410
  26.7 0.1 copy.15.weight
  26.9 1.3 %shard_map.108.mine = f32[72,128]{1,0:T(8,128)S(1)} custom-call(f32[4,2,64,128]{3,2,1,0:T(8,128)S(1)} %copy-done, f32[2,64,128]{2,1,0:T(8,128)S(1)} %copy-done.1, f32[2,64,128]{2,1,0:T(8,128)S(1)} %copy-done.2, f32[2,64,128]{2,1,0:T(8,128)S(1)} %copy-done.3, f32[16,8,128]{2,1,0:T(8,128)S(1)} %collective-permute-done.2.below, ...), custom_call_target="tpu_custom_call" | custom-call | flops 600000000 | bytes 1800000000 | tf_op jit(solution)/shard_map/pallas_call | solution.py:23
  28.2 0.1 collective-permute-start.4
  28.3 2.6 %shard_map.105 = (f32[4,2,64,128]{3,2,1,0:T(8,128)}, f32[2,5,2,9,8,128]{5,4,3,2,1,0:T(8,128)S(1)}) custom-call(f32[4,2,64,128]{3,2,1,0:T(8,128)S(1)} %copy-done, f32[2,64,128]{2,1,0:T(8,128)S(1)} %copy-done.1, f32[2,64,128]{2,1,0:T(8,128)S(1)} %copy-done.2, f32[2,64,128]{2,1,0:T(8,128)S(1)} %copy-done.3, f32[16,8,128]{2,1,0:T(8,128)S(1)} %collective-permute-done.2.below, ...), custom_call_target="tpu_custom_call" | custom-call | flops 600000000 | bytes 1800000000 | tf_op jit(solution)/shard_map/pallas_call | solution.py:23
  30.8 0.5 collective-permute-done.4.other
  31.4 1.1 %all-to-all-done = f32[128,1,128]{2,1,0:T(1,128)S(1)} async-done(((f32[128,1,128]{2,1,0:T(1,128)}), f32[128,1,128]{2,1,0:T(1,128)S(1)}, u32[]{:S(2)}, u32[]{:S(2)}) %all-to-all-start) | async-done | bytes 65568 | tf_op jit(solution)/shard_map/all_to_all | solution.py:410
  32.5 1.2 %shard_map.109.values = f32[128,128]{1,0:T(8,128)} custom-call(f32[128,128]{1,0:T(8,128)S(1)} %bitcast.13, f32[72,128]{1,0:T(8,128)S(1)} %shard_map.108.mine, f32[72,128]{1,0:T(8,128)S(1)} %collective-permute-done.4.other, f32[2,5,2,9,8,128]{5,4,3,2,1,0:T(8,128)S(1)} %get-tuple-element.27.coef), custom_call_target="tpu_custom_call" | custom-call | flops 600000000 | bytes 1800000000 | tf_op jit(solution)/shard_map/pallas_call | solution.py:23
  33.7 12.8 %all-to-all-start.1 = ((f32[128,1,128]{2,1,0:T(1,128)}), f32[128,1,128]{2,1,0:T(1,128)S(1)}, u32[]{:S(2)}, u32[]{:S(2)}) async-start(f32[128,1,128]{2,1,0:T(1,128)} %bitcast.7), calls=%async_computation.1 | async-start | bytes 131072 | tf_op jit(solution)/shard_map/all_to_all | solution.py:410
  46.5 0.8 %shard_map.111.force = f32[72,128]{1,0:T(8,128)S(1)} custom-call(f32[128,128]{1,0:T(8,128)S(1)} %bitcast.14, f32[72,128]{1,0:T(8,128)S(1)} %shard_map.108.mine, f32[72,128]{1,0:T(8,128)S(1)} %collective-permute-done.4.other, f32[128,128]{1,0:T(8,128)} %shard_map.109.values), custom_call_target="tpu_custom_call" | custom-call | flops 600000000 | bytes 1800000000 | tf_op jit(solution)/shard_map/pallas_call | solution.py:23
  47.3 0.0 collective-permute-start.6
  47.3 1.7 %collective-permute-start.5 = (f32[72,128]{1,0:T(8,128)S(1)}, f32[72,128]{1,0:T(8,128)S(1)}, u32[]{:S(2)}, u32[]{:S(2)}) collective-permute-start(f32[72,128]{1,0:T(8,128)S(1)} %shard_map.111.force), channel_id=1, source_target_pairs={{0,1},{1,2},{2,3},{3,4},{4,5},{5,6},{6,7},{7,0},{8,9},{9,10},{10,1... | collective-permute-start | bytes 110600 | tf_op jit(solution)/shard_map/ppermute | solution.py:393
  49.0 2.0 %collective-permute-done.6.right = f32[72,128]{1,0:T(8,128)S(1)} collective-permute-done((f32[72,128]{1,0:T(8,128)S(1)}, f32[72,128]{1,0:T(8,128)S(1)}, u32[]{:S(2)}, u32[]{:S(2)}) %collective-permute-start.6) | collective-permute-done | bytes 36896 | tf_op jit(solution)/shard_map/ppermute | solution.py:393
  51.0 1.7 %shard_map.112 = f32[4,2,64,128]{3,2,1,0:T(8,128)} custom-call(f32[72,128]{1,0:T(8,128)S(1)} %shard_map.111.force, f32[72,128]{1,0:T(8,128)S(1)} %collective-permute-done.5.left, f32[72,128]{1,0:T(8,128)S(1)} %collective-permute-done.6.right, f32[2,5,2,9,8,128]{5,4,3,2,1,0:T(8,128)S(1)} %get-tuple-element.27.coef, f32[4,2]{1,0:T(4,128)S(1)} %copy.15.weight), custom_call_target="tpu_custom_call" | custom-call | flops 600000000 | bytes 1800000000 | tf_op jit(solution)/shard_map/pallas_call | solution.py:23
  52.7 0.8 %shard_map.110 = f32[4,128]{1,0:T(4,128)} custom-call(f32[128,128]{1,0:T(8,128)S(1)} %bitcast.12, s32[4,128]{1,0:T(4,128)S(1)} %get-tuple-element.23.owner, s32[4,128]{1,0:T(4,128)S(1)} %get-tuple-element.28.rank), custom_call_target="tpu_custom_call" | custom-call | flops 1000000 | bytes 3000000 | tf_op jit(solution)/shard_map/pallas_call | solution.py:23
  (15 shorter events, 0.0 us)
Async XLA Ops:
  2.0 4.5 %collective-permute-start = (f32[64,128]{1,0:T(8,128)S(1)}, f32[64,128]{1,0:T(8,128)S(1)}, u32[]{:S(2)}, u32[]{:S(2)}) collective-permute-start(f32[64,128]{1,0:T(8,128)S(1)} %get-tuple-element.18), channel_id=1, source_target_pairs={{0,1},{1,2},{2,3},{3,4},{4,5},{5,6},{6,7},{7,0},{8,9},{9,10},{10,1... | collective-permute-start | bytes 98312 | tf_op jit(solution)/shard_map/ppermute | solution.py:393
  4.7 3.3 %collective-permute-start.1 = (f32[64,128]{1,0:T(8,128)S(1)}, f32[64,128]{1,0:T(8,128)S(1)}, u32[]{:S(2)}, u32[]{:S(2)}) collective-permute-start(f32[64,128]{1,0:T(8,128)S(1)} %get-tuple-element.19), channel_id=1, source_target_pairs={{0,7},{1,0},{2,1},{3,2},{4,3},{5,4},{6,5},{7,6},{8,15},{9,8},{10,9... | collective-permute-start | bytes 98312 | tf_op jit(solution)/shard_map/ppermute | solution.py:393
  8.0 18.8 %collective-permute-start.2 = (f32[16,8,128]{2,1,0:T(8,128)S(1)}, f32[16,8,128]{2,1,0:T(8,128)S(1)}, u32[]{:S(2)}, u32[]{:S(2)}) collective-permute-start(f32[16,8,128]{2,1,0:T(8,128)S(1)} %get-tuple-element.20), channel_id=1, source_target_pairs={{0,8},{8,16},{16,24},{24,32},{32,40},{40,48},{48,56},{56,64},{64,7... | collective-permute-start | bytes 196616 | tf_op jit(solution)/shard_map/ppermute | solution.py:403
  9.8 17.1 %collective-permute-start.3 = (f32[16,8,128]{2,1,0:T(8,128)S(1)}, f32[16,8,128]{2,1,0:T(8,128)S(1)}, u32[]{:S(2)}, u32[]{:S(2)}) collective-permute-start(f32[16,8,128]{2,1,0:T(8,128)S(1)} %get-tuple-element.21.__1_), channel_id=1, source_target_pairs={{0,248},{8,0},{16,8},{24,16},{32,24},{40,32},{48,40},{56,48},{64,5... | collective-permute-start | bytes 196616 | tf_op jit(solution)/shard_map/ppermute | solution.py:403
  16.0 10.8 %copy-start.4 = (f32[4,2]{0,1:T(2,128)S(1)}, f32[4,2]{0,1:T(2,128)}, u32[]{:S(2)}) copy-start(f32[4,2]{0,1:T(2,128)} %param.12) | copy-start | bytes 100
  16.0 10.9 %copy-start = (f32[4,2,64,128]{3,2,1,0:T(8,128)S(1)}, f32[4,2,64,128]{3,2,1,0:T(8,128)}, u32[]{:S(2)}) copy-start(f32[4,2,64,128]{3,2,1,0:T(8,128)} %conc.5) | copy-start | bytes 786436
  16.0 10.9 %copy-start.3 = (f32[2,64,128]{2,1,0:T(8,128)S(1)}, f32[2,64,128]{2,1,0:T(8,128)}, u32[]{:S(2)}) copy-start(f32[2,64,128]{2,1,0:T(8,128)} %vv.5) | copy-start | bytes 196612
  16.0 10.9 %copy-start.1 = (f32[2,64,128]{2,1,0:T(8,128)S(1)}, f32[2,64,128]{2,1,0:T(8,128)}, u32[]{:S(2)}) copy-start(f32[2,64,128]{2,1,0:T(8,128)} %kk.5) | copy-start | bytes 196612
  16.0 10.9 %copy-start.2 = (f32[2,64,128]{2,1,0:T(8,128)S(1)}, f32[2,64,128]{2,1,0:T(8,128)}, u32[]{:S(2)}) copy-start(f32[2,64,128]{2,1,0:T(8,128)} %uu.5) | copy-start | bytes 196612
  16.0 16.5 %all-to-all-start = ((f32[128,1,128]{2,1,0:T(1,128)}), f32[128,1,128]{2,1,0:T(1,128)S(1)}, u32[]{:S(2)}, u32[]{:S(2)}) async-start(f32[128,1,128]{2,1,0:T(1,128)} %bitcast.4), calls=%async_computation | async-start | bytes 131072 | tf_op jit(solution)/shard_map/all_to_all | solution.py:410
  28.2 3.2 %collective-permute-start.4 = (f32[72,128]{1,0:T(8,128)S(1)}, f32[72,128]{1,0:T(8,128)S(1)}, u32[]{:S(2)}, u32[]{:S(2)}) collective-permute-start(f32[72,128]{1,0:T(8,128)S(1)} %shard_map.108.mine), channel_id=1, source_target_pairs={{0,128},{128,0},{1,129},{129,1},{2,130},{130,2},{3,131},{131,3},{4... | collective-permute-start | bytes 110600 | tf_op jit(solution)/shard_map/ppermute | solution.py:460
  33.7 19.0 %all-to-all-start.1 = ((f32[128,1,128]{2,1,0:T(1,128)}), f32[128,1,128]{2,1,0:T(1,128)S(1)}, u32[]{:S(2)}, u32[]{:S(2)}) async-start(f32[128,1,128]{2,1,0:T(1,128)} %bitcast.7), calls=%async_computation.1 | async-start | bytes 131072 | tf_op jit(solution)/shard_map/all_to_all | solution.py:410
  47.3 3.7 %collective-permute-start.6 = (f32[72,128]{1,0:T(8,128)S(1)}, f32[72,128]{1,0:T(8,128)S(1)}, u32[]{:S(2)}, u32[]{:S(2)}) collective-permute-start(f32[72,128]{1,0:T(8,128)S(1)} %shard_map.111.force), channel_id=1, source_target_pairs={{0,7},{1,0},{2,1},{3,2},{4,3},{5,4},{6,5},{7,6},{8,15},{9,8},{10,9... | collective-permute-start | bytes 110600 | tf_op jit(solution)/shard_map/ppermute | solution.py:393
  47.3 3.7 %collective-permute-start.5 = (f32[72,128]{1,0:T(8,128)S(1)}, f32[72,128]{1,0:T(8,128)S(1)}, u32[]{:S(2)}, u32[]{:S(2)}) collective-permute-start(f32[72,128]{1,0:T(8,128)S(1)} %shard_map.111.force), channel_id=1, source_target_pairs={{0,1},{1,2},{2,3},{3,4},{4,5},{5,6},{6,7},{7,0},{8,9},{9,10},{10,1... | collective-permute-start | bytes 110600 | tf_op jit(solution)/shard_map/ppermute | solution.py:393

commit v10 on v6

--- a/solution.py
+++ b/solution.py
@@ -389,6 +389,16 @@
     return lax.ppermute(value, axis, [(i, (i + step) % n) for i in range(n)])
 
 
+def long_ring(value, step):
+    n = lax.axis_size("gx")
+    pairs = []
+    for l in range(2):
+        for i in range(n):
+            to = i + step
+            pairs.append((l * n + i, l * n + to if 0 <= to < n else (1 - l) * n + to % n))
+    return lax.ppermute(value, ("lev", "gx"), pairs)
+
+
 def exchange(value):
     nx, ny = lax.axis_size("gx"), lax.axis_size("gy")
     order = [tile_at(t, nx * ny) for t in range(nx * ny)]
@@ -426,7 +436,7 @@
     )
     edge = S((fields + 2, EDGE, m), F32)
     high, low = call(corners_body, (edge, edge), (high, low, left, right))
-    above, below = ring(low, "gx", -1), ring(high, "gx", 1)
+    above, below = long_ring(low, -1), long_ring(high, 1)
     asked = exchange(after(req, low))
     inputs = (conc, kk, uu, vv, below, above, left, right)
     strip = S((n + EDGE, m), F32)

time: 53.7 us -> 53.7 us (level)
    ppermute x6 -> x4, starting transfers between devices: 13.2 us -> 5.04 us  [ring(): return lax.ppermute(value, axis, [(i, (i + step) % n) for i in range(n)])]
    ppermute x0 -> x2, starting transfers between devices: none -> 7.94 us  [long_ring(): return lax.ppermute(value, ('lev', 'gx'), pairs)]
    ppermute x6 -> x4, waiting for transfers between devices: 3.47 us -> 3.47 us  [ring(): return lax.ppermute(value, axis, [(i, (i + step) % n) for i in range(n)])]
where the time goes in v10:
time: 53.7 us; the launch traced here: 53.5 us
  starting transfers between devices  36.6 us (68%)
  Pallas kernels  10.9 us (20%)
  waiting for transfers between devices  5.15 us (10%)
  between operations  0.73 us (1%)
    all_to_all x2, starting transfers between devices, exchange(): lax.all_to_all(value, ('lev', 'gx', 'gy'), 0, 0, axis_index_groups=groups...  23.5 us
    pallas_call x10, Pallas kernels, call(): pl.pallas_call(body, out_shape=outs, in_specs=specs or [VMEM] * len(input...  10.9 us
    ppermute x2, starting transfers between devices, long_ring(): return lax.ppermute(value, ('lev', 'gx'), pairs)  7.94 us
    ppermute x4, starting transfers between devices, ring(): return lax.ppermute(value, axis, [(i, (i + step) % n) for i in range(n)])  5.04 us
    ppermute x4, waiting for transfers between devices, ring(): return lax.ppermute(value, axis, [(i, (i + step) % n) for i in range(n)])  3.47 us
    all_to_all x2, waiting for transfers between devices, exchange(): lax.all_to_all(value, ('lev', 'gx', 'gy'), 0, 0, axis_index_groups=groups...  1.14 us
  transfers between devices with their start and end apart: 9, of which 4 were waited for; matrix products, arithmetic and copies ran while one was open for 0% of the time, Pallas kernels for 14%

profile of v10, /device:TPU:1, one launch (start us, length us, event | category | flops | bytes accessed | tf_op | source)
XLA Modules:
  0.0 53.5 jit_solution(5439129603742614359)
XLA Ops:
  0.6 1.3 %shard_map.103 = (f32[64,128]{1,0:T(8,128)S(1)}, f32[64,128]{1,0:T(8,128)S(1)}, f32[14,8,128]{2,1,0:T(8,128)S(1)}, f32[14,8,128]{2,1,0:T(8,128)S(1)}, s32[4,128]...) custom-call(f32[4,2,64,128]{3,2,1,0:T(8,128)} %conc.5, f32[2,64,128]{2,1,0:T(8,128)} %kk.5, ...), custom_call_target="tpu_custom_call" | custom-call | flops 1000000 | bytes 3000000 | tf_op jit(solution)/shard_map/pallas_call | solution.py:23
  2.0 2.7 %collective-permute-start = (f32[64,128]{1,0:T(8,128)S(1)}, f32[64,128]{1,0:T(8,128)S(1)}, u32[]{:S(2)}, u32[]{:S(2)}) collective-permute-start(f32[64,128]{1,0:T(8,128)S(1)} %get-tuple-element.18), channel_id=1, source_target_pairs={{0,1},{1,2},{2,3},{3,4},{4,5},{5,6},{6,7},{7,0},{8,9},{9,10},{10,1... | collective-permute-start | bytes 98312 | tf_op jit(solution)/shard_map/ppermute | solution.py:389
  4.7 0.6 %collective-permute-start.1 = (f32[64,128]{1,0:T(8,128)S(1)}, f32[64,128]{1,0:T(8,128)S(1)}, u32[]{:S(2)}, u32[]{:S(2)}) collective-permute-start(f32[64,128]{1,0:T(8,128)S(1)} %get-tuple-element.19), channel_id=1, source_target_pairs={{0,7},{1,0},{2,1},{3,2},{4,3},{5,4},{6,5},{7,6},{8,15},{9,8},{10,9... | collective-permute-start | bytes 98312 | tf_op jit(solution)/shard_map/ppermute | solution.py:389
  5.3 1.2 %shard_map.106 = (f32[128,128]{1,0:T(8,128)}, s32[4,128]{1,0:T(4,128)S(1)}) custom-call(s32[4,128]{1,0:T(4,128)S(1)} %get-tuple-element.23.owner, s32[4,128]{1,0:T(4,128)S(1)} %get-tuple-element.24.column, f32[4,128]{1,0:T(4,128)S(1)} %get-tuple-element.25.observed), custom_call_target="tpu_custom_call" | custom-call | flops 600000000 | bytes 1800000000 | tf_op jit(solution)/shard_map/pallas_call | solution.py:23
  6.5 0.0 collective-permute-done.left
  6.5 1.5 %collective-permute-done.1.right = f32[64,128]{1,0:T(8,128)S(1)} collective-permute-done((f32[64,128]{1,0:T(8,128)S(1)}, f32[64,128]{1,0:T(8,128)S(1)}, u32[]{:S(2)}, u32[]{:S(2)}) %collective-permute-start.1) | collective-permute-done | bytes 32800 | tf_op jit(solution)/shard_map/ppermute | solution.py:389
  8.0 1.7 %collective-permute-start.2 = (f32[16,8,128]{2,1,0:T(8,128)S(1)}, f32[16,8,128]{2,1,0:T(8,128)S(1)}, u32[]{:S(2)}, u32[]{:S(2)}) collective-permute-start(f32[16,8,128]{2,1,0:T(8,128)S(1)} %get-tuple-element.20), channel_id=1, source_target_pairs={{0,8},{8,16},{16,24},{24,32},{32,40},{40,48},{48,56},{56,64},{64,7... | collective-permute-start | bytes 196616 | tf_op jit(solution)/shard_map/ppermute | solution.py:399
  9.8 6.2 %collective-permute-start.3 = (f32[16,8,128]{2,1,0:T(8,128)S(1)}, f32[16,8,128]{2,1,0:T(8,128)S(1)}, u32[]{:S(2)}, u32[]{:S(2)}) collective-permute-start(f32[16,8,128]{2,1,0:T(8,128)S(1)} %get-tuple-element.21.__1_), channel_id=1, source_target_pairs={{0,248},{8,0},{16,8},{24,16},{32,24},{40,32},{48,40},{56,48},{64,5... | collective-permute-start | bytes 196616 | tf_op jit(solution)/shard_map/ppermute | solution.py:399
  16.0 0.0 copy-start.2
  16.0 10.7 %all-to-all-start = ((f32[128,1,128]{2,1,0:T(1,128)}), f32[128,1,128]{2,1,0:T(1,128)S(1)}, u32[]{:S(2)}, u32[]{:S(2)}) async-start(f32[128,1,128]{2,1,0:T(1,128)} %bitcast.4), calls=%async_computation | async-start | bytes 131072 | tf_op jit(solution)/shard_map/all_to_all | solution.py:406
  26.7 0.1 copy.15.weight
  26.9 1.3 %shard_map.108.mine = f32[72,128]{1,0:T(8,128)S(1)} custom-call(f32[4,2,64,128]{3,2,1,0:T(8,128)S(1)} %copy-done, f32[2,64,128]{2,1,0:T(8,128)S(1)} %copy-done.1, f32[2,64,128]{2,1,0:T(8,128)S(1)} %copy-done.2, f32[2,64,128]{2,1,0:T(8,128)S(1)} %copy-done.3, f32[16,8,128]{2,1,0:T(8,128)S(1)} %collective-permute-done.2.below, ...), custom_call_target="tpu_custom_call" | custom-call | flops 600000000 | bytes 1800000000 | tf_op jit(solution)/shard_map/pallas_call | solution.py:23
  28.2 0.1 collective-permute-start.4
  28.3 2.6 %shard_map.105 = (f32[4,2,64,128]{3,2,1,0:T(8,128)}, f32[2,5,2,9,8,128]{5,4,3,2,1,0:T(8,128)S(1)}) custom-call(f32[4,2,64,128]{3,2,1,0:T(8,128)S(1)} %copy-done, f32[2,64,128]{2,1,0:T(8,128)S(1)} %copy-done.1, f32[2,64,128]{2,1,0:T(8,128)S(1)} %copy-done.2, f32[2,64,128]{2,1,0:T(8,128)S(1)} %copy-done.3, f32[16,8,128]{2,1,0:T(8,128)S(1)} %collective-permute-done.2.below, ...), custom_call_target="tpu_custom_call" | custom-call | flops 600000000 | bytes 1800000000 | tf_op jit(solution)/shard_map/pallas_call | solution.py:23
  30.8 0.5 %collective-permute-done.4.other = f32[72,128]{1,0:T(8,128)S(1)} collective-permute-done((f32[72,128]{1,0:T(8,128)S(1)}, f32[72,128]{1,0:T(8,128)S(1)}, u32[]{:S(2)}, u32[]{:S(2)}) %collective-permute-start.4) | collective-permute-done | bytes 36896 | tf_op jit(solution)/shard_map/ppermute | solution.py:456
  31.4 1.1 %all-to-all-done = f32[128,1,128]{2,1,0:T(1,128)S(1)} async-done(((f32[128,1,128]{2,1,0:T(1,128)}), f32[128,1,128]{2,1,0:T(1,128)S(1)}, u32[]{:S(2)}, u32[]{:S(2)}) %all-to-all-start) | async-done | bytes 65568 | tf_op jit(solution)/shard_map/all_to_all | solution.py:406
  32.5 1.2 %shard_map.109.values = f32[128,128]{1,0:T(8,128)} custom-call(f32[128,128]{1,0:T(8,128)S(1)} %bitcast.13, f32[72,128]{1,0:T(8,128)S(1)} %shard_map.108.mine, f32[72,128]{1,0:T(8,128)S(1)} %collective-permute-done.4.other, f32[2,5,2,9,8,128]{5,4,3,2,1,0:T(8,128)S(1)} %get-tuple-element.27.coef), custom_call_target="tpu_custom_call" | custom-call | flops 600000000 | bytes 1800000000 | tf_op jit(solution)/shard_map/pallas_call | solution.py:23
  33.7 12.8 %all-to-all-start.1 = ((f32[128,1,128]{2,1,0:T(1,128)}), f32[128,1,128]{2,1,0:T(1,128)S(1)}, u32[]{:S(2)}, u32[]{:S(2)}) async-start(f32[128,1,128]{2,1,0:T(1,128)} %bitcast.7), calls=%async_computation.1 | async-start | bytes 131072 | tf_op jit(solution)/shard_map/all_to_all | solution.py:406
  46.5 0.8 %shard_map.111.force = f32[72,128]{1,0:T(8,128)S(1)} custom-call(f32[128,128]{1,0:T(8,128)S(1)} %bitcast.14, f32[72,128]{1,0:T(8,128)S(1)} %shard_map.108.mine, f32[72,128]{1,0:T(8,128)S(1)} %collective-permute-done.4.other, f32[128,128]{1,0:T(8,128)} %shard_map.109.values), custom_call_target="tpu_custom_call" | custom-call | flops 600000000 | bytes 1800000000 | tf_op jit(solution)/shard_map/pallas_call | solution.py:23
  47.3 0.0 collective-permute-start.6
  47.3 1.7 %collective-permute-start.5 = (f32[72,128]{1,0:T(8,128)S(1)}, f32[72,128]{1,0:T(8,128)S(1)}, u32[]{:S(2)}, u32[]{:S(2)}) collective-permute-start(f32[72,128]{1,0:T(8,128)S(1)} %shard_map.111.force), channel_id=1, source_target_pairs={{0,1},{1,2},{2,3},{3,4},{4,5},{5,6},{6,7},{7,0},{8,9},{9,10},{10,1... | collective-permute-start | bytes 110600 | tf_op jit(solution)/shard_map/ppermute | solution.py:389
  49.0 2.0 %collective-permute-done.6.right = f32[72,128]{1,0:T(8,128)S(1)} collective-permute-done((f32[72,128]{1,0:T(8,128)S(1)}, f32[72,128]{1,0:T(8,128)S(1)}, u32[]{:S(2)}, u32[]{:S(2)}) %collective-permute-start.6) | collective-permute-done | bytes 36896 | tf_op jit(solution)/shard_map/ppermute | solution.py:389
  51.0 1.7 %shard_map.112 = f32[4,2,64,128]{3,2,1,0:T(8,128)} custom-call(f32[72,128]{1,0:T(8,128)S(1)} %shard_map.111.force, f32[72,128]{1,0:T(8,128)S(1)} %collective-permute-done.5.left, f32[72,128]{1,0:T(8,128)S(1)} %collective-permute-done.6.right, f32[2,5,2,9,8,128]{5,4,3,2,1,0:T(8,128)S(1)} %get-tuple-element.27.coef, f32[4,2]{1,0:T(4,128)S(1)} %copy.15.weight), custom_call_target="tpu_custom_call" | custom-call | flops 600000000 | bytes 1800000000 | tf_op jit(solution)/shard_map/pallas_call | solution.py:23
  52.7 0.8 %shard_map.110 = f32[4,128]{1,0:T(4,128)} custom-call(f32[128,128]{1,0:T(8,128)S(1)} %bitcast.12, s32[4,128]{1,0:T(4,128)S(1)} %get-tuple-element.23.owner, s32[4,128]{1,0:T(4,128)S(1)} %get-tuple-element.28.rank), custom_call_target="tpu_custom_call" | custom-call | flops 1000000 | bytes 3000000 | tf_op jit(solution)/shard_map/pallas_call | solution.py:23
  (15 shorter events, 0.0 us)
Async XLA Ops:
  2.0 4.5 %collective-permute-start = (f32[64,128]{1,0:T(8,128)S(1)}, f32[64,128]{1,0:T(8,128)S(1)}, u32[]{:S(2)}, u32[]{:S(2)}) collective-permute-start(f32[64,128]{1,0:T(8,128)S(1)} %get-tuple-element.18), channel_id=1, source_target_pairs={{0,1},{1,2},{2,3},{3,4},{4,5},{5,6},{6,7},{7,0},{8,9},{9,10},{10,1... | collective-permute-start | bytes 98312 | tf_op jit(solution)/shard_map/ppermute | solution.py:389
  4.7 3.3 %collective-permute-start.1 = (f32[64,128]{1,0:T(8,128)S(1)}, f32[64,128]{1,0:T(8,128)S(1)}, u32[]{:S(2)}, u32[]{:S(2)}) collective-permute-start(f32[64,128]{1,0:T(8,128)S(1)} %get-tuple-element.19), channel_id=1, source_target_pairs={{0,7},{1,0},{2,1},{3,2},{4,3},{5,4},{6,5},{7,6},{8,15},{9,8},{10,9... | collective-permute-start | bytes 98312 | tf_op jit(solution)/shard_map/ppermute | solution.py:389
  8.0 18.8 %collective-permute-start.2 = (f32[16,8,128]{2,1,0:T(8,128)S(1)}, f32[16,8,128]{2,1,0:T(8,128)S(1)}, u32[]{:S(2)}, u32[]{:S(2)}) collective-permute-start(f32[16,8,128]{2,1,0:T(8,128)S(1)} %get-tuple-element.20), channel_id=1, source_target_pairs={{0,8},{8,16},{16,24},{24,32},{32,40},{40,48},{48,56},{56,64},{64,7... | collective-permute-start | bytes 196616 | tf_op jit(solution)/shard_map/ppermute | solution.py:399
  9.8 17.1 %collective-permute-start.3 = (f32[16,8,128]{2,1,0:T(8,128)S(1)}, f32[16,8,128]{2,1,0:T(8,128)S(1)}, u32[]{:S(2)}, u32[]{:S(2)}) collective-permute-start(f32[16,8,128]{2,1,0:T(8,128)S(1)} %get-tuple-element.21.__1_), channel_id=1, source_target_pairs={{0,248},{8,0},{16,8},{24,16},{32,24},{40,32},{48,40},{56,48},{64,5... | collective-permute-start | bytes 196616 | tf_op jit(solution)/shard_map/ppermute | solution.py:399
  16.0 10.8 %copy-start.4 = (f32[4,2]{0,1:T(2,128)S(1)}, f32[4,2]{0,1:T(2,128)}, u32[]{:S(2)}) copy-start(f32[4,2]{0,1:T(2,128)} %param.12) | copy-start | bytes 100
  16.0 10.9 %copy-start = (f32[4,2,64,128]{3,2,1,0:T(8,128)S(1)}, f32[4,2,64,128]{3,2,1,0:T(8,128)}, u32[]{:S(2)}) copy-start(f32[4,2,64,128]{3,2,1,0:T(8,128)} %conc.5) | copy-start | bytes 786436
  16.0 10.9 %copy-start.3 = (f32[2,64,128]{2,1,0:T(8,128)S(1)}, f32[2,64,128]{2,1,0:T(8,128)}, u32[]{:S(2)}) copy-start(f32[2,64,128]{2,1,0:T(8,128)} %vv.5) | copy-start | bytes 196612
  16.0 10.9 %copy-start.1 = (f32[2,64,128]{2,1,0:T(8,128)S(1)}, f32[2,64,128]{2,1,0:T(8,128)}, u32[]{:S(2)}) copy-start(f32[2,64,128]{2,1,0:T(8,128)} %kk.5) | copy-start | bytes 196612
  16.0 10.9 %copy-start.2 = (f32[2,64,128]{2,1,0:T(8,128)S(1)}, f32[2,64,128]{2,1,0:T(8,128)}, u32[]{:S(2)}) copy-start(f32[2,64,128]{2,1,0:T(8,128)} %uu.5) | copy-start | bytes 196612
  16.0 16.5 %all-to-all-start = ((f32[128,1,128]{2,1,0:T(1,128)}), f32[128,1,128]{2,1,0:T(1,128)S(1)}, u32[]{:S(2)}, u32[]{:S(2)}) async-start(f32[128,1,128]{2,1,0:T(1,128)} %bitcast.4), calls=%async_computation | async-start | bytes 131072 | tf_op jit(solution)/shard_map/all_to_all | solution.py:406
  28.2 3.2 %collective-permute-start.4 = (f32[72,128]{1,0:T(8,128)S(1)}, f32[72,128]{1,0:T(8,128)S(1)}, u32[]{:S(2)}, u32[]{:S(2)}) collective-permute-start(f32[72,128]{1,0:T(8,128)S(1)} %shard_map.108.mine), channel_id=1, source_target_pairs={{0,128},{128,0},{1,129},{129,1},{2,130},{130,2},{3,131},{131,3},{4... | collective-permute-start | bytes 110600 | tf_op jit(solution)/shard_map/ppermute | solution.py:456
  33.7 19.0 %all-to-all-start.1 = ((f32[128,1,128]{2,1,0:T(1,128)}), f32[128,1,128]{2,1,0:T(1,128)S(1)}, u32[]{:S(2)}, u32[]{:S(2)}) async-start(f32[128,1,128]{2,1,0:T(1,128)} %bitcast.7), calls=%async_computation.1 | async-start | bytes 131072 | tf_op jit(solution)/shard_map/all_to_all | solution.py:406
  47.3 3.7 %collective-permute-start.6 = (f32[72,128]{1,0:T(8,128)S(1)}, f32[72,128]{1,0:T(8,128)S(1)}, u32[]{:S(2)}, u32[]{:S(2)}) collective-permute-start(f32[72,128]{1,0:T(8,128)S(1)} %shard_map.111.force), channel_id=1, source_target_pairs={{0,7},{1,0},{2,1},{3,2},{4,3},{5,4},{6,5},{7,6},{8,15},{9,8},{10,9... | collective-permute-start | bytes 110600 | tf_op jit(solution)/shard_map/ppermute | solution.py:389
  47.3 3.7 %collective-permute-start.5 = (f32[72,128]{1,0:T(8,128)S(1)}, f32[72,128]{1,0:T(8,128)S(1)}, u32[]{:S(2)}, u32[]{:S(2)}) collective-permute-start(f32[72,128]{1,0:T(8,128)S(1)} %shard_map.111.force), channel_id=1, source_target_pairs={{0,1},{1,2},{2,3},{3,4},{4,5},{5,6},{6,7},{7,0},{8,9},{9,10},{10,1... | collective-permute-start | bytes 110600 | tf_op jit(solution)/shard_map/ppermute | solution.py:389
